TPU v7x, 512 devices: a whole 4x8x8 slice. The times are simulated.
512 devices in a mesh: panel: 2 (over y_lo), lon: 16 (over z, core), lat: 16 (over y_hi, x).
Axes of the slice: x: 4, y: 8 (y_hi: 4, y_lo: 2; y = y_hi * 2 + y_lo), z: 8, core: 2. Of those that a mesh axis runs over, the one named last changes fastest.
Arguments:
- pressure: float32 [2, 256, 512, 128], P('panel', 'lat', 'lon'), may hold values from -6 to 6
- porosity: float32 [2, 256, 512, 128], P('panel', 'lat', 'lon'), may hold values from 0.5 to 2
- source: float32 [2, 256, 512, 128], P('panel', 'lat', 'lon'), may hold values from -6 to 6
- bulk: float32 [2, 256, 512, 128], P('panel', 'lat', 'lon'), may hold values from 0.5 to 2
- lat_codes: int32 [2, 2, 2, 512], P('panel', None, None, 'lon'), may hold values from 0 to 8158, as said below
- lat_weights: float32 [2, 4, 2, 2, 512], P('panel', None, None, None, 'lon'), may hold values from 0 to 1, as said below
- lon_codes: int32 [2, 2, 2, 256], P('panel', None, None, 'lat'), may hold values from 0 to 8174, as said below
- lon_weights: float32 [2, 4, 2, 2, 256], P('panel', None, None, None, 'lat'), may hold values from 0 to 1, as said below
Outputs:
- pressure_out: float32 [2, 256, 512, 128], P('panel', 'lat', 'lon')
- porosity_out: float32 [2, 256, 512, 128], P('panel', 'lat', 'lon')
Inputs may be any that keep to these rules, and one draw needn't show every extreme that they name: `lat_codes`: an intersection map of the shell, which may differ from draw to draw: code = a * 32 + c with a < 255 a latitude of the whole panel and c < 31 an offset inside the longitude block of the ghost cell. `lon_codes`: an intersection map of the shell, which may differ from draw to draw: code = b * 16 + r with b < 511 a longitude of the whole panel and r < 15 an offset inside the latitude block of the ghost cell. `lat_weights`: the four weights of a ghost cell are non-negative and sum to one. `lon_weights`: the four weights of a ghost cell are non-negative and sum to one.
All inputs are finite; a program needn't handle non-finite values.
Results may differ from a plain program's by a relative error of at most 0.0003.
Values sent between devices are 32-bit elements; how exact they have to be, the bound alone decides.
A program may use at most 64 MiB of HBM per device.

v0:
```python
import jax
import jax.numpy as jnp
from jax import lax
from jax.sharding import PartitionSpec as P

SWEEPS = 3


stencil_offsets = ((0, 0), (0, 1), (1, 0), (1, 1))
radial_weight = 0.25
buoyancy = 0.5
time_step = 0.04


def padded_2(cells, sides, width):
    for axis, dim in sides:
        count = lax.axis_size(axis)
        ends = count - 1
        head = lax.slice_in_dim(cells, 0, width, axis=dim)
        tail = lax.slice_in_dim(cells, cells.shape[dim] - width, cells.shape[dim], axis=dim)
        cells = jnp.concatenate(
            [
                lax.ppermute(tail, axis, [(i, (i + 1) % count) for i in range(ends)]),
                cells,
                lax.ppermute(head, axis, [((i + 1) % count, i) for i in range(ends)]),
            ],
            axis=dim,
        )
    return cells


def swapped(block, axis, distance):
    count = lax.axis_size(axis)
    route = []
    for low in range(count):
        high = low | 1 << distance
        if high != low and high < count:
            route += [(low, high), (high, low)]
    return lax.ppermute(block, axis, route)


def pad_last(values, before, after):
    widths = [(0, 0)] * (values.ndim - 1) + [(before, after)]
    return jnp.pad(values, widths)


def rim_terms(field, lat_codes, lat_weights, lon_codes, lon_weights, width):
    rows_dev, cols_dev, levels = field.shape
    first_row = lax.axis_index("lat") * rows_dev
    first_col = lax.axis_index("lon") * cols_dev
    chosen = lat_codes[:, :width]
    rows_at = chosen // cols_dev - first_row
    cols_at = chosen % cols_dev
    lat_total = jnp.zeros(chosen.shape + (levels,), jnp.float32)
    for corner, (row_step, col_step) in enumerate(stencil_offsets):
        target = rows_at + row_step
        inside = (target >= 0) & (target < rows_dev)
        picked = field[jnp.clip(target, 0, rows_dev - 1), cols_at + col_step]
        lat_total = (
            lat_total + jnp.where(inside, lat_weights[corner, :, :width], 0.0)[..., None] * picked
        )
    chosen = lon_codes[:, :width]
    cols_at = chosen // rows_dev - first_col
    rows_at = chosen % rows_dev
    lon_total = jnp.zeros(chosen.shape + (levels,), jnp.float32)
    for corner, (row_step, col_step) in enumerate(stencil_offsets):
        target = cols_at + col_step
        inside = (target >= 0) & (target < cols_dev)
        picked = field[rows_at + row_step, jnp.clip(target, 0, cols_dev - 1)]
        lon_total = (
            lon_total + jnp.where(inside, lon_weights[corner, :, :width], 0.0)[..., None] * picked
        )
    return (lat_total, lon_total)


def surround(field, width, lat_codes, lat_weights, lon_codes, lon_weights):
    rows_dev, cols_dev, levels = field.shape
    padded = padded_2(field, (("lat", 0), ("lon", 1)), width)
    lat_terms, lon_terms = rim_terms(field, lat_codes, lat_weights, lon_codes, lon_weights, width)
    lat_summed = lax.psum(lat_terms, "lat")
    lon_summed = lax.psum(lon_terms, "lon")
    arrived = swapped(jnp.concatenate([lat_summed, lon_summed], axis=2), "panel", 0)
    lat_rim = arrived[:, :, :cols_dev]
    lon_rim = arrived[:, :, cols_dev:]
    lat_index = lax.axis_index("lat")
    lon_index = lax.axis_index("lon")
    last_lat = lax.axis_size("lat") - 1
    last_lon = lax.axis_size("lon") - 1
    north = jnp.where(lat_index == 0, lat_rim[0][::-1], padded[:width, width : width + cols_dev])
    padded = padded.at[:width, width : width + cols_dev].set(north)
    south = jnp.where(
        lat_index == last_lat, lat_rim[1], padded[width + rows_dev :, width : width + cols_dev]
    )
    padded = padded.at[width + rows_dev :, width : width + cols_dev].set(south)
    west = jnp.where(
        lon_index == 0,
        jnp.moveaxis(lon_rim[0][::-1], 0, 1),
        padded[width : width + rows_dev, :width],
    )
    padded = padded.at[width : width + rows_dev, :width].set(west)
    east = jnp.where(
        lon_index == last_lon,
        jnp.moveaxis(lon_rim[1], 0, 1),
        padded[width : width + rows_dev, width + cols_dev :],
    )
    padded = padded.at[width : width + rows_dev, width + cols_dev :].set(east)
    return padded


def face_terms(mobility):
    lat_face = 0.5 * (mobility[..., :-1, 1:-1, :] + mobility[..., 1:, 1:-1, :])
    lon_face = 0.5 * (mobility[..., 1:-1, :-1, :] + mobility[..., 1:-1, 1:, :])
    inner = mobility[..., 1:-1, 1:-1, :]
    mean_rad = 0.5 * (inner[..., :-1] + inner[..., 1:])
    return (lat_face, lon_face, mean_rad)


def diagonal_sum(bulk, lat_face, lon_face, mean_rad):
    rad_face = radial_weight * mean_rad
    total = bulk + lat_face[..., :-1, :, :] + lat_face[..., 1:, :, :]
    total = total + lon_face[..., :, :-1, :] + lon_face[..., :, 1:, :]
    return total + pad_last(rad_face, 1, 0) + pad_last(rad_face, 0, 1)


def neighbour_total(padded, source, lat_face, lon_face, mean_rad):
    inner = padded[..., 1:-1, 1:-1, :]
    rad_face = radial_weight * mean_rad
    total = source + lat_face[..., :-1, :, :] * padded[..., :-2, 1:-1, :]
    total = total + lat_face[..., 1:, :, :] * padded[..., 2:, 1:-1, :]
    total = total + lon_face[..., :, :-1, :] * padded[..., 1:-1, :-2, :]
    total = total + lon_face[..., :, 1:, :] * padded[..., 1:-1, 2:, :]
    total = (
        total
        + pad_last(rad_face * inner[..., :-1], 1, 0)
        + pad_last(rad_face * inner[..., 1:], 0, 1)
    )
    return total


def advect(pressure_pad, porosity_pad, lat_face, lon_face, mean_rad, bulk):
    pressure_in = pressure_pad[..., 1:-1, 1:-1, :]
    porosity_in = porosity_pad[..., 2:-2, 2:-2, :]
    lat_speed = -lat_face * (pressure_pad[..., 1:, 1:-1, :] - pressure_pad[..., :-1, 1:-1, :])
    lat_left = 1.5 * porosity_pad[..., 1:-2, 2:-2, :] - 0.5 * porosity_pad[..., :-3, 2:-2, :]
    lat_right = 1.5 * porosity_pad[..., 2:-1, 2:-2, :] - 0.5 * porosity_pad[..., 3:, 2:-2, :]
    lat_flux = lat_speed * jnp.where(lat_speed > 0, lat_left, lat_right)
    lon_speed = -lon_face * (pressure_pad[..., 1:-1, 1:, :] - pressure_pad[..., 1:-1, :-1, :])
    lon_left = 1.5 * porosity_pad[..., 2:-2, 1:-2, :] - 0.5 * porosity_pad[..., 2:-2, :-3, :]
    lon_right = 1.5 * porosity_pad[..., 2:-2, 2:-1, :] - 0.5 * porosity_pad[..., 2:-2, 3:, :]
    lon_flux = lon_speed * jnp.where(lon_speed > 0, lon_left, lon_right)
    rad_speed = (
        -radial_weight * mean_rad * (pressure_in[..., 1:] - pressure_in[..., :-1])
        + buoyancy * mean_rad
    )
    rad_flux = rad_speed * jnp.where(rad_speed > 0, porosity_in[..., :-1], porosity_in[..., 1:])
    divergence = lat_flux[..., 1:, :, :] - lat_flux[..., :-1, :, :]
    divergence = divergence + lon_flux[..., :, 1:, :] - lon_flux[..., :, :-1, :]
    divergence = divergence + pad_last(rad_flux, 0, 1) - pad_last(rad_flux, 1, 0)
    return porosity_in - time_step * (divergence + bulk * pressure_in)


def body(pressure, porosity, source, bulk, lat_codes, lat_weights, lon_codes, lon_weights):
    current = pressure[0]
    porosity_now = porosity[0]
    source_now = source[0]
    bulk_now = bulk[0]
    lat_code_now = lat_codes[0]
    lat_weight_now = lat_weights[0]
    lon_code_now = lon_codes[0]
    lon_weight_now = lon_weights[0]
    porosity_pad = surround(
        porosity_now, 2, lat_code_now, lat_weight_now, lon_code_now, lon_weight_now
    )
    near = porosity_pad[1:-1, 1:-1, :]
    mobility = near * near * near
    lat_face, lon_face, mean_rad = face_terms(mobility)
    denominator = diagonal_sum(bulk_now, lat_face, lon_face, mean_rad)
    for sweep_index in range(SWEEPS):
        padded = surround(current, 1, lat_code_now, lat_weight_now, lon_code_now, lon_weight_now)
        current = neighbour_total(padded, source_now, lat_face, lon_face, mean_rad) / denominator
    pressure_pad = surround(current, 1, lat_code_now, lat_weight_now, lon_code_now, lon_weight_now)
    porosity_new = advect(pressure_pad, porosity_pad, lat_face, lon_face, mean_rad, bulk_now)
    return (current[None], porosity_new[None])


def solution(mesh):
    placed = (
        P("panel", "lat", "lon", None),
        P("panel", "lat", "lon", None),
        P("panel", "lat", "lon", None),
        P("panel", "lat", "lon", None),
        P("panel", None, None, "lon"),
        P("panel", None, None, None, "lon"),
        P("panel", None, None, "lat"),
        P("panel", None, None, None, "lat"),
    )
    return jax.shard_map(
        body,
        mesh=mesh,
        in_specs=placed,
        out_specs=(P("panel", "lat", "lon", None), P("panel", "lat", "lon", None)),
        check_vma=False,
    )
```

profile of v0, /device:TPU:296, one launch (start us, length us, event | category | flops | bytes accessed | tf_op | source)
XLA Modules:
  0.0 695.2 jit_solution(16272074655665553990)
XLA Ops:
  8.1 1.9 gather_fusion.1
  10.0 1.2 gather_fusion.2
  11.3 1.2 gather_fusion.3
  12.6 1.2 gather_fusion
  14.9 3.5 collective-permute-start
  18.5 6.7 collective-permute-start.1
  36.6 76.8 %psum.72 = f32[2,1,32,128]{3,2,1,0:T(8,128)S(1)} all-reduce(f32[2,1,32,128]{3,2,1,0:T(8,128)S(1)} %multiply_add_fusion.4), channel_id=1, replica_groups=mesh['panel'=2,'lon'=16,'lat'=16] {'lat'}, use_global_device_ids=true, to_apply=%region_3.4 | all-reduce | flops 8192 | bytes 65536 | tf_op jit(solution)/shard_map/psum | solution.py:80
  113.6 47.4 %all-reduce.10 = (f32[2,1,16,128]{3,2,1,0:T(8,128)S(1)}, f32[2,2,16,128]{3,2,1,0:T(8,128)S(1)}) all-reduce(f32[2,1,16,128]{3,2,1,0:T(8,128)S(1)} %multiply_add_fusion.9, f32[2,2,16,128]{3,2,1,0:T(8,128)S(1)} %multiply_add_fusion.5), channel_id=1, replica_groups=mesh['panel'=2,'lon'=16,'lat'=16] {'lon'}, use_global_device_ids=true, to_apply=%region_4.5 | all-reduce | flops 12288 | bytes 98304 | tf_op jit(solution)/shard_map/psum | solution.py:81
  160.9 3.3 collective-permute-start.9
  164.2 1.9 collective-permute-start.5
  166.2 8.1 %collective-permute-start.6 = (f32[1,32,128]{2,1,0:T(8,128)S(1)}, f32[1,32,128]{2,1,0:T(8,128)S(1)}, u32[]{:S(2)}, u32[]{:S(2)}) collective-permute-start(f32[1,32,128]{2,1,0:T(8,128)S(1)} %get-tuple-element.306), channel_id=1, source_target_pairs={{1,0},{2,1},{3,2},{4,3},{5,4},{6,5},{7,6},{8,7},{9,8},{10,9},{11,1... | collective-permute-start | bytes 49160 | tf_op jit(solution)/shard_map/ppermute | solution.py:25
  175.8 1.9 collective-permute-start.7
  177.7 4.9 collective-permute-start.8
  184.0 1.9 collective-permute-start.2
  185.9 4.9 collective-permute-start.3
  190.8 1.4 scatter.74
  193.5 2.7 collective-permute-start.4
  196.3 3.7 collective-permute-done.4
  200.1 2.0 dynamic-slice_select_fusion
  202.1 1.5 scatter.66
  207.5 0.9 gather_fusion.16
  208.3 0.9 gather_fusion.17
  209.2 0.9 gather_fusion.18
  210.1 0.9 gather_fusion.19
  213.8 1.2 fusion.127
  215.1 1.0 fusion.128
  216.2 83.2 %psum.74 = f32[2,1,32,128]{3,2,1,0:T(8,128)S(1)} all-reduce(f32[2,1,32,128]{3,2,1,0:T(8,128)S(1)} %multiply_add_fusion.3), channel_id=1, replica_groups=mesh['panel'=2,'lon'=16,'lat'=16] {'lat'}, use_global_device_ids=true, to_apply=%region_5.6 | all-reduce | flops 8192 | bytes 65536 | tf_op jit(solution)/shard_map/psum | solution.py:80
  299.4 1.9 collective-permute-start.10
  301.3 8.1 %collective-permute-start.11 = (f32[1,32,128]{2,0,1:T(1,128)S(1)}, f32[1,32,128]{2,0,1:T(1,128)S(1)}, u32[]{:S(2)}, u32[]{:S(2)}) collective-permute-start(f32[1,32,128]{2,0,1:T(1,128)S(1)} %slice.1292), channel_id=1, source_target_pairs={{1,0},{2,1},{3,2},{4,3},{5,4},{6,5},{7,6},{8,7},{9,8},{10,9},{11,1... | collective-permute-start | bytes 49160 | tf_op jit(solution)/shard_map/ppermute | solution.py:25
  309.5 45.7 %psum.75 = f32[2,1,16,128]{3,2,1,0:T(8,128)S(1)} all-reduce(f32[2,1,16,128]{3,2,1,0:T(8,128)S(1)} %multiply_add_fusion.8), channel_id=1, replica_groups=mesh['panel'=2,'lon'=16,'lat'=16] {'lon'}, use_global_device_ids=true, to_apply=%region_6.7 | all-reduce | flops 4096 | bytes 32768 | tf_op jit(solution)/shard_map/psum | solution.py:81
  355.3 1.9 collective-permute-start.12
  357.2 4.9 collective-permute-start.13
  362.1 2.6 collective-permute-start.14
  364.8 3.3 collective-permute-done.14
  368.1 1.3 scatter.80
  370.1 0.9 copy-done.7
  371.1 1.0 fusion.29
  372.2 0.9 gather_fusion.24
  373.1 0.9 gather_fusion.25
  374.0 0.9 gather_fusion.26
  374.8 0.9 gather_fusion.27
  378.7 76.9 %psum.76 = f32[2,1,32,128]{3,2,1,0:T(8,128)S(1)} all-reduce(f32[2,1,32,128]{3,2,1,0:T(8,128)S(1)} %multiply_add_fusion.2), channel_id=1, replica_groups=mesh['panel'=2,'lon'=16,'lat'=16] {'lat'}, use_global_device_ids=true, to_apply=%region_7.8 | all-reduce | flops 8192 | bytes 65536 | tf_op jit(solution)/shard_map/psum | solution.py:80
  455.6 1.9 collective-permute-start.15
  457.5 8.1 %collective-permute-start.16 = (f32[1,32,128]{2,0,1:T(1,128)S(1)}, f32[1,32,128]{2,0,1:T(1,128)S(1)}, u32[]{:S(2)}, u32[]{:S(2)}) collective-permute-start(f32[1,32,128]{2,0,1:T(1,128)S(1)} %slice.1307), channel_id=1, source_target_pairs={{1,0},{2,1},{3,2},{4,3},{5,4},{6,5},{7,6},{8,7},{9,8},{10,9},{11,1... | collective-permute-start | bytes 49160 | tf_op jit(solution)/shard_map/ppermute | solution.py:25
  465.7 45.7 %psum.77 = f32[2,1,16,128]{3,2,1,0:T(8,128)S(1)} all-reduce(f32[2,1,16,128]{3,2,1,0:T(8,128)S(1)} %multiply_add_fusion.7), channel_id=1, replica_groups=mesh['panel'=2,'lon'=16,'lat'=16] {'lon'}, use_global_device_ids=true, to_apply=%region_8.9 | all-reduce | flops 4096 | bytes 32768 | tf_op jit(solution)/shard_map/psum | solution.py:81
  511.5 1.9 collective-permute-start.17
  513.4 4.9 collective-permute-start.18
  518.3 2.4 collective-permute-start.19
  520.8 3.5 collective-permute-done.19
  524.3 1.3 scatter.86
  526.5 0.9 copy-done.8
  527.6 1.0 fusion.23
  528.7 0.9 gather_fusion.32
  529.6 0.9 gather_fusion.33
  530.4 0.9 gather_fusion.34
  535.2 76.8 %psum.78 = f32[2,1,32,128]{3,2,1,0:T(8,128)S(1)} all-reduce(f32[2,1,32,128]{3,2,1,0:T(8,128)S(1)} %multiply_add_fusion.1), channel_id=1, replica_groups=mesh['panel'=2,'lon'=16,'lat'=16] {'lat'}, use_global_device_ids=true, to_apply=%region_9.10 | all-reduce | flops 8192 | bytes 65536 | tf_op jit(solution)/shard_map/psum | solution.py:80
  611.9 1.9 collective-permute-start.20
  613.9 8.1 %collective-permute-start.21 = (f32[1,32,128]{2,0,1:T(1,128)S(1)}, f32[1,32,128]{2,0,1:T(1,128)S(1)}, u32[]{:S(2)}, u32[]{:S(2)}) collective-permute-start(f32[1,32,128]{2,0,1:T(1,128)S(1)} %slice.1323), channel_id=1, source_target_pairs={{1,0},{2,1},{3,2},{4,3},{5,4},{6,5},{7,6},{8,7},{9,8},{10,9},{11,1... | collective-permute-start | bytes 49160 | tf_op jit(solution)/shard_map/ppermute | solution.py:25
  622.1 45.7 %psum.79 = f32[2,1,16,128]{3,2,1,0:T(8,128)S(1)} all-reduce(f32[2,1,16,128]{3,2,1,0:T(8,128)S(1)} %multiply_add_fusion.6), channel_id=1, replica_groups=mesh['panel'=2,'lon'=16,'lat'=16] {'lon'}, use_global_device_ids=true, to_apply=%region_10.11 | all-reduce | flops 4096 | bytes 32768 | tf_op jit(solution)/shard_map/psum | solution.py:81
  667.9 1.9 collective-permute-start.22
  669.8 4.9 collective-permute-start.23
  674.7 2.4 collective-permute-start.24
  678.0 2.7 collective-permute-done.24
  680.7 1.3 scatter.94
  (252 shorter events, 40.7 us)
Async XLA Ops:
  7.2 185.5 %all-reduce.13.cloned.1.call-start = ((), (), s32[]{:S(2)}) async-start(), calls=%async_computation | async-start | bytes 131072 | tf_op jit(solution)/shard_map/psum | solution.py:80
  7.2 0.7 copy-start.22
  8.1 1.9 copy-start
  12.6 1.2 copy-start.19
  14.7 10.4 %copy-start.20 = (f32[1,4,2,2,16]{4,3,2,1,0:T(2,128)S(1)}, f32[1,4,2,2,16]{4,3,2,1,0:T(2,128)}, u32[]{:S(2)}) copy-start(f32[1,4,2,2,16]{4,3,2,1,0:T(2,128)} %param.55) | copy-start | bytes 3076
  14.7 10.4 %copy-start.21 = (s32[1,2,2,16]{3,2,1,0:T(2,128)S(1)}, s32[1,2,2,16]{3,2,1,0:T(2,128)}, u32[]{:S(2)}) copy-start(s32[1,2,2,16]{3,2,1,0:T(2,128)} %param.54) | copy-start | bytes 772
  14.9 10.7 %copy-start.1 = (f32[1,16,32,128]{3,2,1,0:T(8,128)S(1)}, f32[1,16,32,128]{3,2,1,0:T(8,128)}, u32[]{:S(2)}) copy-start(f32[1,16,32,128]{3,2,1,0:T(8,128)} %param.48) | copy-start | bytes 786436
  14.9 169.0 %collective-permute-start = (f32[2,32,128]{2,0,1:T(2,128)S(1)}, f32[2,32,128]{2,0,1:T(2,128)S(1)}, u32[]{:S(2)}, u32[]{:S(2)}) collective-permute-start(f32[2,32,128]{2,0,1:T(2,128)S(1)} %get-tuple-element.301), channel_id=1, source_target_pairs={{0,1},{1,2},{2,3},{3,4},{4,5},{5,6},{6,7},{7,8},{8,9},{9,10},{10,1... | collective-permute-start | bytes 98312 | tf_op jit(solution)/shard_map/ppermute | solution.py:23
  18.5 165.5 %collective-permute-start.1 = (f32[2,32,128]{2,0,1:T(2,128)S(1)}, f32[2,32,128]{2,0,1:T(2,128)S(1)}, u32[]{:S(2)}, u32[]{:S(2)}) collective-permute-start(f32[2,32,128]{2,0,1:T(2,128)S(1)} %get-tuple-element.302), channel_id=1, source_target_pairs={{1,0},{2,1},{3,2},{4,3},{5,4},{6,5},{7,6},{8,7},{9,8},{10,9},{11,1... | collective-permute-start | bytes 98312 | tf_op jit(solution)/shard_map/ppermute | solution.py:25
  160.9 29.8 %collective-permute-start.9 = (f32[2,1,48,128]{3,2,1,0:T(8,128)S(1)}, f32[2,1,48,128]{3,2,1,0:T(8,128)S(1)}, u32[]{:S(2)}, u32[]{:S(2)}) collective-permute-start(f32[2,1,48,128]{3,2,1,0:T(8,128)S(1)} %pad_maximum_fusion.6), channel_id=1, source_target_pairs={{0,256},{256,0},{1,257},{257,1},{2,258},{258,2},{3,259},{259,3},{4... | collective-permute-start | bytes 147464 | tf_op jit(solution)/shard_map/ppermute | solution.py:39
  164.2 11.5 %collective-permute-start.5 = (f32[1,32,128]{2,1,0:T(8,128)S(1)}, f32[1,32,128]{2,1,0:T(8,128)S(1)}, u32[]{:S(2)}, u32[]{:S(2)}) collective-permute-start(f32[1,32,128]{2,1,0:T(8,128)S(1)} %get-tuple-element.305), channel_id=1, source_target_pairs={{0,1},{1,2},{2,3},{3,4},{4,5},{5,6},{6,7},{7,8},{8,9},{9,10},{10,1... | collective-permute-start | bytes 49160 | tf_op jit(solution)/shard_map/ppermute | solution.py:23
  166.2 8.2 %copy-start.23 = (s32[3]{0:T(128)S(1)}, s32[3]{0:T(128)}, u32[]{:S(2)}) copy-start(s32[3]{0:T(128)} %constant.643.clone.1) | copy-start | bytes 40
  166.2 9.6 %collective-permute-start.6 = (f32[1,32,128]{2,1,0:T(8,128)S(1)}, f32[1,32,128]{2,1,0:T(8,128)S(1)}, u32[]{:S(2)}, u32[]{:S(2)}) collective-permute-start(f32[1,32,128]{2,1,0:T(8,128)S(1)} %get-tuple-element.306), channel_id=1, source_target_pairs={{1,0},{2,1},{3,2},{4,3},{5,4},{6,5},{7,6},{8,7},{9,8},{10,9},{11,1... | collective-permute-start | bytes 49160 | tf_op jit(solution)/shard_map/ppermute | solution.py:25
  175.8 7.4 %collective-permute-start.7 = (f32[18,1,128]{2,1,0:T(1,128)S(1)}, f32[18,1,128]{2,1,0:T(1,128)S(1)}, u32[]{:S(2)}, u32[]{:S(2)}) collective-permute-start(f32[18,1,128]{2,1,0:T(1,128)S(1)} %get-tuple-element.297), channel_id=1, source_target_pairs={{0,16},{16,32},{32,48},{48,64},{64,80},{80,96},{96,112},{112,128},... | collective-permute-start | bytes 27656 | tf_op jit(solution)/shard_map/ppermute | solution.py:23
  177.7 6.2 collective-permute-start.8
  184.0 12.2 %collective-permute-start.2 = (f32[20,2,128]{2,0,1:T(8,128)S(1)}, f32[20,2,128]{2,0,1:T(8,128)S(1)}, u32[]{:S(2)}, u32[]{:S(2)}) collective-permute-start(f32[20,2,128]{2,0,1:T(8,128)S(1)} %get-tuple-element.289), channel_id=1, source_target_pairs={{0,16},{16,32},{32,48},{48,64},{64,80},{80,96},{96,112},{112,128},... | collective-permute-start | bytes 61448 | tf_op jit(solution)/shard_map/ppermute | solution.py:23
  185.9 10.3 %collective-permute-start.3 = (f32[20,2,128]{2,0,1:T(8,128)S(1)}, f32[20,2,128]{2,0,1:T(8,128)S(1)}, u32[]{:S(2)}, u32[]{:S(2)}) collective-permute-start(f32[20,2,128]{2,0,1:T(8,128)S(1)} %get-tuple-element.290), channel_id=1, source_target_pairs={{16,0},{32,16},{48,32},{64,48},{80,64},{96,80},{112,96},{128,112},... | collective-permute-start | bytes 61448 | tf_op jit(solution)/shard_map/ppermute | solution.py:25
  193.5 6.5 collective-permute-start.4
  204.3 0.7 copy-start.2
  204.3 0.8 copy-start.4
  205.4 1.0 copy-start.6
  205.4 1.0 copy-start.17
  299.4 55.9 %collective-permute-start.10 = (f32[1,32,128]{2,1,0:T(8,128)S(1)}, f32[1,32,128]{2,1,0:T(8,128)S(1)}, u32[]{:S(2)}, u32[]{:S(2)}) collective-permute-start(f32[1,32,128]{2,1,0:T(8,128)S(1)} %slice.1291), channel_id=1, source_target_pairs={{0,1},{1,2},{2,3},{3,4},{4,5},{5,6},{6,7},{7,8},{8,9},{9,10},{10,1... | collective-permute-start | bytes 49160 | tf_op jit(solution)/shard_map/ppermute | solution.py:23
  301.3 54.0 %collective-permute-start.11 = (f32[1,32,128]{2,0,1:T(1,128)S(1)}, f32[1,32,128]{2,0,1:T(1,128)S(1)}, u32[]{:S(2)}, u32[]{:S(2)}) collective-permute-start(f32[1,32,128]{2,0,1:T(1,128)S(1)} %slice.1292), channel_id=1, source_target_pairs={{1,0},{2,1},{3,2},{4,3},{5,4},{6,5},{7,6},{8,7},{9,8},{10,9},{11,1... | collective-permute-start | bytes 49160 | tf_op jit(solution)/shard_map/ppermute | solution.py:25
  355.3 9.4 %collective-permute-start.12 = (f32[18,1,128]{2,0,1:T(8,128)S(1)}, f32[18,1,128]{2,0,1:T(8,128)S(1)}, u32[]{:S(2)}, u32[]{:S(2)}) collective-permute-start(f32[18,1,128]{2,0,1:T(8,128)S(1)} %get-tuple-element.295), channel_id=1, source_target_pairs={{0,16},{16,32},{32,48},{48,64},{64,80},{80,96},{96,112},{112,128},... | collective-permute-start | bytes 27656 | tf_op jit(solution)/shard_map/ppermute | solution.py:23
  357.2 7.5 %collective-permute-start.13 = (f32[18,1,128]{2,0,1:T(8,128)S(1)}, f32[18,1,128]{2,0,1:T(8,128)S(1)}, u32[]{:S(2)}, u32[]{:S(2)}) collective-permute-start(f32[18,1,128]{2,0,1:T(8,128)S(1)} %get-tuple-element.296), channel_id=1, source_target_pairs={{16,0},{32,16},{48,32},{64,48},{80,64},{96,80},{112,96},{128,112},... | collective-permute-start | bytes 27656 | tf_op jit(solution)/shard_map/ppermute | solution.py:25
  362.1 6.0 collective-permute-start.14
  370.0 1.0 copy-start.7
  455.6 55.9 %collective-permute-start.15 = (f32[1,32,128]{2,1,0:T(8,128)S(1)}, f32[1,32,128]{2,1,0:T(8,128)S(1)}, u32[]{:S(2)}, u32[]{:S(2)}) collective-permute-start(f32[1,32,128]{2,1,0:T(8,128)S(1)} %slice.1306), channel_id=1, source_target_pairs={{0,1},{1,2},{2,3},{3,4},{4,5},{5,6},{6,7},{7,8},{8,9},{9,10},{10,1... | collective-permute-start | bytes 49160 | tf_op jit(solution)/shard_map/ppermute | solution.py:23
  457.5 54.0 %collective-permute-start.16 = (f32[1,32,128]{2,0,1:T(1,128)S(1)}, f32[1,32,128]{2,0,1:T(1,128)S(1)}, u32[]{:S(2)}, u32[]{:S(2)}) collective-permute-start(f32[1,32,128]{2,0,1:T(1,128)S(1)} %slice.1307), channel_id=1, source_target_pairs={{1,0},{2,1},{3,2},{4,3},{5,4},{6,5},{7,6},{8,7},{9,8},{10,9},{11,1... | collective-permute-start | bytes 49160 | tf_op jit(solution)/shard_map/ppermute | solution.py:25
  511.5 9.2 %collective-permute-start.17 = (f32[18,1,128]{2,0,1:T(8,128)S(1)}, f32[18,1,128]{2,0,1:T(8,128)S(1)}, u32[]{:S(2)}, u32[]{:S(2)}) collective-permute-start(f32[18,1,128]{2,0,1:T(8,128)S(1)} %get-tuple-element.293), channel_id=1, source_target_pairs={{0,16},{16,32},{32,48},{48,64},{64,80},{80,96},{96,112},{112,128},... | collective-permute-start | bytes 27656 | tf_op jit(solution)/shard_map/ppermute | solution.py:23
  513.4 7.3 %collective-permute-start.18 = (f32[18,1,128]{2,0,1:T(8,128)S(1)}, f32[18,1,128]{2,0,1:T(8,128)S(1)}, u32[]{:S(2)}, u32[]{:S(2)}) collective-permute-start(f32[18,1,128]{2,0,1:T(8,128)S(1)} %get-tuple-element.294), channel_id=1, source_target_pairs={{16,0},{32,16},{48,32},{64,48},{80,64},{96,80},{112,96},{128,112},... | collective-permute-start | bytes 27656 | tf_op jit(solution)/shard_map/ppermute | solution.py:25
  518.3 6.0 collective-permute-start.19
  526.5 1.0 copy-start.8
  611.9 55.9 %collective-permute-start.20 = (f32[1,32,128]{2,1,0:T(8,128)S(1)}, f32[1,32,128]{2,1,0:T(8,128)S(1)}, u32[]{:S(2)}, u32[]{:S(2)}) collective-permute-start(f32[1,32,128]{2,1,0:T(8,128)S(1)} %slice.1322), channel_id=1, source_target_pairs={{0,1},{1,2},{2,3},{3,4},{4,5},{5,6},{6,7},{7,8},{8,9},{9,10},{10,1... | collective-permute-start | bytes 49160 | tf_op jit(solution)/shard_map/ppermute | solution.py:23
  613.9 54.0 %collective-permute-start.21 = (f32[1,32,128]{2,0,1:T(1,128)S(1)}, f32[1,32,128]{2,0,1:T(1,128)S(1)}, u32[]{:S(2)}, u32[]{:S(2)}) collective-permute-start(f32[1,32,128]{2,0,1:T(1,128)S(1)} %slice.1323), channel_id=1, source_target_pairs={{1,0},{2,1},{3,2},{4,3},{5,4},{6,5},{7,6},{8,7},{9,8},{10,9},{11,1... | collective-permute-start | bytes 49160 | tf_op jit(solution)/shard_map/ppermute | solution.py:25
  667.9 10.0 %collective-permute-start.22 = (f32[18,1,128]{2,0,1:T(8,128)S(1)}, f32[18,1,128]{2,0,1:T(8,128)S(1)}, u32[]{:S(2)}, u32[]{:S(2)}) collective-permute-start(f32[18,1,128]{2,0,1:T(8,128)S(1)} %get-tuple-element.291), channel_id=1, source_target_pairs={{0,16},{16,32},{32,48},{48,64},{64,80},{80,96},{96,112},{112,128},... | collective-permute-start | bytes 27656 | tf_op jit(solution)/shard_map/ppermute | solution.py:23
  669.8 8.1 %collective-permute-start.23 = (f32[18,1,128]{2,0,1:T(8,128)S(1)}, f32[18,1,128]{2,0,1:T(8,128)S(1)}, u32[]{:S(2)}, u32[]{:S(2)}) collective-permute-start(f32[18,1,128]{2,0,1:T(8,128)S(1)} %get-tuple-element.292), channel_id=1, source_target_pairs={{16,0},{32,16},{48,32},{64,48},{80,64},{96,80},{112,96},{128,112},... | collective-permute-start | bytes 27656 | tf_op jit(solution)/shard_map/ppermute | solution.py:25
  674.7 6.0 collective-permute-start.24
  677.9 4.6 copy-start.5
  678.0 4.5 copy-start.3
  683.0 1.0 copy-start.10
  683.0 1.1 copy-start.11
  683.0 1.2 copy-start.12
  683.1 1.3 copy-start.9
  684.4 1.0 copy-start.13
  684.4 1.0 copy-start.14
  684.4 1.1 copy-start.15
  684.4 1.2 copy-start.16
  686.2 1.0 copy-start.18
Sparse Core Ops, SparseCore 0:
  14.8 158.6 all-reduce.12
where the time goes:
time: 696 us; the launch traced here: 695 us
  blocking collectives  498 us (72%)
  starting transfers between devices  97.7 us (14%)
  local copies, waits for them, and re-layouts  57.8 us (8%)
  between operations  15.5 us (2%)
  waiting for transfers between devices  13.9 us (2%)
  other arithmetic  12 us (2%)
    psum x4, blocking collectives, surround(): lat_summed = lax.psum(lat_terms, 'lat')  314 us
    psum x4, blocking collectives, surround(): lon_summed = lax.psum(lon_terms, 'lon')  185 us
    ppermute x10, starting transfers between devices, padded_2(): lax.ppermute(head, axis, [((i + 1) % count, i) for i in range(ends)])  63.5 us
    ppermute x10, starting transfers between devices, padded_2(): lax.ppermute(tail, axis, [(i, (i + 1) % count) for i in range(ends)])  20.8 us
    gather x20, local copies, waits for them, and re-layouts, rim_terms(): picked = field[jnp.clip(target, 0, rows_dev - 1), cols_at + col_step]  19.7 us
    gather x20, local copies, waits for them, and re-layouts, rim_terms(): picked = field[rows_at + row_step, jnp.clip(target, 0, cols_dev - 1)]  14.8 us
  transfers between devices with their start and end apart: 26, of which 5 were waited for; matrix products, arithmetic and copies ran while one was open for 3% of the time, Pallas kernels for 0%

commit v1 on v0

--- a/solution.py
+++ b/solution.py
@@ -168,15 +168,28 @@
     lat_weight_now = lat_weights[0]
     lon_code_now = lon_codes[0]
     lon_weight_now = lon_weights[0]
-    porosity_pad = surround(
-        porosity_now, 2, lat_code_now, lat_weight_now, lon_code_now, lon_weight_now
-    )
+    levels = porosity_now.shape[-1]
+    both_pad = surround(
+        jnp.concatenate([porosity_now, current], axis=-1),
+        2,
+        lat_code_now,
+        lat_weight_now,
+        lon_code_now,
+        lon_weight_now,
+    )
+    porosity_pad = both_pad[..., :levels]
+    first_pad = both_pad[1:-1, 1:-1, levels:]
     near = porosity_pad[1:-1, 1:-1, :]
     mobility = near * near * near
     lat_face, lon_face, mean_rad = face_terms(mobility)
     denominator = diagonal_sum(bulk_now, lat_face, lon_face, mean_rad)
     for sweep_index in range(SWEEPS):
-        padded = surround(current, 1, lat_code_now, lat_weight_now, lon_code_now, lon_weight_now)
+        if sweep_index == 0:
+            padded = first_pad
+        else:
+            padded = surround(
+                current, 1, lat_code_now, lat_weight_now, lon_code_now, lon_weight_now
+            )
         current = neighbour_total(padded, source_now, lat_face, lon_face, mean_rad) / denominator
     pressure_pad = surround(current, 1, lat_code_now, lat_weight_now, lon_code_now, lon_weight_now)
     porosity_new = advect(pressure_pad, porosity_pad, lat_face, lon_face, mean_rad, bulk_now)

time: 696 us -> 795 us (1.14)
  waiting for transfers between devices: 13.9 us -> 273 us
  blocking collectives: 498 us -> 382 us
  starting transfers between devices: 97.7 us -> 67.7 us
  local copies, waits for them, and re-layouts: 57.8 us -> 46.2 us
    psum x1, waiting for transfers between devices: 0.02 us -> 175 us  [surround(): lat_summed = lax.psum(lat_terms, 'lat')]
    psum x0 -> x1, waiting for transfers between devices: none -> 85.8 us  [surround(): lon_summed = lax.psum(lon_terms, 'lon')]
    psum x4 -> x3, blocking collectives: 314 us -> 245 us  [surround(): lat_summed = lax.psum(lat_terms, 'lat')]
    psum x4 -> x3, blocking collectives: 185 us -> 137 us  [surround(): lon_summed = lax.psum(lon_terms, 'lon')]
    ppermute x10 -> x8, starting transfers between devices: 63.5 us -> 36 us  [padded_2(): lax.ppermute(head, axis, [((i + 1) % count, i) for i in range(ends)])]
    gather x20 -> x16, local copies, waits for them, and re-layouts: 19.7 us -> 15.7 us  [rim_terms(): picked = field[jnp.clip(target, 0, rows_dev - 1), cols_at + col_step]]
    ppermute x10 -> x8, starting transfers between devices: 20.8 us -> 21 us  [padded_2(): lax.ppermute(tail, axis, [(i, (i + 1) % count) for i in range(ends)])]
  transfers between devices with their start and end apart: 26 -> 22, of which waited for: 5 -> 6; matrix products, arithmetic and copies ran while one was open for 3% -> 3% of each run, Pallas kernels for 0% -> 0%
where the time goes in v1:
time: 795 us; the launch traced here: 794 us
  blocking collectives  382 us (48%)
  waiting for transfers between devices  273 us (34%)
  starting transfers between devices  67.7 us (9%)
  local copies, waits for them, and re-layouts  46.2 us (6%)
  between operations  15.1 us (2%)
  other arithmetic  10.1 us (1%)
    psum x3, blocking collectives, surround(): lat_summed = lax.psum(lat_terms, 'lat')  245 us
    psum x1, waiting for transfers between devices, surround(): lat_summed = lax.psum(lat_terms, 'lat')  175 us
    psum x3, blocking collectives, surround(): lon_summed = lax.psum(lon_terms, 'lon')  137 us
    psum x1, waiting for transfers between devices, surround(): lon_summed = lax.psum(lon_terms, 'lon')  85.8 us
    ppermute x8, starting transfers between devices, padded_2(): lax.ppermute(head, axis, [((i + 1) % count, i) for i in range(ends)])  36 us
    ppermute x8, starting transfers between devices, padded_2(): lax.ppermute(tail, axis, [(i, (i + 1) % count) for i in range(ends)])  21 us
  transfers between devices with their start and end apart: 22, of which 6 were waited for; matrix products, arithmetic and copies ran while one was open for 3% of the time, Pallas kernels for 0%

profile of v1, /device:TPU:296, one launch (start us, length us, event | category | flops | bytes accessed | tf_op | source)
XLA Modules:
  0.0 794.1 jit_solution(9546006194397543275)
XLA Ops:
  7.2 1.3 copy_bitcast_fusion
  8.6 3.4 collective-permute-start
  12.0 6.7 collective-permute-start.1
  20.1 0.9 gather_fusion.7
  21.0 0.9 gather_fusion.6
  21.9 0.9 gather_fusion.5
  22.9 0.9 gather_fusion.4
  25.6 1.3 gather_fusion.3
  26.9 1.3 gather_fusion.2
  28.2 1.3 gather_fusion.1
  29.5 1.3 gather_fusion
  30.7 0.8 multiply_add_fusion
  33.9 1.9 collective-permute-start.2
  35.9 4.9 collective-permute-start.3
  40.7 85.8 %all-reduce.15.cloned.1.call-done = f32[2,2,16,256]{3,2,1,0:T(8,128)} async-done(((f32[2,2,16,256]{3,2,1,0:T(8,128)}), f32[2,2,16,256]{3,2,1,0:T(8,128)}) %all-reduce.15.cloned.1.call-update) | async-done | bytes 65552 | tf_op jit(solution)/shard_map/psum | solution.py:81
  126.6 174.8 %all-reduce.13.cloned.1.call-done = f32[2,2,32,256]{3,2,1,0:T(8,128)} async-done(((f32[2,2,32,256]{3,2,1,0:T(8,128)}), f32[2,2,32,256]{3,2,1,0:T(8,128)}) %all-reduce.13.cloned.1.call-update) | async-done | bytes 131088 | tf_op jit(solution)/shard_map/psum | solution.py:80
  301.3 1.0 pad_maximum_fusion.5
  302.3 3.4 collective-permute-start.4
  307.0 2.8 collective-permute-done.4
  310.2 1.9 dynamic-slice_select_fusion
  312.1 1.7 scatter.54
  314.9 0.8 copy-done
  316.4 6.1 collective-permute-start.6
  325.3 1.9 collective-permute-start.5
  327.3 0.9 gather_fusion.11
  328.1 0.9 gather_fusion.10
  329.0 0.9 gather_fusion.9
  329.9 0.9 gather_fusion.8
  330.9 82.9 %psum.58 = f32[2,1,32,128]{3,2,1,0:T(8,128)S(1)} all-reduce(f32[2,1,32,128]{3,2,1,0:T(8,128)S(1)} %multiply_add_fusion.4), channel_id=1, replica_groups=mesh['panel'=2,'lon'=16,'lat'=16] {'lat'}, use_global_device_ids=true, to_apply=%region_3.4 | all-reduce | flops 8192 | bytes 65536 | tf_op jit(solution)/shard_map/psum | solution.py:80
  413.9 45.7 %psum.59 = f32[2,1,16,128]{3,2,1,0:T(8,128)S(1)} all-reduce(f32[2,1,16,128]{3,2,1,0:T(8,128)S(1)} %multiply_add_fusion.7), channel_id=1, replica_groups=mesh['panel'=2,'lon'=16,'lat'=16] {'lon'}, use_global_device_ids=true, to_apply=%region_4.5 | all-reduce | flops 4096 | bytes 32768 | tf_op jit(solution)/shard_map/psum | solution.py:81
  459.6 2.1 collective-permute-start.7
  461.8 4.9 collective-permute-start.8
  466.6 2.4 collective-permute-start.9
  469.2 3.5 collective-permute-done.9
  472.6 1.4 scatter.60
  474.7 0.8 copy-done.2
  479.0 0.9 gather_fusion.19
  479.9 0.9 gather_fusion.18
  480.8 0.9 gather_fusion.17
  481.7 0.9 gather_fusion.16
  482.5 1.9 collective-permute-start.11
  484.5 3.9 collective-permute-start.10
  488.5 80.9 %psum.60 = f32[2,1,32,128]{3,2,1,0:T(8,128)S(1)} all-reduce(f32[2,1,32,128]{3,2,1,0:T(8,128)S(1)} %multiply_add_fusion.3), channel_id=1, replica_groups=mesh['panel'=2,'lon'=16,'lat'=16] {'lat'}, use_global_device_ids=true, to_apply=%region_5.6 | all-reduce | flops 8192 | bytes 65536 | tf_op jit(solution)/shard_map/psum | solution.py:80
  569.5 45.7 %psum.61 = f32[2,1,16,128]{3,2,1,0:T(8,128)S(1)} all-reduce(f32[2,1,16,128]{3,2,1,0:T(8,128)S(1)} %multiply_add_fusion.6), channel_id=1, replica_groups=mesh['panel'=2,'lon'=16,'lat'=16] {'lon'}, use_global_device_ids=true, to_apply=%region_6.7 | all-reduce | flops 4096 | bytes 32768 | tf_op jit(solution)/shard_map/psum | solution.py:81
  615.2 1.9 collective-permute-start.12
  617.2 4.9 collective-permute-start.13
  622.0 2.4 collective-permute-start.14
  624.6 3.5 collective-permute-done.14
  628.0 1.4 scatter.66
  630.1 0.8 copy-done.3
  634.4 0.9 gather_fusion.27
  635.3 0.9 gather_fusion.26
  636.2 0.9 gather_fusion.25
  637.1 0.9 gather_fusion.24
  638.0 1.9 collective-permute-start.16
  639.9 3.9 collective-permute-start.15
  643.9 80.9 %psum.62 = f32[2,1,32,128]{3,2,1,0:T(8,128)S(1)} all-reduce(f32[2,1,32,128]{3,2,1,0:T(8,128)S(1)} %multiply_add_fusion.2), channel_id=1, replica_groups=mesh['panel'=2,'lon'=16,'lat'=16] {'lat'}, use_global_device_ids=true, to_apply=%region_7.8 | all-reduce | flops 8192 | bytes 65536 | tf_op jit(solution)/shard_map/psum | solution.py:80
  724.9 45.7 %psum.63 = f32[2,1,16,128]{3,2,1,0:T(8,128)S(1)} all-reduce(f32[2,1,16,128]{3,2,1,0:T(8,128)S(1)} %multiply_add_fusion.5), channel_id=1, replica_groups=mesh['panel'=2,'lon'=16,'lat'=16] {'lon'}, use_global_device_ids=true, to_apply=%region_8.9 | all-reduce | flops 4096 | bytes 32768 | tf_op jit(solution)/shard_map/psum | solution.py:81
  770.7 1.9 collective-permute-start.17
  772.6 4.9 collective-permute-start.18
  777.5 2.4 collective-permute-start.19
  779.9 0.8 copy.275
  780.8 2.7 collective-permute-done.19
  783.4 1.4 scatter.74
  (178 shorter events, 23.1 us)
Async XLA Ops:
  7.2 119.4 %all-reduce.15.cloned.1.call-start = ((), (), s32[]{:S(2)}) async-start(), calls=%async_computation.1 | async-start | bytes 131072 | tf_op jit(solution)/shard_map/psum | solution.py:81
  8.6 25.3 %collective-permute-start = (f32[2,32,256]{2,0,1:T(2,128)S(1)}, f32[2,32,256]{2,0,1:T(2,128)S(1)}, u32[]{:S(2)}, u32[]{:S(2)}) collective-permute-start(f32[2,32,256]{2,0,1:T(2,128)S(1)} %get-tuple-element.224), channel_id=1, source_target_pairs={{0,1},{1,2},{2,3},{3,4},{4,5},{5,6},{6,7},{7,8},{8,9},{9,10},{10,1... | collective-permute-start | bytes 196616 | tf_op jit(solution)/shard_map/ppermute | solution.py:23
  12.0 21.9 %collective-permute-start.1 = (f32[2,32,256]{2,0,1:T(2,128)S(1)}, f32[2,32,256]{2,0,1:T(2,128)S(1)}, u32[]{:S(2)}, u32[]{:S(2)}) collective-permute-start(f32[2,32,256]{2,0,1:T(2,128)S(1)} %get-tuple-element.225), channel_id=1, source_target_pairs={{1,0},{2,1},{3,2},{4,3},{5,4},{6,5},{7,6},{8,7},{9,8},{10,9},{11,1... | collective-permute-start | bytes 196616 | tf_op jit(solution)/shard_map/ppermute | solution.py:25
  18.7 0.7 copy-start.6
  18.7 0.7 copy-start.4
  24.5 0.7 copy-start.7
  24.5 0.7 copy-start.5
  24.5 276.8 %all-reduce.13.cloned.1.call-start = ((), (), s32[]{:S(2)}) async-start(), calls=%async_computation | async-start | bytes 262144 | tf_op jit(solution)/shard_map/psum | solution.py:80
  31.9 0.7 copy-start.8
  33.9 273.0 %collective-permute-start.2 = (f32[20,2,256]{2,0,1:T(8,128)S(1)}, f32[20,2,256]{2,0,1:T(8,128)S(1)}, u32[]{:S(2)}, u32[]{:S(2)}) collective-permute-start(f32[20,2,256]{2,0,1:T(8,128)S(1)} %get-tuple-element.222), channel_id=1, source_target_pairs={{0,16},{16,32},{32,48},{48,64},{64,80},{80,96},{96,112},{112,128},... | collective-permute-start | bytes 122888 | tf_op jit(solution)/shard_map/ppermute | solution.py:23
  35.9 271.0 %collective-permute-start.3 = (f32[20,2,256]{2,0,1:T(8,128)S(1)}, f32[20,2,256]{2,0,1:T(8,128)S(1)}, u32[]{:S(2)}, u32[]{:S(2)}) collective-permute-start(f32[20,2,256]{2,0,1:T(8,128)S(1)} %get-tuple-element.223), channel_id=1, source_target_pairs={{16,0},{32,16},{48,32},{64,48},{80,64},{96,80},{112,96},{128,112},... | collective-permute-start | bytes 122888 | tf_op jit(solution)/shard_map/ppermute | solution.py:25
  302.3 7.6 collective-permute-start.4
  314.7 1.0 copy-start
  314.7 1.0 copy-start.1
  316.4 143.2 %collective-permute-start.6 = (f32[1,32,128]{2,0,1:T(1,128)S(1)}, f32[1,32,128]{2,0,1:T(1,128)S(1)}, u32[]{:S(2)}, u32[]{:S(2)}) collective-permute-start(f32[1,32,128]{2,0,1:T(1,128)S(1)} %slice.1083), channel_id=1, source_target_pairs={{1,0},{2,1},{3,2},{4,3},{5,4},{6,5},{7,6},{8,7},{9,8},{10,9},{11,1... | collective-permute-start | bytes 49160 | tf_op jit(solution)/shard_map/ppermute | solution.py:25
  325.3 134.3 %collective-permute-start.5 = (f32[1,32,128]{2,1,0:T(8,128)S(1)}, f32[1,32,128]{2,1,0:T(8,128)S(1)}, u32[]{:S(2)}, u32[]{:S(2)}) collective-permute-start(f32[1,32,128]{2,1,0:T(8,128)S(1)} %slice.1082), channel_id=1, source_target_pairs={{0,1},{1,2},{2,3},{3,4},{4,5},{5,6},{6,7},{7,8},{8,9},{9,10},{10,1... | collective-permute-start | bytes 49160 | tf_op jit(solution)/shard_map/ppermute | solution.py:23
  459.6 9.4 %collective-permute-start.7 = (f32[18,1,128]{2,0,1:T(8,128)S(1)}, f32[18,1,128]{2,0,1:T(8,128)S(1)}, u32[]{:S(2)}, u32[]{:S(2)}) collective-permute-start(f32[18,1,128]{2,0,1:T(8,128)S(1)} %get-tuple-element.230), channel_id=1, source_target_pairs={{0,16},{16,32},{32,48},{48,64},{64,80},{80,96},{96,112},{112,128},... | collective-permute-start | bytes 27656 | tf_op jit(solution)/shard_map/ppermute | solution.py:23
  461.8 7.3 collective-permute-start.8
  466.6 6.0 collective-permute-start.9
  474.6 1.0 copy-start.2
  482.5 132.7 %collective-permute-start.11 = (f32[1,32,128]{2,0,1:T(1,128)S(1)}, f32[1,32,128]{2,0,1:T(1,128)S(1)}, u32[]{:S(2)}, u32[]{:S(2)}) collective-permute-start(f32[1,32,128]{2,0,1:T(1,128)S(1)} %slice.1124), channel_id=1, source_target_pairs={{1,0},{2,1},{3,2},{4,3},{5,4},{6,5},{7,6},{8,7},{9,8},{10,9},{11,1... | collective-permute-start | bytes 49160 | tf_op jit(solution)/shard_map/ppermute | solution.py:25
  484.5 130.7 %collective-permute-start.10 = (f32[1,32,128]{2,1,0:T(8,128)S(1)}, f32[1,32,128]{2,1,0:T(8,128)S(1)}, u32[]{:S(2)}, u32[]{:S(2)}) collective-permute-start(f32[1,32,128]{2,1,0:T(8,128)S(1)} %slice.1123), channel_id=1, source_target_pairs={{0,1},{1,2},{2,3},{3,4},{4,5},{5,6},{6,7},{7,8},{8,9},{9,10},{10,1... | collective-permute-start | bytes 49160 | tf_op jit(solution)/shard_map/ppermute | solution.py:23
  615.2 9.2 %collective-permute-start.12 = (f32[18,1,128]{2,0,1:T(8,128)S(1)}, f32[18,1,128]{2,0,1:T(8,128)S(1)}, u32[]{:S(2)}, u32[]{:S(2)}) collective-permute-start(f32[18,1,128]{2,0,1:T(8,128)S(1)} %get-tuple-element.228), channel_id=1, source_target_pairs={{0,16},{16,32},{32,48},{48,64},{64,80},{80,96},{96,112},{112,128},... | collective-permute-start | bytes 27656 | tf_op jit(solution)/shard_map/ppermute | solution.py:23
  617.2 7.3 collective-permute-start.13
  622.0 6.0 collective-permute-start.14
  630.0 1.0 copy-start.3
  638.0 132.7 %collective-permute-start.16 = (f32[1,32,128]{2,0,1:T(1,128)S(1)}, f32[1,32,128]{2,0,1:T(1,128)S(1)}, u32[]{:S(2)}, u32[]{:S(2)}) collective-permute-start(f32[1,32,128]{2,0,1:T(1,128)S(1)} %slice.1140), channel_id=1, source_target_pairs={{1,0},{2,1},{3,2},{4,3},{5,4},{6,5},{7,6},{8,7},{9,8},{10,9},{11,1... | collective-permute-start | bytes 49160 | tf_op jit(solution)/shard_map/ppermute | solution.py:25
  639.9 130.7 %collective-permute-start.15 = (f32[1,32,128]{2,1,0:T(8,128)S(1)}, f32[1,32,128]{2,1,0:T(8,128)S(1)}, u32[]{:S(2)}, u32[]{:S(2)}) collective-permute-start(f32[1,32,128]{2,1,0:T(8,128)S(1)} %slice.1139), channel_id=1, source_target_pairs={{0,1},{1,2},{2,3},{3,4},{4,5},{5,6},{6,7},{7,8},{8,9},{9,10},{10,1... | collective-permute-start | bytes 49160 | tf_op jit(solution)/shard_map/ppermute | solution.py:23
  770.7 10.0 %collective-permute-start.17 = (f32[18,1,128]{2,0,1:T(8,128)S(1)}, f32[18,1,128]{2,0,1:T(8,128)S(1)}, u32[]{:S(2)}, u32[]{:S(2)}) collective-permute-start(f32[18,1,128]{2,0,1:T(8,128)S(1)} %get-tuple-element.226), channel_id=1, source_target_pairs={{0,16},{16,32},{32,48},{48,64},{64,80},{80,96},{96,112},{112,128},... | collective-permute-start | bytes 27656 | tf_op jit(solution)/shard_map/ppermute | solution.py:23
  772.6 8.1 %collective-permute-start.18 = (f32[18,1,128]{2,0,1:T(8,128)S(1)}, f32[18,1,128]{2,0,1:T(8,128)S(1)}, u32[]{:S(2)}, u32[]{:S(2)}) collective-permute-start(f32[18,1,128]{2,0,1:T(8,128)S(1)} %get-tuple-element.227), channel_id=1, source_target_pairs={{16,0},{32,16},{48,32},{64,48},{80,64},{96,80},{112,96},{128,112},... | collective-permute-start | bytes 27656 | tf_op jit(solution)/shard_map/ppermute | solution.py:25
  777.5 6.0 collective-permute-start.19
Sparse Core Ops, SparseCore 0:
  24.6 101.8 all-reduce.14
  130.0 171.2 all-reduce.12

commit v2 on v1

--- a/solution.py
+++ b/solution.py
@@ -1,6 +1,10 @@
+import functools
+
 import jax
 import jax.numpy as jnp
 from jax import lax
+from jax.experimental import pallas as pl
+from jax.experimental.pallas import tpu as pltpu
 from jax.sharding import PartitionSpec as P
 
 SWEEPS = 3
@@ -73,34 +77,112 @@
     return (lat_total, lon_total)
 
 
-def surround(field, width, lat_codes, lat_weights, lon_codes, lon_weights):
+def exchange_kernel(
+    axes, sizes, lat_part, lon_part, lat_rim, lon_rim, lat_buf, lon_buf, send_sems, recv_sems
+):
+    panel = lax.axis_index("panel")
+    lat = lax.axis_index("lat")
+    lon = lax.axis_index("lon")
+    other = 1 - panel
+    last_lat = sizes["lat"] - 1
+    last_lon = sizes["lon"] - 1
+
+    def device(at_lat, at_lon):
+        coords = {"panel": other, "lat": at_lat, "lon": at_lon}
+        return tuple(coords[name] for name in axes)
+
+    routes = (
+        (lat_part.at[0], lat_buf.at[lat], 0, device(0, lon)),
+        (lat_part.at[1], lat_buf.at[lat], 0, device(last_lat, lon)),
+        (lon_part.at[0], lon_buf.at[lon], 1, device(lat, 0)),
+        (lon_part.at[1], lon_buf.at[lon], 1, device(lat, last_lon)),
+    )
+    copies = []
+    for slot, (src, dst, recv, target) in enumerate(routes):
+        copy = pltpu.make_async_remote_copy(
+            src_ref=src,
+            dst_ref=dst,
+            send_sem=send_sems.at[slot],
+            recv_sem=recv_sems.at[recv],
+            device_id=target,
+            device_id_type=pl.DeviceIdType.MESH,
+        )
+        copy.start()
+        copies.append(copy)
+    for copy in copies:
+        copy.wait_send()
+
+    lat_edge = (lat == 0) | (lat == last_lat)
+    lon_edge = (lon == 0) | (lon == last_lon)
+
+    @pl.when(lat_edge)
+    def _():
+        pltpu.make_async_copy(lat_buf, lat_buf, recv_sems.at[0]).wait()
+        lat_rim[...] = jnp.sum(lat_buf[...], axis=0)
+
+    @pl.when(jnp.logical_not(lat_edge))
+    def _():
+        lat_rim[...] = jnp.zeros_like(lat_rim)
+
+    @pl.when(lon_edge)
+    def _():
+        pltpu.make_async_copy(lon_buf, lon_buf, recv_sems.at[1]).wait()
+        lon_rim[...] = jnp.sum(lon_buf[...], axis=0)
+
+    @pl.when(jnp.logical_not(lon_edge))
+    def _():
+        lon_rim[...] = jnp.zeros_like(lon_rim)
+
+
+def exchange(lat_terms, lon_terms, axes):
+    sizes = {name: lax.axis_size(name) for name in ("lat", "lon")}
+    lat_shape = lat_terms.shape[1:]
+    lon_shape = lon_terms.shape[1:]
+    vmem = pl.BlockSpec(memory_space=pltpu.VMEM)
+    moved = 4 * (lat_terms.size + lon_terms.size)
+    return pl.pallas_call(
+        functools.partial(exchange_kernel, axes, sizes),
+        out_shape=(
+            jax.ShapeDtypeStruct(lat_shape, jnp.float32),
+            jax.ShapeDtypeStruct(lon_shape, jnp.float32),
+        ),
+        in_specs=[vmem, vmem],
+        out_specs=(vmem, vmem),
+        scratch_shapes=[
+            pltpu.VMEM((sizes["lat"],) + lat_shape, jnp.float32),
+            pltpu.VMEM((sizes["lon"],) + lon_shape, jnp.float32),
+            pltpu.SemaphoreType.DMA((4,)),
+            pltpu.SemaphoreType.DMA((2,)),
+        ],
+        compiler_params=pltpu.CompilerParams(has_side_effects=True),
+        cost_estimate=pl.CostEstimate(flops=0, transcendentals=0, bytes_accessed=moved),
+    )(lat_terms, lon_terms)
+
+
+def surround(field, width, lat_codes, lat_weights, lon_codes, lon_weights, axes):
     rows_dev, cols_dev, levels = field.shape
     padded = padded_2(field, (("lat", 0), ("lon", 1)), width)
     lat_terms, lon_terms = rim_terms(field, lat_codes, lat_weights, lon_codes, lon_weights, width)
-    lat_summed = lax.psum(lat_terms, "lat")
-    lon_summed = lax.psum(lon_terms, "lon")
-    arrived = swapped(jnp.concatenate([lat_summed, lon_summed], axis=2), "panel", 0)
-    lat_rim = arrived[:, :, :cols_dev]
-    lon_rim = arrived[:, :, cols_dev:]
+    lat_rim, lon_rim = exchange(lat_terms, lon_terms, axes)
     lat_index = lax.axis_index("lat")
     lon_index = lax.axis_index("lon")
     last_lat = lax.axis_size("lat") - 1
     last_lon = lax.axis_size("lon") - 1
-    north = jnp.where(lat_index == 0, lat_rim[0][::-1], padded[:width, width : width + cols_dev])
+    north = jnp.where(lat_index == 0, lat_rim[::-1], padded[:width, width : width + cols_dev])
     padded = padded.at[:width, width : width + cols_dev].set(north)
     south = jnp.where(
-        lat_index == last_lat, lat_rim[1], padded[width + rows_dev :, width : width + cols_dev]
+        lat_index == last_lat, lat_rim, padded[width + rows_dev :, width : width + cols_dev]
     )
     padded = padded.at[width + rows_dev :, width : width + cols_dev].set(south)
     west = jnp.where(
         lon_index == 0,
-        jnp.moveaxis(lon_rim[0][::-1], 0, 1),
+        jnp.moveaxis(lon_rim[::-1], 0, 1),
         padded[width : width + rows_dev, :width],
     )
     padded = padded.at[width : width + rows_dev, :width].set(west)
     east = jnp.where(
         lon_index == last_lon,
-        jnp.moveaxis(lon_rim[1], 0, 1),
+        jnp.moveaxis(lon_rim, 0, 1),
         padded[width : width + rows_dev, width + cols_dev :],
     )
     padded = padded.at[width : width + rows_dev, width + cols_dev :].set(east)
@@ -159,7 +241,7 @@
     return porosity_in - time_step * (divergence + bulk * pressure_in)
 
 
-def body(pressure, porosity, source, bulk, lat_codes, lat_weights, lon_codes, lon_weights):
+def body(axes, pressure, porosity, source, bulk, lat_codes, lat_weights, lon_codes, lon_weights):
     current = pressure[0]
     porosity_now = porosity[0]
     source_now = source[0]
@@ -176,6 +258,7 @@
         lat_weight_now,
         lon_code_now,
         lon_weight_now,
+        axes,
     )
     porosity_pad = both_pad[..., :levels]
     first_pad = both_pad[1:-1, 1:-1, levels:]
@@ -188,10 +271,12 @@
             padded = first_pad
         else:
             padded = surround(
-                current, 1, lat_code_now, lat_weight_now, lon_code_now, lon_weight_now
+                current, 1, lat_code_now, lat_weight_now, lon_code_now, lon_weight_now, axes
             )
         current = neighbour_total(padded, source_now, lat_face, lon_face, mean_rad) / denominator
-    pressure_pad = surround(current, 1, lat_code_now, lat_weight_now, lon_code_now, lon_weight_now)
+    pressure_pad = surround(
+        current, 1, lat_code_now, lat_weight_now, lon_code_now, lon_weight_now, axes
+    )
     porosity_new = advect(pressure_pad, porosity_pad, lat_face, lon_face, mean_rad, bulk_now)
     return (current[None], porosity_new[None])
 
@@ -208,7 +293,7 @@
         P("panel", None, None, None, "lat"),
     )
     return jax.shard_map(
-        body,
+        functools.partial(body, tuple(mesh.axis_names)),
         mesh=mesh,
         in_specs=placed,
         out_specs=(P("panel", "lat", "lon", None), P("panel", "lat", "lon", None)),

time: 795 us -> 223 us (0.28)
  the two profiles are of different devices: /device:TPU:296 before, /device:TPU:193 now
where the time goes in v2:
time: 223 us; the launch traced here: 221 us
  Pallas kernels  101 us (45%)
  local copies, waits for them, and re-layouts  49 us (22%)
  starting transfers between devices  43.5 us (20%)
  other arithmetic  13 us (6%)
  waiting for transfers between devices  12.8 us (6%)
    pallas_call x4, Pallas kernels, exchange(): pl.pallas_call(functools.partial(exchange_kernel, axes, sizes), out_shape...  101 us
    ppermute x8, starting transfers between devices, padded_2(): lax.ppermute(tail, axis, [(i, (i + 1) % count) for i in range(ends)])  30.7 us
    gather x16, local copies, waits for them, and re-layouts, rim_terms(): picked = field[jnp.clip(target, 0, rows_dev - 1), cols_at + col_step]  15.7 us
    ppermute x8, starting transfers between devices, padded_2(): lax.ppermute(head, axis, [((i + 1) % count, i) for i in range(ends)])  12.9 us
    ppermute x8, waiting for transfers between devices, padded_2(): lax.ppermute(head, axis, [((i + 1) % count, i) for i in range(ends)])  12.8 us
    gather x16, local copies, waits for them, and re-layouts, rim_terms(): picked = field[rows_at + row_step, jnp.clip(target, 0, cols_dev - 1)]  12.1 us
    unnamed x36, local copies, waits for them, and re-layouts  8.29 us
    scatter x4, local copies, waits for them, and re-layouts, surround(): padded = padded.at[:width, width:width + cols_dev].set(north)  5.44 us
  transfers between devices with their start and end apart: 16, of which 3 were waited for; matrix products, arithmetic and copies ran while one was open for 12% of the time, Pallas kernels for 46%

profile of v2, /device:TPU:193, one launch (start us, length us, event | category | flops | bytes accessed | tf_op | source)
XLA Modules:
  0.0 221.2 jit_solution(11499554236117822061)
XLA Ops:
  0.6 1.3 copy_bitcast_fusion
  2.0 3.1 %collective-permute-start = (f32[2,32,256]{2,0,1:T(2,128)S(1)}, f32[2,32,256]{2,0,1:T(2,128)S(1)}, u32[]{:S(2)}, u32[]{:S(2)}) collective-permute-start(f32[2,32,256]{2,0,1:T(2,128)S(1)} %get-tuple-element.240), channel_id=1, source_target_pairs={{0,1},{1,2},{2,3},{3,4},{4,5},{5,6},{6,7},{7,8},{8,9},{9,10},{10,1... | collective-permute-start | bytes 196616 | tf_op jit(solution)/shard_map/ppermute | solution.py:27
  5.2 1.3 collective-permute-start.1
  9.3 0.9 gather_fusion.7
  10.2 0.9 gather_fusion.6
  11.1 0.9 gather_fusion.5
  12.0 0.9 gather_fusion.4
  13.0 1.3 gather_fusion.3
  14.2 1.3 gather_fusion.2
  15.5 1.3 gather_fusion.1
  16.8 1.3 gather_fusion
  18.8 0.8 and_reduce_fusion
  19.6 0.7 multiply_add_fusion.1.lon_part
  20.3 0.8 multiply_add_fusion.lat_part
  21.8 6.1 %collective-permute-start.2 = (f32[20,2,256]{2,0,1:T(8,128)S(1)}, f32[20,2,256]{2,0,1:T(8,128)S(1)}, u32[]{:S(2)}, u32[]{:S(2)}) collective-permute-start(f32[20,2,256]{2,0,1:T(8,128)S(1)} %get-tuple-element.238), channel_id=1, source_target_pairs={{0,16},{16,32},{32,48},{48,64},{64,80},{80,96},{96,112},{112,128},... | collective-permute-start | bytes 122888 | tf_op jit(solution)/shard_map/ppermute | solution.py:27
  27.9 1.9 collective-permute-start.3
  31.1 34.5 %shard_map.95 = (f32[2,32,256]{2,1,0:T(8,128)}, f32[2,16,256]{2,1,0:T(8,128)}) custom-call(f32[2,2,32,256]{3,2,1,0:T(8,128)} %multiply_add_fusion.lat_part, f32[2,2,16,256]{3,2,1,0:T(8,128)} %multiply_add_fusion.1.lon_part), custom_call_target="tpu_custom_call" | custom-call | bytes 196608 | tf_op jit(solution)/shard_map/pallas_call | solution.py:143
  65.6 0.9 copy.21
  66.9 2.0 dynamic-slice_select_fusion
  68.9 1.7 scatter.54
  72.3 0.8 copy-done
  73.9 1.3 collective-permute-start.4
  75.2 1.3 collective-permute-start.5
  76.5 0.7 gather_fusion.15
  79.3 0.9 gather_fusion.11
  80.2 0.9 gather_fusion.10
  81.1 0.9 gather_fusion.9
  81.9 0.9 gather_fusion.8
  82.8 0.7 multiply_add_fusion.4.lat_part
  84.2 26.1 %shard_map.96 = (f32[1,32,128]{2,1,0:T(8,128)}, f32[1,16,128]{2,1,0:T(8,128)}) custom-call(f32[2,1,32,128]{3,2,1,0:T(8,128)} %multiply_add_fusion.4.lat_part, f32[2,1,16,128]{3,2,1,0:T(8,128)} %multiply_add_fusion.7.lon_part), custom_call_target="tpu_custom_call" | custom-call | bytes 49152 | tf_op jit(solution)/shard_map/pallas_call | solution.py:143
  110.4 5.9 %collective-permute-start.6 = (f32[18,1,128]{2,0,1:T(8,128)S(1)}, f32[18,1,128]{2,0,1:T(8,128)S(1)}, u32[]{:S(2)}, u32[]{:S(2)}) collective-permute-start(f32[18,1,128]{2,0,1:T(8,128)S(1)} %get-tuple-element.246), channel_id=1, source_target_pairs={{0,16},{16,32},{32,48},{48,64},{64,80},{80,96},{96,112},{112,128},... | collective-permute-start | bytes 27656 | tf_op jit(solution)/shard_map/ppermute | solution.py:27
  116.3 1.9 collective-permute-start.7
  118.2 4.3 %collective-permute-done.7 = f32[18,1,128]{2,0,1:T(8,128)S(1)} collective-permute-done((f32[18,1,128]{2,0,1:T(8,128)S(1)}, f32[18,1,128]{2,0,1:T(8,128)S(1)}, u32[]{:S(2)}, u32[]{:S(2)}) %collective-permute-start.7) | collective-permute-done | bytes 9248 | tf_op jit(solution)/shard_map/ppermute | solution.py:29
  122.6 1.3 scatter.60
  125.1 0.8 copy-done.2
  126.5 0.7 gather_fusion.23
  129.4 0.9 gather_fusion.19
  130.2 0.9 gather_fusion.18
  131.1 0.9 gather_fusion.17
  132.0 0.9 gather_fusion.16
  132.9 1.3 collective-permute-start.8
  134.2 1.3 collective-permute-start.9
  135.5 0.7 multiply_add_fusion.3.lat_part
  136.9 20.3 %shard_map.97 = (f32[1,32,128]{2,1,0:T(8,128)}, f32[1,16,128]{2,1,0:T(8,128)}) custom-call(f32[2,1,32,128]{3,2,1,0:T(8,128)} %multiply_add_fusion.3.lat_part, f32[2,1,16,128]{3,2,1,0:T(8,128)} %multiply_add_fusion.6.lon_part), custom_call_target="tpu_custom_call" | custom-call | bytes 49152 | tf_op jit(solution)/shard_map/pallas_call | solution.py:143
  157.2 5.9 %collective-permute-start.10 = (f32[18,1,128]{2,0,1:T(8,128)S(1)}, f32[18,1,128]{2,0,1:T(8,128)S(1)}, u32[]{:S(2)}, u32[]{:S(2)}) collective-permute-start(f32[18,1,128]{2,0,1:T(8,128)S(1)} %get-tuple-element.244), channel_id=1, source_target_pairs={{0,16},{16,32},{32,48},{48,64},{64,80},{80,96},{96,112},{112,128},... | collective-permute-start | bytes 27656 | tf_op jit(solution)/shard_map/ppermute | solution.py:27
  163.1 1.9 collective-permute-start.11
  165.1 4.3 %collective-permute-done.11 = f32[18,1,128]{2,0,1:T(8,128)S(1)} collective-permute-done((f32[18,1,128]{2,0,1:T(8,128)S(1)}, f32[18,1,128]{2,0,1:T(8,128)S(1)}, u32[]{:S(2)}, u32[]{:S(2)}) %collective-permute-start.11) | collective-permute-done | bytes 9248 | tf_op jit(solution)/shard_map/ppermute | solution.py:29
  169.4 1.3 scatter.66
  171.9 0.8 copy-done.3
  173.4 0.7 gather_fusion.31
  176.2 0.9 gather_fusion.27
  177.1 0.9 gather_fusion.26
  177.9 0.9 gather_fusion.25
  178.8 0.9 gather_fusion.24
  179.7 1.3 collective-permute-start.12
  181.0 1.3 collective-permute-start.13
  182.3 0.7 multiply_add_fusion.2.lat_part
  183.7 0.8 copy.70
  184.5 20.3 %shard_map.98 = (f32[1,32,128]{2,1,0:T(8,128)}, f32[1,16,128]{2,1,0:T(8,128)}) custom-call(f32[2,1,32,128]{3,2,1,0:T(8,128)} %multiply_add_fusion.2.lat_part, f32[2,1,16,128]{3,2,1,0:T(8,128)} %multiply_add_fusion.5.lon_part), custom_call_target="tpu_custom_call" | custom-call | bytes 49152 | tf_op jit(solution)/shard_map/pallas_call | solution.py:143
  204.8 5.9 %collective-permute-start.14 = (f32[18,1,128]{2,0,1:T(8,128)S(1)}, f32[18,1,128]{2,0,1:T(8,128)S(1)}, u32[]{:S(2)}, u32[]{:S(2)}) collective-permute-start(f32[18,1,128]{2,0,1:T(8,128)S(1)} %get-tuple-element.242), channel_id=1, source_target_pairs={{0,16},{16,32},{32,48},{48,64},{64,80},{80,96},{96,112},{112,128},... | collective-permute-start | bytes 27656 | tf_op jit(solution)/shard_map/ppermute | solution.py:27
  210.7 1.9 collective-permute-start.15
  212.7 4.3 %collective-permute-done.15 = f32[18,1,128]{2,0,1:T(8,128)S(1)} collective-permute-done((f32[18,1,128]{2,0,1:T(8,128)S(1)}, f32[18,1,128]{2,0,1:T(8,128)S(1)}, u32[]{:S(2)}, u32[]{:S(2)}) %collective-permute-start.15) | collective-permute-done | bytes 9248 | tf_op jit(solution)/shard_map/ppermute | solution.py:29
  217.0 1.3 scatter.74
  220.4 0.8 copy.71
  (166 shorter events, 22.6 us)
Async XLA Ops:
  2.0 19.8 %collective-permute-start = (f32[2,32,256]{2,0,1:T(2,128)S(1)}, f32[2,32,256]{2,0,1:T(2,128)S(1)}, u32[]{:S(2)}, u32[]{:S(2)}) collective-permute-start(f32[2,32,256]{2,0,1:T(2,128)S(1)} %get-tuple-element.240), channel_id=1, source_target_pairs={{0,1},{1,2},{2,3},{3,4},{4,5},{5,6},{6,7},{7,8},{8,9},{9,10},{10,1... | collective-permute-start | bytes 196616 | tf_op jit(solution)/shard_map/ppermute | solution.py:27
  5.2 16.6 %collective-permute-start.1 = (f32[2,32,256]{2,0,1:T(2,128)S(1)}, f32[2,32,256]{2,0,1:T(2,128)S(1)}, u32[]{:S(2)}, u32[]{:S(2)}) collective-permute-start(f32[2,32,256]{2,0,1:T(2,128)S(1)} %get-tuple-element.241), channel_id=1, source_target_pairs={{1,0},{2,1},{3,2},{4,3},{5,4},{6,5},{7,6},{8,7},{9,8},{10,9},{11,1... | collective-permute-start | bytes 196616 | tf_op jit(solution)/shard_map/ppermute | solution.py:29
  6.5 0.7 copy-start.12
  6.5 0.7 copy-start.14
  7.2 0.7 copy-start.13
  7.2 0.7 copy-start.15
  18.2 0.7 copy-start.16
  21.8 44.9 %collective-permute-start.2 = (f32[20,2,256]{2,0,1:T(8,128)S(1)}, f32[20,2,256]{2,0,1:T(8,128)S(1)}, u32[]{:S(2)}, u32[]{:S(2)}) collective-permute-start(f32[20,2,256]{2,0,1:T(8,128)S(1)} %get-tuple-element.238), channel_id=1, source_target_pairs={{0,16},{16,32},{32,48},{48,64},{64,80},{80,96},{96,112},{112,128},... | collective-permute-start | bytes 122888 | tf_op jit(solution)/shard_map/ppermute | solution.py:27
  27.9 38.9 %collective-permute-start.3 = (f32[20,2,256]{2,0,1:T(8,128)S(1)}, f32[20,2,256]{2,0,1:T(8,128)S(1)}, u32[]{:S(2)}, u32[]{:S(2)}) collective-permute-start(f32[20,2,256]{2,0,1:T(8,128)S(1)} %get-tuple-element.239), channel_id=1, source_target_pairs={{16,0},{32,16},{48,32},{64,48},{80,64},{96,80},{112,96},{128,112},... | collective-permute-start | bytes 122888 | tf_op jit(solution)/shard_map/ppermute | solution.py:29
  68.9 1.7 copy-start.4
  70.6 0.8 copy-start.5
  72.1 1.0 copy-start
  72.2 1.0 copy-start.1
  73.9 36.5 %collective-permute-start.4 = (f32[1,32,128]{2,0,1:T(1,128)S(1)}, f32[1,32,128]{2,0,1:T(1,128)S(1)}, u32[]{:S(2)}, u32[]{:S(2)}) collective-permute-start(f32[1,32,128]{2,0,1:T(1,128)S(1)} %get-tuple-element.252), channel_id=1, source_target_pairs={{0,1},{1,2},{2,3},{3,4},{4,5},{5,6},{6,7},{7,8},{8,9},{9,10},{10,1... | collective-permute-start | bytes 49160 | tf_op jit(solution)/shard_map/ppermute | solution.py:27
  75.2 35.2 %collective-permute-start.5 = (f32[1,32,128]{2,0,1:T(1,128)S(1)}, f32[1,32,128]{2,0,1:T(1,128)S(1)}, u32[]{:S(2)}, u32[]{:S(2)}) collective-permute-start(f32[1,32,128]{2,0,1:T(1,128)S(1)} %get-tuple-element.253), channel_id=1, source_target_pairs={{1,0},{2,1},{3,2},{4,3},{5,4},{6,5},{7,6},{8,7},{9,8},{10,9},{11,1... | collective-permute-start | bytes 49160 | tf_op jit(solution)/shard_map/ppermute | solution.py:29
  110.4 7.8 %copy-start.7 = (f32[1,32,128]{2,1,0:T(8,128)S(1)}, f32[1,32,128]{2,1,0:T(8,128)}, u32[]{:S(2)}) copy-start(f32[1,32,128]{2,1,0:T(8,128)} %get-tuple-element.204) | copy-start | bytes 49156
  110.4 7.8 %collective-permute-start.6 = (f32[18,1,128]{2,0,1:T(8,128)S(1)}, f32[18,1,128]{2,0,1:T(8,128)S(1)}, u32[]{:S(2)}, u32[]{:S(2)}) collective-permute-start(f32[18,1,128]{2,0,1:T(8,128)S(1)} %get-tuple-element.246), channel_id=1, source_target_pairs={{0,16},{16,32},{32,48},{48,64},{64,80},{80,96},{96,112},{112,128},... | collective-permute-start | bytes 27656 | tf_op jit(solution)/shard_map/ppermute | solution.py:27
  116.3 6.2 %collective-permute-start.7 = (f32[18,1,128]{2,0,1:T(8,128)S(1)}, f32[18,1,128]{2,0,1:T(8,128)S(1)}, u32[]{:S(2)}, u32[]{:S(2)}) collective-permute-start(f32[18,1,128]{2,0,1:T(8,128)S(1)} %get-tuple-element.247), channel_id=1, source_target_pairs={{16,0},{32,16},{48,32},{64,48},{80,64},{96,80},{112,96},{128,112},... | collective-permute-start | bytes 27656 | tf_op jit(solution)/shard_map/ppermute | solution.py:29
  123.9 0.7 copy-start.10
  124.9 1.0 copy-start.2
  132.9 24.3 %collective-permute-start.8 = (f32[1,32,128]{2,0,1:T(1,128)S(1)}, f32[1,32,128]{2,0,1:T(1,128)S(1)}, u32[]{:S(2)}, u32[]{:S(2)}) collective-permute-start(f32[1,32,128]{2,0,1:T(1,128)S(1)} %get-tuple-element.250), channel_id=1, source_target_pairs={{0,1},{1,2},{2,3},{3,4},{4,5},{5,6},{6,7},{7,8},{8,9},{9,10},{10,1... | collective-permute-start | bytes 49160 | tf_op jit(solution)/shard_map/ppermute | solution.py:27
  134.2 23.0 %collective-permute-start.9 = (f32[1,32,128]{2,0,1:T(1,128)S(1)}, f32[1,32,128]{2,0,1:T(1,128)S(1)}, u32[]{:S(2)}, u32[]{:S(2)}) collective-permute-start(f32[1,32,128]{2,0,1:T(1,128)S(1)} %get-tuple-element.251), channel_id=1, source_target_pairs={{1,0},{2,1},{3,2},{4,3},{5,4},{6,5},{7,6},{8,7},{9,8},{10,9},{11,1... | collective-permute-start | bytes 49160 | tf_op jit(solution)/shard_map/ppermute | solution.py:29
  157.2 7.8 %copy-start.8 = (f32[1,32,128]{2,1,0:T(8,128)S(1)}, f32[1,32,128]{2,1,0:T(8,128)}, u32[]{:S(2)}) copy-start(f32[1,32,128]{2,1,0:T(8,128)} %get-tuple-element.206) | copy-start | bytes 49156
  157.2 7.8 %collective-permute-start.10 = (f32[18,1,128]{2,0,1:T(8,128)S(1)}, f32[18,1,128]{2,0,1:T(8,128)S(1)}, u32[]{:S(2)}, u32[]{:S(2)}) collective-permute-start(f32[18,1,128]{2,0,1:T(8,128)S(1)} %get-tuple-element.244), channel_id=1, source_target_pairs={{0,16},{16,32},{32,48},{48,64},{64,80},{80,96},{96,112},{112,128},... | collective-permute-start | bytes 27656 | tf_op jit(solution)/shard_map/ppermute | solution.py:27
  163.1 6.2 %collective-permute-start.11 = (f32[18,1,128]{2,0,1:T(8,128)S(1)}, f32[18,1,128]{2,0,1:T(8,128)S(1)}, u32[]{:S(2)}, u32[]{:S(2)}) collective-permute-start(f32[18,1,128]{2,0,1:T(8,128)S(1)} %get-tuple-element.245), channel_id=1, source_target_pairs={{16,0},{32,16},{48,32},{64,48},{80,64},{96,80},{112,96},{128,112},... | collective-permute-start | bytes 27656 | tf_op jit(solution)/shard_map/ppermute | solution.py:29
  170.7 0.7 copy-start.11
  171.7 1.0 copy-start.3
  179.7 25.1 %collective-permute-start.12 = (f32[1,32,128]{2,0,1:T(1,128)S(1)}, f32[1,32,128]{2,0,1:T(1,128)S(1)}, u32[]{:S(2)}, u32[]{:S(2)}) collective-permute-start(f32[1,32,128]{2,0,1:T(1,128)S(1)} %get-tuple-element.248), channel_id=1, source_target_pairs={{0,1},{1,2},{2,3},{3,4},{4,5},{5,6},{6,7},{7,8},{8,9},{9,10},{10,1... | collective-permute-start | bytes 49160 | tf_op jit(solution)/shard_map/ppermute | solution.py:27
  181.0 23.8 %collective-permute-start.13 = (f32[1,32,128]{2,0,1:T(1,128)S(1)}, f32[1,32,128]{2,0,1:T(1,128)S(1)}, u32[]{:S(2)}, u32[]{:S(2)}) collective-permute-start(f32[1,32,128]{2,0,1:T(1,128)S(1)} %get-tuple-element.249), channel_id=1, source_target_pairs={{1,0},{2,1},{3,2},{4,3},{5,4},{6,5},{7,6},{8,7},{9,8},{10,9},{11,1... | collective-permute-start | bytes 49160 | tf_op jit(solution)/shard_map/ppermute | solution.py:29
  204.8 7.8 %copy-start.6 = (f32[1,32,128]{2,1,0:T(8,128)S(1)}, f32[1,32,128]{2,1,0:T(8,128)}, u32[]{:S(2)}) copy-start(f32[1,32,128]{2,1,0:T(8,128)} %get-tuple-element.208) | copy-start | bytes 49156
  204.8 7.8 %collective-permute-start.14 = (f32[18,1,128]{2,0,1:T(8,128)S(1)}, f32[18,1,128]{2,0,1:T(8,128)S(1)}, u32[]{:S(2)}, u32[]{:S(2)}) collective-permute-start(f32[18,1,128]{2,0,1:T(8,128)S(1)} %get-tuple-element.242), channel_id=1, source_target_pairs={{0,16},{16,32},{32,48},{48,64},{64,80},{80,96},{96,112},{112,128},... | collective-permute-start | bytes 27656 | tf_op jit(solution)/shard_map/ppermute | solution.py:27
  210.7 6.2 %collective-permute-start.15 = (f32[18,1,128]{2,0,1:T(8,128)S(1)}, f32[18,1,128]{2,0,1:T(8,128)S(1)}, u32[]{:S(2)}, u32[]{:S(2)}) collective-permute-start(f32[18,1,128]{2,0,1:T(8,128)S(1)} %get-tuple-element.243), channel_id=1, source_target_pairs={{16,0},{32,16},{48,32},{64,48},{80,64},{96,80},{112,96},{128,112},... | collective-permute-start | bytes 27656 | tf_op jit(solution)/shard_map/ppermute | solution.py:29
  218.3 0.7 copy-start.9

commit v3 on v2

--- a/solution.py
+++ b/solution.py
@@ -97,6 +97,26 @@
         (lon_part.at[0], lon_buf.at[lon], 1, device(lat, 0)),
         (lon_part.at[1], lon_buf.at[lon], 1, device(lat, last_lon)),
     )
+    lat_edge = (lat == 0) | (lat == last_lat)
+    lon_edge = (lon == 0) | (lon == last_lon)
+
+    barrier = pltpu.get_barrier_semaphore()
+
+    @pl.when(lat_edge)
+    def _():
+        for sender in range(sizes["lat"]):
+            pl.semaphore_signal(
+                barrier, inc=1, device_id=device(sender, lon), device_id_type=pl.DeviceIdType.MESH
+            )
+
+    @pl.when(lon_edge)
+    def _():
+        for sender in range(sizes["lon"]):
+            pl.semaphore_signal(
+                barrier, inc=1, device_id=device(lat, sender), device_id_type=pl.DeviceIdType.MESH
+            )
+
+    pl.semaphore_wait(barrier, len(routes))
     copies = []
     for slot, (src, dst, recv, target) in enumerate(routes):
         copy = pltpu.make_async_remote_copy(
@@ -112,9 +132,6 @@
     for copy in copies:
         copy.wait_send()
 
-    lat_edge = (lat == 0) | (lat == last_lat)
-    lon_edge = (lon == 0) | (lon == last_lon)
-
     @pl.when(lat_edge)
     def _():
         pltpu.make_async_copy(lat_buf, lat_buf, recv_sems.at[0]).wait()
@@ -134,7 +151,7 @@
         lon_rim[...] = jnp.zeros_like(lon_rim)
 
 
-def exchange(lat_terms, lon_terms, axes):
+def exchange(lat_terms, lon_terms, axes, kernel_id):
     sizes = {name: lax.axis_size(name) for name in ("lat", "lon")}
     lat_shape = lat_terms.shape[1:]
     lon_shape = lon_terms.shape[1:]
@@ -154,7 +171,7 @@
             pltpu.SemaphoreType.DMA((4,)),
             pltpu.SemaphoreType.DMA((2,)),
         ],
-        compiler_params=pltpu.CompilerParams(has_side_effects=True),
+        compiler_params=pltpu.CompilerParams(collective_id=kernel_id, has_side_effects=True),
         cost_estimate=pl.CostEstimate(flops=0, transcendentals=0, bytes_accessed=moved),
     )(lat_terms, lon_terms)
 
@@ -163,7 +180,7 @@
     rows_dev, cols_dev, levels = field.shape
     padded = padded_2(field, (("lat", 0), ("lon", 1)), width)
     lat_terms, lon_terms = rim_terms(field, lat_codes, lat_weights, lon_codes, lon_weights, width)
-    lat_rim, lon_rim = exchange(lat_terms, lon_terms, axes)
+    lat_rim, lon_rim = exchange(lat_terms, lon_terms, axes, width - 1)
     lat_index = lax.axis_index("lat")
     lon_index = lax.axis_index("lon")
     last_lat = lax.axis_size("lat") - 1

time: 223 us -> 180 us (0.81)
  the two profiles are of different devices: /device:TPU:193 before, /device:TPU:1 now
where the time goes in v3:
time: 180 us; the launch traced here: 178 us
  Pallas kernels  66.2 us (37%)
  local copies, waits for them, and re-layouts  49.2 us (27%)
  starting transfers between devices  43.4 us (24%)
  other arithmetic  13 us (7%)
  waiting for transfers between devices  4.5 us (2%)
    pallas_call x4, Pallas kernels, exchange(): pl.pallas_call(functools.partial(exchange_kernel, axes, sizes), out_shape...  66.2 us
    ppermute x8, starting transfers between devices, padded_2(): lax.ppermute(tail, axis, [(i, (i + 1) % count) for i in range(ends)])  25.2 us
    ppermute x8, starting transfers between devices, padded_2(): lax.ppermute(head, axis, [((i + 1) % count, i) for i in range(ends)])  18.2 us
    gather x16, local copies, waits for them, and re-layouts, rim_terms(): picked = field[jnp.clip(target, 0, rows_dev - 1), cols_at + col_step]  15.7 us
    gather x16, local copies, waits for them, and re-layouts, rim_terms(): picked = field[rows_at + row_step, jnp.clip(target, 0, cols_dev - 1)]  12.1 us
    unnamed x36, local copies, waits for them, and re-layouts  8.47 us
    scatter x4, local copies, waits for them, and re-layouts, surround(): padded = padded.at[:width, width:width + cols_dev].set(north)  5.62 us
    ppermute x8, waiting for transfers between devices, padded_2(): lax.ppermute(head, axis, [((i + 1) % count, i) for i in range(ends)])  4.48 us
  transfers between devices with their start and end apart: 16, of which 3 were waited for; matrix products, arithmetic and copies ran while one was open for 15% of the time, Pallas kernels for 37%

profile of v3, /device:TPU:1, one launch (start us, length us, event | category | flops | bytes accessed | tf_op | source)
XLA Modules:
  0.0 178.1 jit_solution(11976876235727672959)
XLA Ops:
  0.6 1.3 copy_bitcast_fusion
  2.0 3.9 %collective-permute-start = (f32[2,32,256]{2,0,1:T(2,128)S(1)}, f32[2,32,256]{2,0,1:T(2,128)S(1)}, u32[]{:S(2)}, u32[]{:S(2)}) collective-permute-start(f32[2,32,256]{2,0,1:T(2,128)S(1)} %get-tuple-element.240), channel_id=1, source_target_pairs={{0,1},{1,2},{2,3},{3,4},{4,5},{5,6},{6,7},{7,8},{8,9},{9,10},{10,1... | collective-permute-start | bytes 196616 | tf_op jit(solution)/shard_map/ppermute | solution.py:27
  6.0 1.3 collective-permute-start.1
  10.1 0.9 gather_fusion.7
  11.0 0.9 gather_fusion.6
  12.0 0.9 gather_fusion.5
  12.9 0.9 gather_fusion.4
  13.8 1.3 gather_fusion.3
  15.1 1.3 gather_fusion.2
  16.3 1.3 gather_fusion.1
  17.6 1.3 gather_fusion
  19.7 0.8 and_reduce_fusion
  20.4 0.7 multiply_add_fusion.1.lon_part
  21.2 0.8 multiply_add_fusion.lat_part
  22.6 4.8 %collective-permute-start.2 = (f32[20,2,256]{2,0,1:T(8,128)S(1)}, f32[20,2,256]{2,0,1:T(8,128)S(1)}, u32[]{:S(2)}, u32[]{:S(2)}) collective-permute-start(f32[20,2,256]{2,0,1:T(8,128)S(1)} %get-tuple-element.238), channel_id=1, source_target_pairs={{0,16},{16,32},{32,48},{48,64},{64,80},{80,96},{96,112},{112,128},... | collective-permute-start | bytes 122888 | tf_op jit(solution)/shard_map/ppermute | solution.py:27
  27.5 2.6 %collective-permute-start.3 = (f32[20,2,256]{2,0,1:T(8,128)S(1)}, f32[20,2,256]{2,0,1:T(8,128)S(1)}, u32[]{:S(2)}, u32[]{:S(2)}) collective-permute-start(f32[20,2,256]{2,0,1:T(8,128)S(1)} %get-tuple-element.239), channel_id=1, source_target_pairs={{16,0},{32,16},{48,32},{64,48},{80,64},{96,80},{112,96},{128,112},... | collective-permute-start | bytes 122888 | tf_op jit(solution)/shard_map/ppermute | solution.py:29
  31.3 25.4 %shard_map.95 = (f32[2,32,256]{2,1,0:T(8,128)}, f32[2,16,256]{2,1,0:T(8,128)}) custom-call(f32[2,2,32,256]{3,2,1,0:T(8,128)} %multiply_add_fusion.lat_part, f32[2,2,16,256]{3,2,1,0:T(8,128)} %multiply_add_fusion.1.lon_part), custom_call_target="tpu_custom_call" | custom-call | bytes 196608 | tf_op jit(solution)/shard_map/pallas_call | solution.py:160
  56.8 0.9 copy.21
  58.0 2.0 %dynamic-slice_select_fusion = f32[2,32,256]{2,0,1:T(2,128)S(1)} fusion(f32[20,36,256]{2,0,1:T(8,128)S(1)} %pad_maximum_fusion, s32[]{:T(128)} %bitcast.23, s32[]{:T(128)} %bitcast.24, f32[2,32,256]{2,0,1:T(2,128)S(1)} %rev.6, f32[2,32,256]{2,0,1:T(2,128)S(1)} %collective-permute-done, pred[]{:T(512)S(6)} %eq.20, pred[]{:T(512)} %and_reduce_fusion), kind=kLoop, calls=%fused_computation.135 | loop fusion | flops 32768 | bytes 262154 | tf_op jit(solution)/shard_map/select.16
  60.1 1.7 scatter.54
  63.5 0.8 copy-done
  65.0 1.3 collective-permute-start.4
  66.3 1.3 collective-permute-start.5
  67.6 0.7 gather_fusion.15
  70.5 0.9 gather_fusion.11
  71.3 0.9 gather_fusion.10
  72.2 0.9 gather_fusion.9
  73.1 0.9 gather_fusion.8
  74.0 0.7 multiply_add_fusion.4.lat_part
  75.4 14.8 %shard_map.96 = (f32[1,32,128]{2,1,0:T(8,128)}, f32[1,16,128]{2,1,0:T(8,128)}) custom-call(f32[2,1,32,128]{3,2,1,0:T(8,128)} %multiply_add_fusion.4.lat_part, f32[2,1,16,128]{3,2,1,0:T(8,128)} %multiply_add_fusion.7.lon_part), custom_call_target="tpu_custom_call" | custom-call | bytes 49152 | tf_op jit(solution)/shard_map/pallas_call | solution.py:160
  90.3 4.2 %collective-permute-start.6 = (f32[18,1,128]{2,0,1:T(8,128)S(1)}, f32[18,1,128]{2,0,1:T(8,128)S(1)}, u32[]{:S(2)}, u32[]{:S(2)}) collective-permute-start(f32[18,1,128]{2,0,1:T(8,128)S(1)} %get-tuple-element.246), channel_id=1, source_target_pairs={{0,16},{16,32},{32,48},{48,64},{64,80},{80,96},{96,112},{112,128},... | collective-permute-start | bytes 27656 | tf_op jit(solution)/shard_map/ppermute | solution.py:27
  94.5 2.6 %collective-permute-start.7 = (f32[18,1,128]{2,0,1:T(8,128)S(1)}, f32[18,1,128]{2,0,1:T(8,128)S(1)}, u32[]{:S(2)}, u32[]{:S(2)}) collective-permute-start(f32[18,1,128]{2,0,1:T(8,128)S(1)} %get-tuple-element.247), channel_id=1, source_target_pairs={{16,0},{32,16},{48,32},{64,48},{80,64},{96,80},{112,96},{128,112},... | collective-permute-start | bytes 27656 | tf_op jit(solution)/shard_map/ppermute | solution.py:29
  97.2 2.3 %collective-permute-done.7 = f32[18,1,128]{2,0,1:T(8,128)S(1)} collective-permute-done((f32[18,1,128]{2,0,1:T(8,128)S(1)}, f32[18,1,128]{2,0,1:T(8,128)S(1)}, u32[]{:S(2)}, u32[]{:S(2)}) %collective-permute-start.7) | collective-permute-done | bytes 9248 | tf_op jit(solution)/shard_map/ppermute | solution.py:29
  99.6 1.4 scatter.60
  102.3 0.8 copy-done.2
  103.7 0.7 gather_fusion.23
  106.5 0.9 gather_fusion.19
  107.4 0.9 gather_fusion.18
  108.3 0.9 gather_fusion.17
  109.2 0.9 gather_fusion.16
  110.1 1.3 collective-permute-start.8
  111.4 1.3 collective-permute-start.9
  112.7 0.7 multiply_add_fusion.3.lat_part
  114.1 13.1 %shard_map.97 = (f32[1,32,128]{2,1,0:T(8,128)}, f32[1,16,128]{2,1,0:T(8,128)}) custom-call(f32[2,1,32,128]{3,2,1,0:T(8,128)} %multiply_add_fusion.3.lat_part, f32[2,1,16,128]{3,2,1,0:T(8,128)} %multiply_add_fusion.6.lon_part), custom_call_target="tpu_custom_call" | custom-call | bytes 49152 | tf_op jit(solution)/shard_map/pallas_call | solution.py:160
  127.3 3.9 %collective-permute-start.10 = (f32[18,1,128]{2,0,1:T(8,128)S(1)}, f32[18,1,128]{2,0,1:T(8,128)S(1)}, u32[]{:S(2)}, u32[]{:S(2)}) collective-permute-start(f32[18,1,128]{2,0,1:T(8,128)S(1)} %get-tuple-element.244), channel_id=1, source_target_pairs={{0,16},{16,32},{32,48},{48,64},{64,80},{80,96},{96,112},{112,128},... | collective-permute-start | bytes 27656 | tf_op jit(solution)/shard_map/ppermute | solution.py:27
  131.2 3.6 %collective-permute-start.11 = (f32[18,1,128]{2,0,1:T(8,128)S(1)}, f32[18,1,128]{2,0,1:T(8,128)S(1)}, u32[]{:S(2)}, u32[]{:S(2)}) collective-permute-start(f32[18,1,128]{2,0,1:T(8,128)S(1)} %get-tuple-element.245), channel_id=1, source_target_pairs={{16,0},{32,16},{48,32},{64,48},{80,64},{96,80},{112,96},{128,112},... | collective-permute-start | bytes 27656 | tf_op jit(solution)/shard_map/ppermute | solution.py:29
  134.8 1.4 collective-permute-done.11
  136.3 1.3 scatter.66
  138.8 0.8 copy-done.3
  140.2 0.7 gather_fusion.31
  143.1 0.9 gather_fusion.27
  143.9 0.9 gather_fusion.26
  144.8 0.9 gather_fusion.25
  145.7 0.9 gather_fusion.24
  146.6 1.9 %collective-permute-start.12 = (f32[1,32,128]{2,0,1:T(1,128)S(1)}, f32[1,32,128]{2,0,1:T(1,128)S(1)}, u32[]{:S(2)}, u32[]{:S(2)}) collective-permute-start(f32[1,32,128]{2,0,1:T(1,128)S(1)} %get-tuple-element.248), channel_id=1, source_target_pairs={{0,1},{1,2},{2,3},{3,4},{4,5},{5,6},{6,7},{7,8},{8,9},{9,10},{10,1... | collective-permute-start | bytes 49160 | tf_op jit(solution)/shard_map/ppermute | solution.py:27
  148.5 1.3 collective-permute-start.13
  149.8 0.7 multiply_add_fusion.2.lat_part
  151.2 0.8 copy.70
  152.0 12.9 %shard_map.98 = (f32[1,32,128]{2,1,0:T(8,128)}, f32[1,16,128]{2,1,0:T(8,128)}) custom-call(f32[2,1,32,128]{3,2,1,0:T(8,128)} %multiply_add_fusion.2.lat_part, f32[2,1,16,128]{3,2,1,0:T(8,128)} %multiply_add_fusion.5.lon_part), custom_call_target="tpu_custom_call" | custom-call | bytes 49152 | tf_op jit(solution)/shard_map/pallas_call | solution.py:160
  164.9 3.8 %collective-permute-start.14 = (f32[18,1,128]{2,0,1:T(8,128)S(1)}, f32[18,1,128]{2,0,1:T(8,128)S(1)}, u32[]{:S(2)}, u32[]{:S(2)}) collective-permute-start(f32[18,1,128]{2,0,1:T(8,128)S(1)} %get-tuple-element.242), channel_id=1, source_target_pairs={{0,16},{16,32},{32,48},{48,64},{64,80},{80,96},{96,112},{112,128},... | collective-permute-start | bytes 27656 | tf_op jit(solution)/shard_map/ppermute | solution.py:27
  168.8 4.2 %collective-permute-start.15 = (f32[18,1,128]{2,0,1:T(8,128)S(1)}, f32[18,1,128]{2,0,1:T(8,128)S(1)}, u32[]{:S(2)}, u32[]{:S(2)}) collective-permute-start(f32[18,1,128]{2,0,1:T(8,128)S(1)} %get-tuple-element.243), channel_id=1, source_target_pairs={{16,0},{32,16},{48,32},{64,48},{80,64},{96,80},{112,96},{128,112},... | collective-permute-start | bytes 27656 | tf_op jit(solution)/shard_map/ppermute | solution.py:29
  173.0 0.8 collective-permute-done.15
  173.9 1.3 scatter.74
  177.3 0.8 copy.71
  (166 shorter events, 22.6 us)
Async XLA Ops:
  2.0 20.6 %collective-permute-start = (f32[2,32,256]{2,0,1:T(2,128)S(1)}, f32[2,32,256]{2,0,1:T(2,128)S(1)}, u32[]{:S(2)}, u32[]{:S(2)}) collective-permute-start(f32[2,32,256]{2,0,1:T(2,128)S(1)} %get-tuple-element.240), channel_id=1, source_target_pairs={{0,1},{1,2},{2,3},{3,4},{4,5},{5,6},{6,7},{7,8},{8,9},{9,10},{10,1... | collective-permute-start | bytes 196616 | tf_op jit(solution)/shard_map/ppermute | solution.py:27
  6.0 16.6 %collective-permute-start.1 = (f32[2,32,256]{2,0,1:T(2,128)S(1)}, f32[2,32,256]{2,0,1:T(2,128)S(1)}, u32[]{:S(2)}, u32[]{:S(2)}) collective-permute-start(f32[2,32,256]{2,0,1:T(2,128)S(1)} %get-tuple-element.241), channel_id=1, source_target_pairs={{1,0},{2,1},{3,2},{4,3},{5,4},{6,5},{7,6},{8,7},{9,8},{10,9},{11,1... | collective-permute-start | bytes 196616 | tf_op jit(solution)/shard_map/ppermute | solution.py:29
  7.3 0.7 copy-start.12
  7.3 0.7 copy-start.14
  8.0 0.7 copy-start.13
  8.0 0.7 copy-start.15
  19.0 0.7 copy-start.16
  22.6 35.3 %collective-permute-start.2 = (f32[20,2,256]{2,0,1:T(8,128)S(1)}, f32[20,2,256]{2,0,1:T(8,128)S(1)}, u32[]{:S(2)}, u32[]{:S(2)}) collective-permute-start(f32[20,2,256]{2,0,1:T(8,128)S(1)} %get-tuple-element.238), channel_id=1, source_target_pairs={{0,16},{16,32},{32,48},{48,64},{64,80},{80,96},{96,112},{112,128},... | collective-permute-start | bytes 122888 | tf_op jit(solution)/shard_map/ppermute | solution.py:27
  27.5 30.4 %collective-permute-start.3 = (f32[20,2,256]{2,0,1:T(8,128)S(1)}, f32[20,2,256]{2,0,1:T(8,128)S(1)}, u32[]{:S(2)}, u32[]{:S(2)}) collective-permute-start(f32[20,2,256]{2,0,1:T(8,128)S(1)} %get-tuple-element.239), channel_id=1, source_target_pairs={{16,0},{32,16},{48,32},{64,48},{80,64},{96,80},{112,96},{128,112},... | collective-permute-start | bytes 122888 | tf_op jit(solution)/shard_map/ppermute | solution.py:29
  60.1 1.7 copy-start.4
  61.8 0.8 copy-start.5
  63.3 1.0 copy-start
  63.3 1.0 copy-start.1
  65.0 25.2 %collective-permute-start.4 = (f32[1,32,128]{2,0,1:T(1,128)S(1)}, f32[1,32,128]{2,0,1:T(1,128)S(1)}, u32[]{:S(2)}, u32[]{:S(2)}) collective-permute-start(f32[1,32,128]{2,0,1:T(1,128)S(1)} %get-tuple-element.252), channel_id=1, source_target_pairs={{0,1},{1,2},{2,3},{3,4},{4,5},{5,6},{6,7},{7,8},{8,9},{9,10},{10,1... | collective-permute-start | bytes 49160 | tf_op jit(solution)/shard_map/ppermute | solution.py:27
  66.3 23.9 %collective-permute-start.5 = (f32[1,32,128]{2,0,1:T(1,128)S(1)}, f32[1,32,128]{2,0,1:T(1,128)S(1)}, u32[]{:S(2)}, u32[]{:S(2)}) collective-permute-start(f32[1,32,128]{2,0,1:T(1,128)S(1)} %get-tuple-element.253), channel_id=1, source_target_pairs={{1,0},{2,1},{3,2},{4,3},{5,4},{6,5},{7,6},{8,7},{9,8},{10,9},{11,1... | collective-permute-start | bytes 49160 | tf_op jit(solution)/shard_map/ppermute | solution.py:29
  90.2 6.9 %copy-start.7 = (f32[1,32,128]{2,1,0:T(8,128)S(1)}, f32[1,32,128]{2,1,0:T(8,128)}, u32[]{:S(2)}) copy-start(f32[1,32,128]{2,1,0:T(8,128)} %get-tuple-element.204) | copy-start | bytes 49156
  90.3 6.9 %collective-permute-start.6 = (f32[18,1,128]{2,0,1:T(8,128)S(1)}, f32[18,1,128]{2,0,1:T(8,128)S(1)}, u32[]{:S(2)}, u32[]{:S(2)}) collective-permute-start(f32[18,1,128]{2,0,1:T(8,128)S(1)} %get-tuple-element.246), channel_id=1, source_target_pairs={{0,16},{16,32},{32,48},{48,64},{64,80},{80,96},{96,112},{112,128},... | collective-permute-start | bytes 27656 | tf_op jit(solution)/shard_map/ppermute | solution.py:27
  94.5 5.0 %collective-permute-start.7 = (f32[18,1,128]{2,0,1:T(8,128)S(1)}, f32[18,1,128]{2,0,1:T(8,128)S(1)}, u32[]{:S(2)}, u32[]{:S(2)}) collective-permute-start(f32[18,1,128]{2,0,1:T(8,128)S(1)} %get-tuple-element.247), channel_id=1, source_target_pairs={{16,0},{32,16},{48,32},{64,48},{80,64},{96,80},{112,96},{128,112},... | collective-permute-start | bytes 27656 | tf_op jit(solution)/shard_map/ppermute | solution.py:29
  101.0 0.7 copy-start.10
  102.1 1.0 copy-start.2
  110.1 17.1 %collective-permute-start.8 = (f32[1,32,128]{2,0,1:T(1,128)S(1)}, f32[1,32,128]{2,0,1:T(1,128)S(1)}, u32[]{:S(2)}, u32[]{:S(2)}) collective-permute-start(f32[1,32,128]{2,0,1:T(1,128)S(1)} %get-tuple-element.250), channel_id=1, source_target_pairs={{0,1},{1,2},{2,3},{3,4},{4,5},{5,6},{6,7},{7,8},{8,9},{9,10},{10,1... | collective-permute-start | bytes 49160 | tf_op jit(solution)/shard_map/ppermute | solution.py:27
  111.4 15.8 %collective-permute-start.9 = (f32[1,32,128]{2,0,1:T(1,128)S(1)}, f32[1,32,128]{2,0,1:T(1,128)S(1)}, u32[]{:S(2)}, u32[]{:S(2)}) collective-permute-start(f32[1,32,128]{2,0,1:T(1,128)S(1)} %get-tuple-element.251), channel_id=1, source_target_pairs={{1,0},{2,1},{3,2},{4,3},{5,4},{6,5},{7,6},{8,7},{9,8},{10,9},{11,1... | collective-permute-start | bytes 49160 | tf_op jit(solution)/shard_map/ppermute | solution.py:29
  127.2 7.6 %copy-start.8 = (f32[1,32,128]{2,1,0:T(8,128)S(1)}, f32[1,32,128]{2,1,0:T(8,128)}, u32[]{:S(2)}) copy-start(f32[1,32,128]{2,1,0:T(8,128)} %get-tuple-element.206) | copy-start | bytes 49156
  127.3 7.6 %collective-permute-start.10 = (f32[18,1,128]{2,0,1:T(8,128)S(1)}, f32[18,1,128]{2,0,1:T(8,128)S(1)}, u32[]{:S(2)}, u32[]{:S(2)}) collective-permute-start(f32[18,1,128]{2,0,1:T(8,128)S(1)} %get-tuple-element.244), channel_id=1, source_target_pairs={{0,16},{16,32},{32,48},{48,64},{64,80},{80,96},{96,112},{112,128},... | collective-permute-start | bytes 27656 | tf_op jit(solution)/shard_map/ppermute | solution.py:27
  131.2 5.0 %collective-permute-start.11 = (f32[18,1,128]{2,0,1:T(8,128)S(1)}, f32[18,1,128]{2,0,1:T(8,128)S(1)}, u32[]{:S(2)}, u32[]{:S(2)}) collective-permute-start(f32[18,1,128]{2,0,1:T(8,128)S(1)} %get-tuple-element.245), channel_id=1, source_target_pairs={{16,0},{32,16},{48,32},{64,48},{80,64},{96,80},{112,96},{128,112},... | collective-permute-start | bytes 27656 | tf_op jit(solution)/shard_map/ppermute | solution.py:29
  137.6 0.7 copy-start.11
  138.6 1.0 copy-start.3
  146.6 18.3 %collective-permute-start.12 = (f32[1,32,128]{2,0,1:T(1,128)S(1)}, f32[1,32,128]{2,0,1:T(1,128)S(1)}, u32[]{:S(2)}, u32[]{:S(2)}) collective-permute-start(f32[1,32,128]{2,0,1:T(1,128)S(1)} %get-tuple-element.248), channel_id=1, source_target_pairs={{0,1},{1,2},{2,3},{3,4},{4,5},{5,6},{6,7},{7,8},{8,9},{9,10},{10,1... | collective-permute-start | bytes 49160 | tf_op jit(solution)/shard_map/ppermute | solution.py:27
  148.5 16.4 %collective-permute-start.13 = (f32[1,32,128]{2,0,1:T(1,128)S(1)}, f32[1,32,128]{2,0,1:T(1,128)S(1)}, u32[]{:S(2)}, u32[]{:S(2)}) collective-permute-start(f32[1,32,128]{2,0,1:T(1,128)S(1)} %get-tuple-element.249), channel_id=1, source_target_pairs={{1,0},{2,1},{3,2},{4,3},{5,4},{6,5},{7,6},{8,7},{9,8},{10,9},{11,1... | collective-permute-start | bytes 49160 | tf_op jit(solution)/shard_map/ppermute | solution.py:29
  164.9 8.1 %copy-start.6 = (f32[1,32,128]{2,1,0:T(8,128)S(1)}, f32[1,32,128]{2,1,0:T(8,128)}, u32[]{:S(2)}) copy-start(f32[1,32,128]{2,1,0:T(8,128)} %get-tuple-element.208) | copy-start | bytes 49156
  164.9 8.1 %collective-permute-start.14 = (f32[18,1,128]{2,0,1:T(8,128)S(1)}, f32[18,1,128]{2,0,1:T(8,128)S(1)}, u32[]{:S(2)}, u32[]{:S(2)}) collective-permute-start(f32[18,1,128]{2,0,1:T(8,128)S(1)} %get-tuple-element.242), channel_id=1, source_target_pairs={{0,16},{16,32},{32,48},{48,64},{64,80},{80,96},{96,112},{112,128},... | collective-permute-start | bytes 27656 | tf_op jit(solution)/shard_map/ppermute | solution.py:27
  168.8 5.0 %collective-permute-start.15 = (f32[18,1,128]{2,0,1:T(8,128)S(1)}, f32[18,1,128]{2,0,1:T(8,128)S(1)}, u32[]{:S(2)}, u32[]{:S(2)}) collective-permute-start(f32[18,1,128]{2,0,1:T(8,128)S(1)} %get-tuple-element.243), channel_id=1, source_target_pairs={{16,0},{32,16},{48,32},{64,48},{80,64},{96,80},{112,96},{128,112},... | collective-permute-start | bytes 27656 | tf_op jit(solution)/shard_map/ppermute | solution.py:29
  175.2 0.7 copy-start.9

commit v4 on v3

--- a/solution.py
+++ b/solution.py
@@ -14,33 +14,6 @@
 radial_weight = 0.25
 buoyancy = 0.5
 time_step = 0.04
-
-
-def padded_2(cells, sides, width):
-    for axis, dim in sides:
-        count = lax.axis_size(axis)
-        ends = count - 1
-        head = lax.slice_in_dim(cells, 0, width, axis=dim)
-        tail = lax.slice_in_dim(cells, cells.shape[dim] - width, cells.shape[dim], axis=dim)
-        cells = jnp.concatenate(
-            [
-                lax.ppermute(tail, axis, [(i, (i + 1) % count) for i in range(ends)]),
-                cells,
-                lax.ppermute(head, axis, [((i + 1) % count, i) for i in range(ends)]),
-            ],
-            axis=dim,
-        )
-    return cells
-
-
-def swapped(block, axis, distance):
-    count = lax.axis_size(axis)
-    route = []
-    for low in range(count):
-        high = low | 1 << distance
-        if high != low and high < count:
-            route += [(low, high), (high, low)]
-    return lax.ppermute(block, axis, route)
 
 
 def pad_last(values, before, after):
@@ -78,7 +51,24 @@
 
 
 def exchange_kernel(
-    axes, sizes, lat_part, lon_part, lat_rim, lon_rim, lat_buf, lon_buf, send_sems, recv_sems
+    axes,
+    sizes,
+    width,
+    field,
+    lat_part,
+    lon_part,
+    north,
+    south,
+    west,
+    east,
+    lat_buf,
+    lon_buf,
+    north_buf,
+    south_buf,
+    west_buf,
+    east_buf,
+    send_sems,
+    recv_sems,
 ):
     panel = lax.axis_index("panel")
     lat = lax.axis_index("lat")
@@ -86,124 +76,196 @@
     other = 1 - panel
     last_lat = sizes["lat"] - 1
     last_lon = sizes["lon"] - 1
-
-    def device(at_lat, at_lon):
-        coords = {"panel": other, "lat": at_lat, "lon": at_lon}
+    rows, cols = field.shape[0], field.shape[1]
+    mesh_kind = pl.DeviceIdType.MESH
+
+    def device(at_panel, at_lat, at_lon):
+        coords = {"panel": at_panel, "lat": at_lat, "lon": at_lon}
         return tuple(coords[name] for name in axes)
 
+    always = lat >= 0
     routes = (
-        (lat_part.at[0], lat_buf.at[lat], 0, device(0, lon)),
-        (lat_part.at[1], lat_buf.at[lat], 0, device(last_lat, lon)),
-        (lon_part.at[0], lon_buf.at[lon], 1, device(lat, 0)),
-        (lon_part.at[1], lon_buf.at[lon], 1, device(lat, last_lon)),
+        (always, lat_part.at[0], lat_buf.at[lat], 0, device(other, 0, lon)),
+        (always, lat_part.at[1], lat_buf.at[lat], 0, device(other, last_lat, lon)),
+        (always, lon_part.at[0], lon_buf.at[lon], 1, device(other, lat, 0)),
+        (always, lon_part.at[1], lon_buf.at[lon], 1, device(other, lat, last_lon)),
+        (
+            lat < last_lat,
+            field.at[pl.ds(rows - width, width)],
+            north_buf,
+            2,
+            device(panel, lat + 1, lon),
+        ),
+        (lat > 0, field.at[pl.ds(0, width)], south_buf, 3, device(panel, lat - 1, lon)),
+        (
+            lon < last_lon,
+            field.at[:, pl.ds(cols - width, width)],
+            west_buf,
+            4,
+            device(panel, lat, lon + 1),
+        ),
+        (lon > 0, field.at[:, pl.ds(0, width)], east_buf, 5, device(panel, lat, lon - 1)),
     )
     lat_edge = (lat == 0) | (lat == last_lat)
     lon_edge = (lon == 0) | (lon == last_lon)
 
     barrier = pltpu.get_barrier_semaphore()
 
+    def greet(target):
+        pl.semaphore_signal(barrier, inc=1, device_id=target, device_id_type=mesh_kind)
+
     @pl.when(lat_edge)
     def _():
         for sender in range(sizes["lat"]):
-            pl.semaphore_signal(
-                barrier, inc=1, device_id=device(sender, lon), device_id_type=pl.DeviceIdType.MESH
-            )
+            greet(device(other, sender, lon))
 
     @pl.when(lon_edge)
     def _():
         for sender in range(sizes["lon"]):
-            pl.semaphore_signal(
-                barrier, inc=1, device_id=device(lat, sender), device_id_type=pl.DeviceIdType.MESH
-            )
-
-    pl.semaphore_wait(barrier, len(routes))
+            greet(device(other, lat, sender))
+
+    neighbours = (
+        (lat > 0, device(panel, lat - 1, lon)),
+        (lat < last_lat, device(panel, lat + 1, lon)),
+        (lon > 0, device(panel, lat, lon - 1)),
+        (lon < last_lon, device(panel, lat, lon + 1)),
+    )
+    for present, target in neighbours:
+
+        @pl.when(present)
+        def _():
+            greet(target)
+
+    def above_zero(index, count):
+        return (index + count - 1) // count
+
+    peers = (
+        4
+        + above_zero(lat, sizes["lat"])
+        + above_zero(last_lat - lat, sizes["lat"])
+        + above_zero(lon, sizes["lon"])
+        + above_zero(last_lon - lon, sizes["lon"])
+    )
+    pl.semaphore_wait(barrier, peers)
+
     copies = []
-    for slot, (src, dst, recv, target) in enumerate(routes):
+    for slot, (present, src, dst, recv, target) in enumerate(routes):
         copy = pltpu.make_async_remote_copy(
             src_ref=src,
             dst_ref=dst,
             send_sem=send_sems.at[slot],
             recv_sem=recv_sems.at[recv],
             device_id=target,
-            device_id_type=pl.DeviceIdType.MESH,
+            device_id_type=mesh_kind,
         )
-        copy.start()
-        copies.append(copy)
-    for copy in copies:
-        copy.wait_send()
+
+        @pl.when(present)
+        def _():
+            copy.start()
+
+        copies.append((present, copy))
+    for present, copy in copies:
+
+        @pl.when(present)
+        def _():
+            copy.wait_send()
+
+    def arrived(buf, recv):
+        pltpu.make_async_copy(buf, buf, recv_sems.at[recv]).wait()
 
     @pl.when(lat_edge)
     def _():
-        pltpu.make_async_copy(lat_buf, lat_buf, recv_sems.at[0]).wait()
-        lat_rim[...] = jnp.sum(lat_buf[...], axis=0)
-
-    @pl.when(jnp.logical_not(lat_edge))
-    def _():
-        lat_rim[...] = jnp.zeros_like(lat_rim)
+        arrived(lat_buf, 0)
 
     @pl.when(lon_edge)
     def _():
-        pltpu.make_async_copy(lon_buf, lon_buf, recv_sems.at[1]).wait()
-        lon_rim[...] = jnp.sum(lon_buf[...], axis=0)
-
-    @pl.when(jnp.logical_not(lon_edge))
-    def _():
-        lon_rim[...] = jnp.zeros_like(lon_rim)
-
-
-def exchange(lat_terms, lon_terms, axes, kernel_id):
+        arrived(lon_buf, 1)
+
+    @pl.when(lat == 0)
+    def _():
+        total = jnp.sum(lat_buf[...], axis=0)
+        for depth in range(width):
+            north[width - 1 - depth] = total[depth]
+
+    @pl.when(lat > 0)
+    def _():
+        arrived(north_buf, 2)
+        north[...] = north_buf[...]
+
+    @pl.when(lat == last_lat)
+    def _():
+        south[...] = jnp.sum(lat_buf[...], axis=0)
+
+    @pl.when(lat < last_lat)
+    def _():
+        arrived(south_buf, 3)
+        south[...] = south_buf[...]
+
+    @pl.when(lon == 0)
+    def _():
+        total = jnp.sum(lon_buf[...], axis=0)
+        for depth in range(width):
+            west[width - 1 - depth] = total[depth]
+
+    @pl.when(lon > 0)
+    def _():
+        arrived(west_buf, 4)
+        for depth in range(width):
+            west[depth] = west_buf[:, depth, :]
+
+    @pl.when(lon == last_lon)
+    def _():
+        east[...] = jnp.sum(lon_buf[...], axis=0)
+
+    @pl.when(lon < last_lon)
+    def _():
+        arrived(east_buf, 5)
+        for depth in range(width):
+            east[depth] = east_buf[:, depth, :]
+
+
+def exchange(field, lat_terms, lon_terms, axes, width):
     sizes = {name: lax.axis_size(name) for name in ("lat", "lon")}
-    lat_shape = lat_terms.shape[1:]
-    lon_shape = lon_terms.shape[1:]
+    rows, cols, levels = field.shape
+    lat_shape = (width, cols, levels)
+    lon_shape = (width, rows, levels)
     vmem = pl.BlockSpec(memory_space=pltpu.VMEM)
-    moved = 4 * (lat_terms.size + lon_terms.size)
+    moved = 4 * (lat_terms.size + lon_terms.size + 2 * width * (rows + cols) * levels)
     return pl.pallas_call(
-        functools.partial(exchange_kernel, axes, sizes),
+        functools.partial(exchange_kernel, axes, sizes, width),
         out_shape=(
             jax.ShapeDtypeStruct(lat_shape, jnp.float32),
+            jax.ShapeDtypeStruct(lat_shape, jnp.float32),
+            jax.ShapeDtypeStruct(lon_shape, jnp.float32),
             jax.ShapeDtypeStruct(lon_shape, jnp.float32),
         ),
-        in_specs=[vmem, vmem],
-        out_specs=(vmem, vmem),
+        in_specs=[vmem, vmem, vmem],
+        out_specs=(vmem, vmem, vmem, vmem),
         scratch_shapes=[
             pltpu.VMEM((sizes["lat"],) + lat_shape, jnp.float32),
             pltpu.VMEM((sizes["lon"],) + lon_shape, jnp.float32),
-            pltpu.SemaphoreType.DMA((4,)),
-            pltpu.SemaphoreType.DMA((2,)),
+            pltpu.VMEM(lat_shape, jnp.float32),
+            pltpu.VMEM(lat_shape, jnp.float32),
+            pltpu.VMEM((rows, width, levels), jnp.float32),
+            pltpu.VMEM((rows, width, levels), jnp.float32),
+            pltpu.SemaphoreType.DMA((8,)),
+            pltpu.SemaphoreType.DMA((6,)),
         ],
-        compiler_params=pltpu.CompilerParams(collective_id=kernel_id, has_side_effects=True),
+        compiler_params=pltpu.CompilerParams(collective_id=width - 1, has_side_effects=True),
         cost_estimate=pl.CostEstimate(flops=0, transcendentals=0, bytes_accessed=moved),
-    )(lat_terms, lon_terms)
+    )(field, lat_terms, lon_terms)
 
 
 def surround(field, width, lat_codes, lat_weights, lon_codes, lon_weights, axes):
-    rows_dev, cols_dev, levels = field.shape
-    padded = padded_2(field, (("lat", 0), ("lon", 1)), width)
     lat_terms, lon_terms = rim_terms(field, lat_codes, lat_weights, lon_codes, lon_weights, width)
-    lat_rim, lon_rim = exchange(lat_terms, lon_terms, axes, width - 1)
-    lat_index = lax.axis_index("lat")
-    lon_index = lax.axis_index("lon")
-    last_lat = lax.axis_size("lat") - 1
-    last_lon = lax.axis_size("lon") - 1
-    north = jnp.where(lat_index == 0, lat_rim[::-1], padded[:width, width : width + cols_dev])
-    padded = padded.at[:width, width : width + cols_dev].set(north)
-    south = jnp.where(
-        lat_index == last_lat, lat_rim, padded[width + rows_dev :, width : width + cols_dev]
-    )
-    padded = padded.at[width + rows_dev :, width : width + cols_dev].set(south)
-    west = jnp.where(
-        lon_index == 0,
-        jnp.moveaxis(lon_rim[::-1], 0, 1),
-        padded[width : width + rows_dev, :width],
-    )
-    padded = padded.at[width : width + rows_dev, :width].set(west)
-    east = jnp.where(
-        lon_index == last_lon,
-        jnp.moveaxis(lon_rim, 0, 1),
-        padded[width : width + rows_dev, width + cols_dev :],
-    )
-    padded = padded.at[width : width + rows_dev, width + cols_dev :].set(east)
-    return padded
+    north, south, west, east = exchange(field, lat_terms, lon_terms, axes, width)
+    middle = jnp.concatenate(
+        [jnp.moveaxis(west, 0, 1), field, jnp.moveaxis(east, 0, 1)], axis=1
+    )
+    corners = ((0, 0), (width, width), (0, 0))
+    return jnp.concatenate(
+        [jnp.pad(north, corners), middle, jnp.pad(south, corners)], axis=0
+    )
 
 
 def face_terms(mobility):

time: 180 us -> 117 us (0.65)
  the two profiles are of different devices: /device:TPU:1 before, /device:TPU:2 now
where the time goes in v4:
time: 117 us
  Pallas kernels  63.3 us (54%)
  local copies, waits for them, and re-layouts  36.8 us (31%)
  other arithmetic  15.2 us (13%)
  between operations  1.27 us (1%)
    pallas_call x4, Pallas kernels, exchange(): pl.pallas_call(functools.partial(exchange_kernel, axes, sizes, width), ou...  63.3 us
    gather x16, local copies, waits for them, and re-layouts, rim_terms(): picked = field[jnp.clip(target, 0, rows_dev - 1), cols_at + col_step]  16.3 us
    gather x16, local copies, waits for them, and re-layouts, rim_terms(): picked = field[rows_at + row_step, jnp.clip(target, 0, cols_dev - 1)]  12.1 us
    unnamed x72, local copies, waits for them, and re-layouts  4.47 us
    add x4, other arithmetic, rim_terms(): lat_total + jnp.where(inside, lat_weights[corner, :, :width], 0.0)[..., N...  3.75 us
    add x4, other arithmetic, rim_terms(): lon_total + jnp.where(inside, lon_weights[corner, :, :width], 0.0)[..., N...  2.78 us

profile of v4, /device:TPU:2, one launch (start us, length us, event | category | flops | bytes accessed | tf_op | source)
XLA Modules:
  0.0 116.5 jit_solution(12145939816662271232)
XLA Ops:
  0.6 0.8 fusion.98
  1.4 0.7 fusion.94
  2.2 0.7 fusion.114
  2.9 0.7 fusion.110
  4.5 0.5 copy-done.21
  5.1 0.7 copy-done.30
  6.5 1.0 pad_maximum_fusion.2.field
  7.5 0.9 gather_fusion.7
  8.4 0.9 gather_fusion.6
  9.3 0.9 gather_fusion.5
  10.3 0.9 gather_fusion.4
  11.2 0.7 multiply_add_fusion.1.lon_part
  11.9 1.3 %gather_fusion.3 = f32[128,256]{1,0:T(8,128)S(1)} fusion(f32[16,32,256]{2,1,0:T(8,128)S(1)} %pad_maximum_fusion.2.field, s32[128]{0:T(128)S(1)} %reshape.802), kind=kCustom, calls=%fused_computation.3 | custom fusion | bytes 263168 | tf_op jit(solution)/shard_map/gather | solution.py:35
  13.2 1.3 %gather_fusion.2 = f32[128,256]{1,0:T(8,128)S(1)} fusion(f32[16,32,256]{2,1,0:T(8,128)S(1)} %pad_maximum_fusion.2.field, s32[128]{0:T(128)S(1)} %reshape.796), kind=kCustom, calls=%fused_computation.2 | custom fusion | bytes 263168 | tf_op jit(solution)/shard_map/gather | solution.py:35
  14.5 1.3 %gather_fusion.1 = f32[128,256]{1,0:T(8,128)S(1)} fusion(f32[16,32,256]{2,1,0:T(8,128)S(1)} %pad_maximum_fusion.2.field, s32[128]{0:T(128)S(1)} %reshape.790), kind=kCustom, calls=%fused_computation.1 | custom fusion | bytes 263168 | tf_op jit(solution)/shard_map/gather | solution.py:35
  15.8 1.3 %gather_fusion = f32[128,256]{1,0:T(8,128)S(1)} fusion(f32[16,32,256]{2,1,0:T(8,128)S(1)} %pad_maximum_fusion.2.field, s32[128]{0:T(128)S(1)} %reshape.784), kind=kCustom, calls=%fused_computation | custom fusion | bytes 263168 | tf_op jit(solution)/shard_map/gather | solution.py:35
  17.0 0.8 multiply_add_fusion.lat_part
  17.8 26.5 %shard_map.95 = (f32[2,32,256]{2,1,0:T(8,128)}, f32[2,32,256]{2,1,0:T(8,128)}, f32[2,16,256]{2,1,0:T(8,128)}, f32[2,16,256]{2,1,0:T(8,128)}) custom-call(f32[16,32,256]{2,1,0:T(8,128)} %copy-done, f32[2,2,32,256]{3,2,1,0:T(8,128)} %multiply_add_fusion.lat_part, f32[2,2,16,256]{3,2,1,0:T(8,128)} %multiply_add_fusion.1.lon_part), custom_call_target="tpu_custom_call" | custom-call | bytes 393216 | tf_op jit(solution)/shard_map/pallas_call | solution.py:234
  44.3 0.9 pad.58
  45.2 0.9 pad.59
  46.1 0.8 copy_bitcast_fusion
  47.7 0.7 copy-done.12
  48.4 0.3 copy-done.14
  49.0 0.4 fusion.54.field
  49.4 0.7 gather_fusion.15
  50.1 0.7 gather_fusion.14
  50.8 0.7 gather_fusion.13
  51.5 0.7 gather_fusion.12
  52.2 0.7 multiply_add_fusion.7.lon_part
  52.9 0.9 gather_fusion.11
  53.8 0.9 gather_fusion.10
  54.6 0.9 gather_fusion.9
  55.5 0.9 gather_fusion.8
  56.4 0.7 multiply_add_fusion.4.lat_part
  57.1 13.2 %shard_map.96 = (f32[1,32,128]{2,1,0:T(8,128)}, f32[1,32,128]{2,1,0:T(8,128)}, f32[1,16,128]{2,1,0:T(8,128)}, f32[1,16,128]{2,1,0:T(8,128)}) custom-call(f32[16,32,128]{2,1,0:T(8,128)} %copy-done.3, f32[2,1,32,128]{3,2,1,0:T(8,128)} %multiply_add_fusion.4.lat_part, f32[2,1,16,128]{3,2,1,0:T(8,128)} %multiply_add_fusion.7.lon_part), custom_call_target="tpu_custom_call" | custom-call | bytes 98304 | tf_op jit(solution)/shard_map/pallas_call | solution.py:234
  70.5 0.5 copy-done.24
  71.1 0.3 fusion.46.field
  71.5 0.7 gather_fusion.23
  72.2 0.7 gather_fusion.22
  72.9 0.7 gather_fusion.21
  73.6 0.7 gather_fusion.20
  74.3 0.7 multiply_add_fusion.6.lon_part
  75.0 0.9 gather_fusion.19
  75.8 0.9 gather_fusion.18
  76.7 0.9 gather_fusion.17
  77.6 0.9 gather_fusion.16
  78.5 0.7 multiply_add_fusion.3.lat_part
  79.3 11.8 %shard_map.97 = (f32[1,32,128]{2,1,0:T(8,128)}, f32[1,32,128]{2,1,0:T(8,128)}, f32[1,16,128]{2,1,0:T(8,128)}, f32[1,16,128]{2,1,0:T(8,128)}) custom-call(f32[16,32,128]{2,1,0:T(8,128)} %copy-done.5, f32[2,1,32,128]{3,2,1,0:T(8,128)} %multiply_add_fusion.3.lat_part, f32[2,1,16,128]{3,2,1,0:T(8,128)} %multiply_add_fusion.6.lon_part), custom_call_target="tpu_custom_call" | custom-call | bytes 98304 | tf_op jit(solution)/shard_map/pallas_call | solution.py:234
  91.3 0.5 copy-done.22
  91.9 0.3 fusion.28.field
  92.2 0.7 gather_fusion.31
  92.9 0.7 gather_fusion.30
  93.6 0.7 gather_fusion.29
  94.3 0.7 gather_fusion.28
  95.0 0.7 multiply_add_fusion.5.lon_part
  95.7 0.9 gather_fusion.27
  96.6 0.9 gather_fusion.26
  97.5 0.9 gather_fusion.25
  98.4 1.5 %gather_fusion.24 = f32[64,128]{1,0:T(8,128)} fusion(f32[16,32,128]{2,1,0:T(8,128)S(1)} %fusion.28.field, s32[64]{0:T(128)S(1)} %reshape.834), kind=kCustom, calls=%fused_computation.24 | custom fusion | bytes 66048 | tf_op jit(solution)/shard_map/gather | solution.py:35
  99.9 1.5 %multiply_add_fusion.2.lat_part = f32[2,1,32,128]{3,2,1,0:T(8,128)} fusion(f32[2,1,32,128]{3,2,1,0:T(8,128)S(1)} %bitcast.269, f32[2,1,32,128]{3,2,1,0:T(8,128)S(1)} %bitcast.270, f32[2,1,32,128]{3,2,1,0:T(8,128)S(1)} %bitcast.271, f32[2,1,32,128]{3,2,1,0:T(8,128)} %bitcast.272, f32[2,32]{1,0:T(2,128)S(1)} %bitcast.315, f32[2,32]{1,0:T(2,128)S(1)} %bitcast.318, ...), kind=kLoop, calls=%fused_computation.165 | loop fusion | flops 57344 | bytes 164864 | tf_op jit(solution)/shard_map/add | solution.py:37
  101.4 11.8 %shard_map.98 = (f32[1,32,128]{2,1,0:T(8,128)}, f32[1,32,128]{2,1,0:T(8,128)}, f32[1,16,128]{2,1,0:T(8,128)}, f32[1,16,128]{2,1,0:T(8,128)}) custom-call(f32[16,32,128]{2,1,0:T(8,128)} %copy-done.1, f32[2,1,32,128]{3,2,1,0:T(8,128)} %multiply_add_fusion.2.lat_part, f32[2,1,16,128]{3,2,1,0:T(8,128)} %multiply_add_fusion.5.lon_part), custom_call_target="tpu_custom_call" | custom-call | bytes 98304 | tf_op jit(solution)/shard_map/pallas_call | solution.py:234
  113.3 0.7 copy-done.17
  114.0 1.0 fusion.8
  115.6 0.9 fusion.23
  (120 shorter events, 3.7 us)
Async XLA Ops:
  0.6 5.9 %copy-start.7 = (f32[1,16,32,128]{3,2,1,0:T(8,128)S(1)}, f32[1,16,32,128]{3,2,1,0:T(8,128)}, u32[]{:S(2)}) copy-start(f32[1,16,32,128]{3,2,1,0:T(8,128)} %param.9) | copy-start | bytes 786436
  2.9 75.6 %copy-start.28 = (f32[2,1,32]{2,1,0:T(1,128)}, f32[2,1,32]{2,1,0:T(1,128)S(1)}, u32[]{:S(2)}) copy-start(f32[2,1,32]{2,1,0:T(1,128)S(1)} %get-tuple-element.39) | copy-start | bytes 772
  3.7 74.9 %copy-start.26 = (f32[2,1,32]{2,1,0:T(1,128)}, f32[2,1,32]{2,1,0:T(1,128)S(1)}, u32[]{:S(2)}) copy-start(f32[2,1,32]{2,1,0:T(1,128)S(1)} %get-tuple-element.75) | copy-start | bytes 772
  4.3 0.7 copy-start.21
  4.3 0.7 copy-start.31
  4.3 0.7 copy-start.20
  5.0 0.7 copy-start.30
  7.5 8.2 %copy-start = (f32[16,32,256]{2,1,0:T(8,128)}, f32[16,32,256]{2,1,0:T(8,128)S(1)}, u32[]{:S(2)}) copy-start(f32[16,32,256]{2,1,0:T(8,128)S(1)} %pad_maximum_fusion.2.field) | copy-start | bytes 1572868
  44.3 2.6 %copy-start.8 = (f32[1,16,32,128]{3,2,1,0:T(8,128)S(1)}, f32[1,16,32,128]{3,2,1,0:T(8,128)}, u32[]{:S(2)}) copy-start(f32[1,16,32,128]{3,2,1,0:T(8,128)} %param.8) | copy-start | bytes 786436
  45.2 0.9 copy-start.19
  47.5 0.9 copy-start.12
  47.5 1.2 copy-start.14
  47.5 1.3 %copy-start.9 = (f32[1,16,32,128]{3,2,1,0:T(8,128)S(1)}, f32[1,16,32,128]{3,2,1,0:T(8,128)}, u32[]{:S(2)}) copy-start(f32[1,16,32,128]{3,2,1,0:T(8,128)} %param.11) | copy-start | bytes 786436
  47.5 1.4 %copy-start.16 = (f32[1,16,32,128]{3,2,1,0:T(8,128)S(1)}, f32[1,16,32,128]{3,2,1,0:T(8,128)}, u32[]{:S(2)}) copy-start(f32[1,16,32,128]{3,2,1,0:T(8,128)} %param.10) | copy-start | bytes 786436
  47.7 1.2 %copy-start.10 = (f32[16,34,256]{2,1,0:T(8,128)}, f32[16,34,256]{2,1,0:T(8,128)S(1)}, u32[]{:S(2)}) copy-start(f32[16,34,256]{2,1,0:T(8,128)S(1)} %get-tuple-element.63) | copy-start | bytes 1671172
  49.4 6.2 %copy-start.3 = (f32[16,32,128]{2,1,0:T(8,128)}, f32[16,32,128]{2,1,0:T(8,128)S(1)}, u32[]{:S(2)}) copy-start(f32[16,32,128]{2,1,0:T(8,128)S(1)} %fusion.54.field) | copy-start | bytes 786436
  56.4 13.9 %copy-start.4 = (f32[16,32,128]{2,1,0:T(8,128)S(1)}, f32[16,32,128]{2,1,0:T(8,128)}, u32[]{:S(2)}) copy-start(f32[16,32,128]{2,1,0:T(8,128)} %copy-done.3) | copy-start | bytes 786436
  70.4 0.7 copy-start.24
  70.4 0.7 copy-start.25
  70.4 0.7 copy-start.34
  70.4 0.7 copy-start.35
  71.4 6.2 %copy-start.5 = (f32[16,32,128]{2,1,0:T(8,128)}, f32[16,32,128]{2,1,0:T(8,128)S(1)}, u32[]{:S(2)}) copy-start(f32[16,32,128]{2,1,0:T(8,128)S(1)} %fusion.46.field) | copy-start | bytes 786436
  78.5 12.6 %copy-start.6 = (f32[16,32,128]{2,1,0:T(8,128)S(1)}, f32[16,32,128]{2,1,0:T(8,128)}, u32[]{:S(2)}) copy-start(f32[16,32,128]{2,1,0:T(8,128)} %copy-done.5) | copy-start | bytes 786436
  91.1 0.7 copy-start.22
  91.1 0.7 copy-start.23
  91.1 0.7 copy-start.32
  91.1 0.7 copy-start.33
  92.2 6.2 %copy-start.1 = (f32[16,32,128]{2,1,0:T(8,128)}, f32[16,32,128]{2,1,0:T(8,128)S(1)}, u32[]{:S(2)}) copy-start(f32[16,32,128]{2,1,0:T(8,128)S(1)} %fusion.28.field) | copy-start | bytes 786436
  95.7 4.2 %copy-start.27 = (f32[2,1,32]{2,1,0:T(1,128)S(1)}, f32[2,1,32]{2,1,0:T(1,128)}, u32[]{:S(2)}) copy-start(f32[2,1,32]{2,1,0:T(1,128)} %copy-done.26) | copy-start | bytes 772
  95.7 4.2 %copy-start.29 = (f32[2,1,32]{2,1,0:T(1,128)S(1)}, f32[2,1,32]{2,1,0:T(1,128)}, u32[]{:S(2)}) copy-start(f32[2,1,32]{2,1,0:T(1,128)} %copy-done.28) | copy-start | bytes 772
  95.7 17.6 %copy-start.15 = (f32[18,36,256]{2,1,0:T(8,128)S(1)}, f32[18,36,256]{2,1,0:T(8,128)}, u32[]{:S(2)}) copy-start(f32[18,36,256]{2,1,0:T(8,128)} %copy-done.14) | copy-start | bytes 1990660
  96.6 16.7 %copy-start.13 = (f32[18,36,256]{2,1,0:T(8,128)S(1)}, f32[18,36,256]{2,1,0:T(8,128)}, u32[]{:S(2)}) copy-start(f32[18,36,256]{2,1,0:T(8,128)} %copy-done.12) | copy-start | bytes 1990660
  99.9 13.4 %copy-start.2 = (f32[16,32,128]{2,1,0:T(8,128)S(1)}, f32[16,32,128]{2,1,0:T(8,128)}, u32[]{:S(2)}) copy-start(f32[16,32,128]{2,1,0:T(8,128)} %copy-done.1) | copy-start | bytes 786436
  113.3 0.7 copy-start.17
  114.0 1.1 copy-start.11
  114.0 1.1 copy-start.18

commit v5 on v4

--- a/solution.py
+++ b/solution.py
@@ -21,32 +21,42 @@
     return jnp.pad(values, widths)
 
 
-def rim_terms(field, lat_codes, lat_weights, lon_codes, lon_weights, width):
-    rows_dev, cols_dev, levels = field.shape
+def rim_plan(lat_codes, lat_weights, lon_codes, lon_weights, width, rows_dev, cols_dev):
     first_row = lax.axis_index("lat") * rows_dev
     first_col = lax.axis_index("lon") * cols_dev
+    rows, cols, weights = [], [], []
     chosen = lat_codes[:, :width]
     rows_at = chosen // cols_dev - first_row
     cols_at = chosen % cols_dev
-    lat_total = jnp.zeros(chosen.shape + (levels,), jnp.float32)
     for corner, (row_step, col_step) in enumerate(stencil_offsets):
         target = rows_at + row_step
         inside = (target >= 0) & (target < rows_dev)
-        picked = field[jnp.clip(target, 0, rows_dev - 1), cols_at + col_step]
-        lat_total = (
-            lat_total + jnp.where(inside, lat_weights[corner, :, :width], 0.0)[..., None] * picked
-        )
+        rows.append([jnp.clip(target, 0, rows_dev - 1).reshape(-1)])
+        cols.append([(cols_at + col_step).reshape(-1)])
+        weights.append([jnp.where(inside, lat_weights[corner, :, :width], 0.0).reshape(-1)])
     chosen = lon_codes[:, :width]
     cols_at = chosen // rows_dev - first_col
     rows_at = chosen % rows_dev
-    lon_total = jnp.zeros(chosen.shape + (levels,), jnp.float32)
     for corner, (row_step, col_step) in enumerate(stencil_offsets):
         target = cols_at + col_step
         inside = (target >= 0) & (target < cols_dev)
-        picked = field[rows_at + row_step, jnp.clip(target, 0, cols_dev - 1)]
-        lon_total = (
-            lon_total + jnp.where(inside, lon_weights[corner, :, :width], 0.0)[..., None] * picked
-        )
+        rows[corner].append((rows_at + row_step).reshape(-1))
+        cols[corner].append(jnp.clip(target, 0, cols_dev - 1).reshape(-1))
+        weights[corner].append(jnp.where(inside, lon_weights[corner, :, :width], 0.0).reshape(-1))
+    join = lambda parts: jnp.stack([jnp.concatenate(p) for p in parts])
+    return join(rows), join(cols), join(weights)
+
+
+def rim_terms(field, plan, width):
+    rows_dev, cols_dev, levels = field.shape
+    rows, cols, weights = plan
+    picked = field[rows, cols]
+    total = jnp.zeros(picked.shape[1:], jnp.float32)
+    for corner in range(len(stencil_offsets)):
+        total = total + weights[corner][:, None] * picked[corner]
+    lat_count = 2 * width * cols_dev
+    lat_total = total[:lat_count].reshape(2, width, cols_dev, levels)
+    lon_total = total[lat_count:].reshape(2, width, rows_dev, levels)
     return (lat_total, lon_total)
 
 
@@ -256,8 +266,8 @@
     )(field, lat_terms, lon_terms)
 
 
-def surround(field, width, lat_codes, lat_weights, lon_codes, lon_weights, axes):
-    lat_terms, lon_terms = rim_terms(field, lat_codes, lat_weights, lon_codes, lon_weights, width)
+def surround(field, width, plan, axes):
+    lat_terms, lon_terms = rim_terms(field, plan, width)
     north, south, west, east = exchange(field, lat_terms, lon_terms, axes, width)
     middle = jnp.concatenate(
         [jnp.moveaxis(west, 0, 1), field, jnp.moveaxis(east, 0, 1)], axis=1
@@ -329,16 +339,14 @@
     lat_weight_now = lat_weights[0]
     lon_code_now = lon_codes[0]
     lon_weight_now = lon_weights[0]
-    levels = porosity_now.shape[-1]
-    both_pad = surround(
-        jnp.concatenate([porosity_now, current], axis=-1),
-        2,
-        lat_code_now,
-        lat_weight_now,
-        lon_code_now,
-        lon_weight_now,
-        axes,
-    )
+    rows_dev, cols_dev, levels = porosity_now.shape
+    plans = {
+        width: rim_plan(
+            lat_code_now, lat_weight_now, lon_code_now, lon_weight_now, width, rows_dev, cols_dev
+        )
+        for width in (1, 2)
+    }
+    both_pad = surround(jnp.concatenate([porosity_now, current], axis=-1), 2, plans[2], axes)
     porosity_pad = both_pad[..., :levels]
     first_pad = both_pad[1:-1, 1:-1, levels:]
     near = porosity_pad[1:-1, 1:-1, :]
@@ -349,13 +357,9 @@
         if sweep_index == 0:
             padded = first_pad
         else:
-            padded = surround(
-                current, 1, lat_code_now, lat_weight_now, lon_code_now, lon_weight_now, axes
-            )
+            padded = surround(current, 1, plans[1], axes)
         current = neighbour_total(padded, source_now, lat_face, lon_face, mean_rad) / denominator
-    pressure_pad = surround(
-        current, 1, lat_code_now, lat_weight_now, lon_code_now, lon_weight_now, axes
-    )
+    pressure_pad = surround(current, 1, plans[1], axes)
     porosity_new = advect(pressure_pad, porosity_pad, lat_face, lon_face, mean_rad, bulk_now)
     return (current[None], porosity_new[None])
 

time: 117 us -> 108 us (0.923)
  other arithmetic: 15.2 us -> 9.84 us
  local copies, waits for them, and re-layouts: 36.8 us -> 32.8 us
    gather x32 -> x4, local copies, waits for them, and re-layouts: 28.4 us -> 16.5 us  [rim_terms(): picked = field[rows, cols]]
    slice x0 -> x10, local copies, waits for them, and re-layouts: none -> 6.42 us  [the longest x4 2.51 us: rim_terms(): lat_total = total[:lat_count].reshape(2, width, cols_dev, levels)]
    add x8 -> x6, other arithmetic: 6.53 us -> 0.55 us  [the longest x4 0.53 us: rim_terms(): total = total + weights[corner][:, None] * picked[corner]]
    squeeze x0 -> x10, local copies, waits for them, and re-layouts: none -> 2.23 us  [the longest x1 0.81 us: body(): lat_code_now = lat_codes[0]]
    select_n x14 -> x6, other arithmetic: 2.99 us -> 1.6 us  [the longest x3 0.8 us: rim_plan(): jnp.where(inside, lon_weights[corner, :, :width], 0.0).reshape(-1)]
    min x0 -> x4, other arithmetic: none -> 1.35 us  [the longest x2 0.68 us: rim_plan(): rows.append([jnp.clip(target, 0, rows_dev - 1).reshape(-1)])]
    reshape x0 -> x16, local copies, waits for them, and re-layouts: none -> 1.3 us  [the longest x4 0.32 us: rim_plan(): jnp.where(inside, lat_weights[corner, :, :width], 0.0).reshape(-1)]
    unnamed x72 -> x56, local copies, waits for them, and re-layouts: 4.47 us -> 3.89 us
where the time goes in v5:
time: 108 us; the launch traced here: 107 us
  Pallas kernels  63.2 us (59%)
  local copies, waits for them, and re-layouts  32.8 us (30%)
  other arithmetic  9.84 us (9%)
  between operations  1.2 us (1%)
    pallas_call x4, Pallas kernels, exchange(): pl.pallas_call(functools.partial(exchange_kernel, axes, sizes, width), ou...  63.2 us
    gather x4, local copies, waits for them, and re-layouts, rim_terms(): picked = field[rows, cols]  16.5 us
    unnamed x56, local copies, waits for them, and re-layouts  3.89 us
    slice x4, local copies, waits for them, and re-layouts, rim_terms(): lat_total = total[:lat_count].reshape(2, width, cols_dev, levels)  2.51 us
    slice x4, local copies, waits for them, and re-layouts, rim_terms(): lon_total = total[lat_count:].reshape(2, width, rows_dev, levels)  2.43 us

profile of v5, /device:TPU:2, one launch (start us, length us, event | category | flops | bytes accessed | tf_op | source)
XLA Modules:
  0.0 107.1 jit_solution(10367493777441239429)
XLA Ops:
  0.6 0.8 squeeze.127
  1.5 0.8 squeeze.129
  2.2 0.8 fusion.100
  3.0 0.1 reshape.803
  3.3 0.5 broadcast.664
  3.9 0.7 clamp_reduce_fusion.1
  4.5 0.1 reshape.809
  4.9 0.8 fusion.102
  6.1 0.7 clamp_reduce_fusion.3
  7.5 0.1 reshape.830
  7.6 0.7 fusion.113
  8.3 0.1 squeeze.132
  8.4 0.1 squeeze.135
  8.5 0.1 squeeze.128
  8.6 0.1 squeeze.138
  8.7 0.7 fusion.114
  9.4 0.1 squeeze.133
  9.5 0.1 squeeze.136
  9.6 0.1 squeeze.130
  9.7 0.1 squeeze.139
  9.9 1.0 pad_maximum_fusion.2.field
  10.9 5.5 %gather_fusion = f32[768,256]{1,0:T(8,128)S(1)} fusion(f32[16,32,256]{2,1,0:T(8,128)S(1)} %pad_maximum_fusion.2.field, s32[768]{0:T(1024)S(1)} %reshape.824), kind=kCustom, calls=%fused_computation | custom fusion | bytes 1579008 | tf_op jit(solution)/shard_map/gather | solution.py:53
  16.5 0.2 fusion.63
  16.6 0.6 slice.474
  17.3 0.7 slice.473
  17.9 26.5 %shard_map.95 = (f32[2,32,256]{2,1,0:T(8,128)}, f32[2,32,256]{2,1,0:T(8,128)}, f32[2,16,256]{2,1,0:T(8,128)}, f32[2,16,256]{2,1,0:T(8,128)}) custom-call(f32[16,32,256]{2,1,0:T(8,128)} %copy-done, f32[2,2,32,256]{3,2,1,0:T(8,128)} %bitcast.149, f32[2,2,16,256]{3,2,1,0:T(8,128)} %bitcast.150), custom_call_target="tpu_custom_call" | custom-call | bytes 393216 | tf_op jit(solution)/shard_map/pallas_call | solution.py:244
  44.4 0.9 pad.58
  45.3 0.9 pad.59
  46.2 0.7 copy-done.18
  47.2 0.1 slice_multiply_fusion.13
  47.3 0.1 slice_multiply_fusion.12
  47.5 0.1 maximum_maximum_fusion
  47.6 0.1 maximum_maximum_fusion.1
  47.8 0.7 copy-done.12
  48.5 0.2 copy-done.14
  48.7 0.2 copy-done.10
  48.9 0.1 copy-done.15
  49.1 0.4 fusion.54.field
  49.4 3.7 %gather_fusion.1 = f32[384,128]{1,0:T(8,128)S(1)} fusion(f32[16,32,128]{2,1,0:T(8,128)S(1)} %fusion.54.field, s32[384]{0:T(512)S(1)} %reshape.830), kind=kCustom, calls=%fused_computation.1 | custom fusion | bytes 396288 | tf_op jit(solution)/shard_map/gather | solution.py:53
  53.1 0.1 fusion.72
  53.2 0.6 slice.506
  53.8 0.6 slice.505
  54.5 13.0 %shard_map.96 = (f32[1,32,128]{2,1,0:T(8,128)}, f32[1,32,128]{2,1,0:T(8,128)}, f32[1,16,128]{2,1,0:T(8,128)}, f32[1,16,128]{2,1,0:T(8,128)}) custom-call(f32[16,32,128]{2,1,0:T(8,128)} %copy-done.5, f32[2,1,32,128]{3,2,1,0:T(8,128)} %bitcast.151, f32[2,1,16,128]{3,2,1,0:T(8,128)} %bitcast.154), custom_call_target="tpu_custom_call" | custom-call | bytes 98304 | tf_op jit(solution)/shard_map/pallas_call | solution.py:244
  67.5 0.1 slice_multiply_fusion.11
  67.7 0.5 copy-done.22
  68.2 0.3 fusion.46.field
  68.6 3.7 %gather_fusion.2 = f32[384,128]{1,0:T(8,128)S(1)} fusion(f32[16,32,128]{2,1,0:T(8,128)S(1)} %fusion.46.field, s32[384]{0:T(512)S(1)} %reshape.830), kind=kCustom, calls=%fused_computation.2 | custom fusion | bytes 396288 | tf_op jit(solution)/shard_map/gather | solution.py:53
  72.3 0.1 fusion.69
  72.4 0.6 slice.514
  73.0 0.6 slice.513
  73.6 11.8 %shard_map.97 = (f32[1,32,128]{2,1,0:T(8,128)}, f32[1,32,128]{2,1,0:T(8,128)}, f32[1,16,128]{2,1,0:T(8,128)}, f32[1,16,128]{2,1,0:T(8,128)}) custom-call(f32[16,32,128]{2,1,0:T(8,128)} %copy-done.3, f32[2,1,32,128]{3,2,1,0:T(8,128)} %bitcast.152, f32[2,1,16,128]{3,2,1,0:T(8,128)} %bitcast.155), custom_call_target="tpu_custom_call" | custom-call | bytes 98304 | tf_op jit(solution)/shard_map/pallas_call | solution.py:244
  85.5 0.1 slice_multiply_fusion.9
  85.7 0.5 copy-done.20
  86.2 0.3 fusion.28.field
  86.6 3.7 %gather_fusion.3 = f32[384,128]{1,0:T(8,128)S(1)} fusion(f32[16,32,128]{2,1,0:T(8,128)S(1)} %fusion.28.field, s32[384]{0:T(512)S(1)} %reshape.830), kind=kCustom, calls=%fused_computation.3 | custom fusion | bytes 396288 | tf_op jit(solution)/shard_map/gather | solution.py:53
  90.3 0.1 fusion.66
  90.4 0.6 slice.522
  91.0 0.6 slice.521
  91.6 11.9 %shard_map.98 = (f32[1,32,128]{2,1,0:T(8,128)}, f32[1,32,128]{2,1,0:T(8,128)}, f32[1,16,128]{2,1,0:T(8,128)}, f32[1,16,128]{2,1,0:T(8,128)}) custom-call(f32[16,32,128]{2,1,0:T(8,128)} %copy-done.1, f32[2,1,32,128]{3,2,1,0:T(8,128)} %bitcast.153, f32[2,1,16,128]{3,2,1,0:T(8,128)} %bitcast.156), custom_call_target="tpu_custom_call" | custom-call | bytes 98304 | tf_op jit(solution)/shard_map/pallas_call | solution.py:244
  103.5 0.7 copy-done.16
  104.2 1.4 %fusion.8 = f32[17,32,128]{2,1,0:T(8,128)S(1)} fusion(f32[18,36,256]{2,1,0:T(8,128)} %copy-done.14, f32[18,36,256]{2,1,0:T(8,128)S(1)} %copy-done.13, f32[16,1,128]{2,1,0:T(1,128)} %bitcast.159, f32[16,32,128]{2,1,0:T(8,128)S(1)} %copy-done.2, f32[16,1,128]{2,1,0:T(1,128)S(1)} %bitcast.157, f32[1,32,128]{2,1,0:T(8,128)} %get-tuple-element.33, ...), kind=kLoop, calls=%fused_computation.30 | loop fusion | flops 1671168 | bytes 2260992 | tf_op jit(solution)/shard_map/mul | solution.py:317
  105.6 0.3 fusion.2
  105.9 0.3 fusion.15
  106.2 0.9 fusion.23
  (88 shorter events, 2.2 us)
Async XLA Ops:
  0.6 9.3 %copy-start.7 = (f32[1,16,32,128]{3,2,1,0:T(8,128)S(1)}, f32[1,16,32,128]{3,2,1,0:T(8,128)}, u32[]{:S(2)}) copy-start(f32[1,16,32,128]{3,2,1,0:T(8,128)} %param.9) | copy-start | bytes 786436
  10.9 5.5 %copy-start = (f32[16,32,256]{2,1,0:T(8,128)}, f32[16,32,256]{2,1,0:T(8,128)S(1)}, u32[]{:S(2)}) copy-start(f32[16,32,256]{2,1,0:T(8,128)S(1)} %pad_maximum_fusion.2.field) | copy-start | bytes 1572868
  44.4 2.6 %copy-start.8 = (f32[1,16,32,128]{3,2,1,0:T(8,128)S(1)}, f32[1,16,32,128]{3,2,1,0:T(8,128)}, u32[]{:S(2)}) copy-start(f32[1,16,32,128]{3,2,1,0:T(8,128)} %param.8) | copy-start | bytes 786436
  45.3 0.9 copy-start.19
  46.2 0.8 copy-start.18
  47.6 0.9 copy-start.12
  47.6 1.1 %copy-start.14 = (f32[18,36,256]{2,1,0:T(8,128)}, f32[18,36,256]{2,1,0:T(8,128)S(1)}, u32[]{:S(2)}) copy-start(f32[18,36,256]{2,1,0:T(8,128)S(1)} %get-tuple-element.65) | copy-start | bytes 1990660
  47.6 1.3 %copy-start.9 = (f32[1,16,32,128]{3,2,1,0:T(8,128)S(1)}, f32[1,16,32,128]{3,2,1,0:T(8,128)}, u32[]{:S(2)}) copy-start(f32[1,16,32,128]{3,2,1,0:T(8,128)} %param.11) | copy-start | bytes 786436
  47.6 1.4 %copy-start.15 = (f32[1,16,32,128]{3,2,1,0:T(8,128)S(1)}, f32[1,16,32,128]{3,2,1,0:T(8,128)}, u32[]{:S(2)}) copy-start(f32[1,16,32,128]{3,2,1,0:T(8,128)} %param.10) | copy-start | bytes 786436
  47.8 1.2 %copy-start.10 = (f32[16,34,256]{2,1,0:T(8,128)}, f32[16,34,256]{2,1,0:T(8,128)S(1)}, u32[]{:S(2)}) copy-start(f32[16,34,256]{2,1,0:T(8,128)S(1)} %get-tuple-element.71) | copy-start | bytes 1671172
  49.4 3.7 %copy-start.5 = (f32[16,32,128]{2,1,0:T(8,128)}, f32[16,32,128]{2,1,0:T(8,128)S(1)}, u32[]{:S(2)}) copy-start(f32[16,32,128]{2,1,0:T(8,128)S(1)} %fusion.54.field) | copy-start | bytes 786436
  53.2 14.3 %copy-start.6 = (f32[16,32,128]{2,1,0:T(8,128)S(1)}, f32[16,32,128]{2,1,0:T(8,128)}, u32[]{:S(2)}) copy-start(f32[16,32,128]{2,1,0:T(8,128)} %copy-done.5) | copy-start | bytes 786436
  67.5 0.7 copy-start.22
  67.5 0.7 copy-start.23
  67.5 0.7 copy-start.26
  67.5 0.7 copy-start.27
  68.6 3.7 %copy-start.3 = (f32[16,32,128]{2,1,0:T(8,128)}, f32[16,32,128]{2,1,0:T(8,128)S(1)}, u32[]{:S(2)}) copy-start(f32[16,32,128]{2,1,0:T(8,128)S(1)} %fusion.46.field) | copy-start | bytes 786436
  72.4 13.1 %copy-start.4 = (f32[16,32,128]{2,1,0:T(8,128)S(1)}, f32[16,32,128]{2,1,0:T(8,128)}, u32[]{:S(2)}) copy-start(f32[16,32,128]{2,1,0:T(8,128)} %copy-done.3) | copy-start | bytes 786436
  85.5 0.7 copy-start.20
  85.5 0.7 copy-start.21
  85.5 0.7 copy-start.24
  85.5 0.7 copy-start.25
  86.6 3.7 %copy-start.1 = (f32[16,32,128]{2,1,0:T(8,128)}, f32[16,32,128]{2,1,0:T(8,128)S(1)}, u32[]{:S(2)}) copy-start(f32[16,32,128]{2,1,0:T(8,128)S(1)} %fusion.28.field) | copy-start | bytes 786436
  86.6 16.9 %copy-start.13 = (f32[18,36,256]{2,1,0:T(8,128)S(1)}, f32[18,36,256]{2,1,0:T(8,128)}, u32[]{:S(2)}) copy-start(f32[18,36,256]{2,1,0:T(8,128)} %copy-done.12) | copy-start | bytes 1990660
  90.4 13.1 %copy-start.2 = (f32[16,32,128]{2,1,0:T(8,128)S(1)}, f32[16,32,128]{2,1,0:T(8,128)}, u32[]{:S(2)}) copy-start(f32[16,32,128]{2,1,0:T(8,128)} %copy-done.1) | copy-start | bytes 786436
  103.5 0.7 copy-start.16
  104.2 1.4 %copy-start.11 = (f32[16,34,256]{2,1,0:T(8,128)S(1)}, f32[16,34,256]{2,1,0:T(8,128)}, u32[]{:S(2)}) copy-start(f32[16,34,256]{2,1,0:T(8,128)} %copy-done.10) | copy-start | bytes 1671172
  104.2 1.4 %copy-start.17 = (f32[1,16,128]{2,1,0:T(8,128)S(1)}, f32[1,16,128]{2,1,0:T(8,128)}, u32[]{:S(2)}) copy-start(f32[1,16,128]{2,1,0:T(8,128)} %get-tuple-element.31) | copy-start | bytes 24580

commit v6 on v5

--- a/solution.py
+++ b/solution.py
@@ -54,10 +54,7 @@
     total = jnp.zeros(picked.shape[1:], jnp.float32)
     for corner in range(len(stencil_offsets)):
         total = total + weights[corner][:, None] * picked[corner]
-    lat_count = 2 * width * cols_dev
-    lat_total = total[:lat_count].reshape(2, width, cols_dev, levels)
-    lon_total = total[lat_count:].reshape(2, width, rows_dev, levels)
-    return (lat_total, lon_total)
+    return total
 
 
 def exchange_kernel(
@@ -65,8 +62,7 @@
     sizes,
     width,
     field,
-    lat_part,
-    lon_part,
+    rim,
     north,
     south,
     west,
@@ -94,11 +90,15 @@
         return tuple(coords[name] for name in axes)
 
     always = lat >= 0
+    lat_span = width * cols
+    lon_span = width * rows
+    lat_part = [rim.at[pl.ds(edge * lat_span, lat_span)] for edge in range(2)]
+    lon_part = [rim.at[pl.ds(2 * lat_span + edge * lon_span, lon_span)] for edge in range(2)]
     routes = (
-        (always, lat_part.at[0], lat_buf.at[lat], 0, device(other, 0, lon)),
-        (always, lat_part.at[1], lat_buf.at[lat], 0, device(other, last_lat, lon)),
-        (always, lon_part.at[0], lon_buf.at[lon], 1, device(other, lat, 0)),
-        (always, lon_part.at[1], lon_buf.at[lon], 1, device(other, lat, last_lon)),
+        (always, lat_part[0], lat_buf.at[lat], 0, device(other, 0, lon)),
+        (always, lat_part[1], lat_buf.at[lat], 0, device(other, last_lat, lon)),
+        (always, lon_part[0], lon_buf.at[lon], 1, device(other, lat, 0)),
+        (always, lon_part[1], lon_buf.at[lon], 1, device(other, lat, last_lon)),
         (
             lat < last_lat,
             field.at[pl.ds(rows - width, width)],
@@ -195,7 +195,7 @@
     def _():
         total = jnp.sum(lat_buf[...], axis=0)
         for depth in range(width):
-            north[width - 1 - depth] = total[depth]
+            north[width - 1 - depth] = total[depth * cols : (depth + 1) * cols]
 
     @pl.when(lat > 0)
     def _():
@@ -204,7 +204,9 @@
 
     @pl.when(lat == last_lat)
     def _():
-        south[...] = jnp.sum(lat_buf[...], axis=0)
+        total = jnp.sum(lat_buf[...], axis=0)
+        for depth in range(width):
+            south[depth] = total[depth * cols : (depth + 1) * cols]
 
     @pl.when(lat < last_lat)
     def _():
@@ -215,7 +217,7 @@
     def _():
         total = jnp.sum(lon_buf[...], axis=0)
         for depth in range(width):
-            west[width - 1 - depth] = total[depth]
+            west[width - 1 - depth] = total[depth * rows : (depth + 1) * rows]
 
     @pl.when(lon > 0)
     def _():
@@ -225,7 +227,9 @@
 
     @pl.when(lon == last_lon)
     def _():
-        east[...] = jnp.sum(lon_buf[...], axis=0)
+        total = jnp.sum(lon_buf[...], axis=0)
+        for depth in range(width):
+            east[depth] = total[depth * rows : (depth + 1) * rows]
 
     @pl.when(lon < last_lon)
     def _():
@@ -234,13 +238,13 @@
             east[depth] = east_buf[:, depth, :]
 
 
-def exchange(field, lat_terms, lon_terms, axes, width):
+def exchange(field, rim, axes, width):
     sizes = {name: lax.axis_size(name) for name in ("lat", "lon")}
     rows, cols, levels = field.shape
     lat_shape = (width, cols, levels)
     lon_shape = (width, rows, levels)
     vmem = pl.BlockSpec(memory_space=pltpu.VMEM)
-    moved = 4 * (lat_terms.size + lon_terms.size + 2 * width * (rows + cols) * levels)
+    moved = 4 * (rim.size + 2 * width * (rows + cols) * levels)
     return pl.pallas_call(
         functools.partial(exchange_kernel, axes, sizes, width),
         out_shape=(
@@ -249,11 +253,11 @@
             jax.ShapeDtypeStruct(lon_shape, jnp.float32),
             jax.ShapeDtypeStruct(lon_shape, jnp.float32),
         ),
-        in_specs=[vmem, vmem, vmem],
+        in_specs=[vmem, vmem],
         out_specs=(vmem, vmem, vmem, vmem),
         scratch_shapes=[
-            pltpu.VMEM((sizes["lat"],) + lat_shape, jnp.float32),
-            pltpu.VMEM((sizes["lon"],) + lon_shape, jnp.float32),
+            pltpu.VMEM((sizes["lat"], width * cols, levels), jnp.float32),
+            pltpu.VMEM((sizes["lon"], width * rows, levels), jnp.float32),
             pltpu.VMEM(lat_shape, jnp.float32),
             pltpu.VMEM(lat_shape, jnp.float32),
             pltpu.VMEM((rows, width, levels), jnp.float32),
@@ -263,12 +267,12 @@
         ],
         compiler_params=pltpu.CompilerParams(collective_id=width - 1, has_side_effects=True),
         cost_estimate=pl.CostEstimate(flops=0, transcendentals=0, bytes_accessed=moved),
-    )(field, lat_terms, lon_terms)
+    )(field, rim)
 
 
 def surround(field, width, plan, axes):
-    lat_terms, lon_terms = rim_terms(field, plan, width)
-    north, south, west, east = exchange(field, lat_terms, lon_terms, axes, width)
+    rim = rim_terms(field, plan, width)
+    north, south, west, east = exchange(field, rim, axes, width)
     middle = jnp.concatenate(
         [jnp.moveaxis(west, 0, 1), field, jnp.moveaxis(east, 0, 1)], axis=1
     )

time: 108 us -> 106 us (0.981)
  local copies, waits for them, and re-layouts: 32.8 us -> 27.9 us
  other arithmetic: 9.84 us -> 12.4 us
    slice x8 -> x0, local copies, waits for them, and re-layouts: 4.95 us -> none  [the longest x4 2.51 us: rim_terms(): lat_total = total[:lat_count].reshape(2, width, cols_dev, levels)]
    add x4, other arithmetic: 0.53 us -> 3.07 us  [rim_terms(): total = total + weights[corner][:, None] * picked[corner]]
where the time goes in v6:
time: 106 us; the launch traced here: 105 us
  Pallas kernels  63.5 us (60%)
  local copies, waits for them, and re-layouts  27.9 us (26%)
  other arithmetic  12.4 us (12%)
  between operations  1.15 us (1%)
    pallas_call x4, Pallas kernels, exchange(): pl.pallas_call(functools.partial(exchange_kernel, axes, sizes, width), ou...  63.5 us
    gather x4, local copies, waits for them, and re-layouts, rim_terms(): picked = field[rows, cols]  16.5 us
    unnamed x56, local copies, waits for them, and re-layouts  3.88 us
    add x4, other arithmetic, rim_terms(): total = total + weights[corner][:, None] * picked[corner]  3.07 us

profile of v6, /device:TPU:2, one launch (start us, length us, event | category | flops | bytes accessed | tf_op | source)
XLA Modules:
  0.0 104.9 jit_solution(6630431840800169792)
XLA Ops:
  0.6 0.8 squeeze.127
  1.5 0.8 squeeze.129
  2.2 0.8 fusion.100
  3.0 0.1 reshape.777
  3.3 0.1 reshape.787
  3.3 0.5 broadcast.664
  3.9 0.7 clamp_reduce_fusion.1
  4.5 0.1 reshape.783
  4.9 0.8 fusion.102
  5.6 0.1 reshape.776
  5.7 0.1 reshape.790
  5.8 0.1 reshape.788
  6.0 0.1 reshape.786
  6.1 0.7 clamp_reduce_fusion.3
  6.8 0.1 reshape.778
  7.0 0.1 reshape.780
  7.1 0.1 reshape.784
  7.5 0.1 reshape.798
  7.6 0.7 fusion.113
  8.3 0.1 squeeze.132
  8.4 0.1 squeeze.135
  8.5 0.1 squeeze.128
  8.6 0.1 squeeze.138
  8.7 0.7 fusion.114
  9.4 0.1 squeeze.133
  9.5 0.1 squeeze.136
  9.6 0.1 squeeze.130
  9.7 0.1 squeeze.139
  9.9 1.0 pad_maximum_fusion.2.field
  10.9 5.5 %gather_fusion = f32[768,256]{1,0:T(8,128)S(1)} fusion(f32[16,32,256]{2,1,0:T(8,128)S(1)} %pad_maximum_fusion.2.field, s32[768]{0:T(1024)S(1)} %reshape.792), kind=kCustom, calls=%fused_computation | custom fusion | bytes 1579008 | tf_op jit(solution)/shard_map/gather | solution.py:53
  16.5 0.8 fusion.63.rim
  17.3 26.4 %shard_map.95 = (f32[2,32,256]{2,1,0:T(8,128)}, f32[2,32,256]{2,1,0:T(8,128)}, f32[2,16,256]{2,1,0:T(8,128)}, f32[2,16,256]{2,1,0:T(8,128)}) custom-call(f32[16,32,256]{2,1,0:T(8,128)} %copy-done, f32[192,256]{1,0:T(8,128)} %fusion.63.rim), custom_call_target="tpu_custom_call" | custom-call | bytes 393216 | tf_op jit(solution)/shard_map/pallas_call | solution.py:248
  43.8 0.9 pad.58
  44.7 0.9 pad.59
  45.6 0.7 copy-done.18
  46.5 0.1 slice_multiply_fusion.13
  46.7 0.1 slice_multiply_fusion.12
  46.8 0.1 maximum_maximum_fusion
  47.0 0.1 maximum_maximum_fusion.1
  47.1 0.7 copy-done.12
  47.8 0.2 copy-done.14
  48.1 0.2 copy-done.10
  48.3 0.1 copy-done.15
  48.4 0.4 fusion.54.field
  48.8 3.7 %gather_fusion.1 = f32[384,128]{1,0:T(8,128)S(1)} fusion(f32[16,32,128]{2,1,0:T(8,128)S(1)} %fusion.54.field, s32[384]{0:T(512)S(1)} %reshape.798), kind=kCustom, calls=%fused_computation.1 | custom fusion | bytes 396288 | tf_op jit(solution)/shard_map/gather | solution.py:53
  52.4 0.7 fusion.72.rim
  53.2 13.1 %shard_map.96 = (f32[1,32,128]{2,1,0:T(8,128)}, f32[1,32,128]{2,1,0:T(8,128)}, f32[1,16,128]{2,1,0:T(8,128)}, f32[1,16,128]{2,1,0:T(8,128)}) custom-call(f32[16,32,128]{2,1,0:T(8,128)} %copy-done.5, f32[96,128]{1,0:T(8,128)} %fusion.72.rim), custom_call_target="tpu_custom_call" | custom-call | bytes 98304 | tf_op jit(solution)/shard_map/pallas_call | solution.py:248
  66.4 0.1 slice_multiply_fusion.11
  66.5 0.5 copy-done.22
  67.1 0.3 fusion.46.field
  67.4 3.7 %gather_fusion.2 = f32[384,128]{1,0:T(8,128)S(1)} fusion(f32[16,32,128]{2,1,0:T(8,128)S(1)} %fusion.46.field, s32[384]{0:T(512)S(1)} %reshape.798), kind=kCustom, calls=%fused_computation.2 | custom fusion | bytes 396288 | tf_op jit(solution)/shard_map/gather | solution.py:53
  71.1 0.7 fusion.69.rim
  71.9 12.0 %shard_map.97 = (f32[1,32,128]{2,1,0:T(8,128)}, f32[1,32,128]{2,1,0:T(8,128)}, f32[1,16,128]{2,1,0:T(8,128)}, f32[1,16,128]{2,1,0:T(8,128)}) custom-call(f32[16,32,128]{2,1,0:T(8,128)} %copy-done.3, f32[96,128]{1,0:T(8,128)} %fusion.69.rim), custom_call_target="tpu_custom_call" | custom-call | bytes 98304 | tf_op jit(solution)/shard_map/pallas_call | solution.py:248
  83.9 0.1 slice_multiply_fusion.9
  84.0 0.5 copy-done.20
  84.6 0.3 fusion.28.field
  84.9 3.7 %gather_fusion.3 = f32[384,128]{1,0:T(8,128)S(1)} fusion(f32[16,32,128]{2,1,0:T(8,128)S(1)} %fusion.28.field, s32[384]{0:T(512)S(1)} %reshape.798), kind=kCustom, calls=%fused_computation.3 | custom fusion | bytes 396288 | tf_op jit(solution)/shard_map/gather | solution.py:53
  88.6 0.7 fusion.66.rim
  89.4 12.0 %shard_map.98 = (f32[1,32,128]{2,1,0:T(8,128)}, f32[1,32,128]{2,1,0:T(8,128)}, f32[1,16,128]{2,1,0:T(8,128)}, f32[1,16,128]{2,1,0:T(8,128)}) custom-call(f32[16,32,128]{2,1,0:T(8,128)} %copy-done.1, f32[96,128]{1,0:T(8,128)} %fusion.66.rim), custom_call_target="tpu_custom_call" | custom-call | bytes 98304 | tf_op jit(solution)/shard_map/pallas_call | solution.py:248
  101.4 0.7 copy-done.16
  102.0 1.4 %fusion.8 = f32[17,32,128]{2,1,0:T(8,128)S(1)} fusion(f32[18,36,256]{2,1,0:T(8,128)} %copy-done.14, f32[18,36,256]{2,1,0:T(8,128)S(1)} %copy-done.13, f32[16,1,128]{2,1,0:T(1,128)} %bitcast.143, f32[16,32,128]{2,1,0:T(8,128)S(1)} %copy-done.2, f32[16,1,128]{2,1,0:T(1,128)S(1)} %bitcast.141, f32[1,32,128]{2,1,0:T(8,128)} %get-tuple-element.33, ...), kind=kLoop, calls=%fused_computation.30 | loop fusion | flops 1671168 | bytes 2260992 | tf_op jit(solution)/shard_map/mul | solution.py:321
  103.5 0.3 fusion.2
  103.7 0.3 fusion.15
  104.0 0.9 fusion.23
  (80 shorter events, 1.6 us)
Async XLA Ops:
  0.6 9.3 %copy-start.7 = (f32[1,16,32,128]{3,2,1,0:T(8,128)S(1)}, f32[1,16,32,128]{3,2,1,0:T(8,128)}, u32[]{:S(2)}) copy-start(f32[1,16,32,128]{3,2,1,0:T(8,128)} %param.9) | copy-start | bytes 786436
  10.9 5.5 %copy-start = (f32[16,32,256]{2,1,0:T(8,128)}, f32[16,32,256]{2,1,0:T(8,128)S(1)}, u32[]{:S(2)}) copy-start(f32[16,32,256]{2,1,0:T(8,128)S(1)} %pad_maximum_fusion.2.field) | copy-start | bytes 1572868
  43.8 2.6 %copy-start.8 = (f32[1,16,32,128]{3,2,1,0:T(8,128)S(1)}, f32[1,16,32,128]{3,2,1,0:T(8,128)}, u32[]{:S(2)}) copy-start(f32[1,16,32,128]{3,2,1,0:T(8,128)} %param.8) | copy-start | bytes 786436
  44.7 0.9 copy-start.19
  45.5 0.8 copy-start.18
  46.9 0.9 copy-start.12
  46.9 1.1 %copy-start.14 = (f32[18,36,256]{2,1,0:T(8,128)}, f32[18,36,256]{2,1,0:T(8,128)S(1)}, u32[]{:S(2)}) copy-start(f32[18,36,256]{2,1,0:T(8,128)S(1)} %get-tuple-element.65) | copy-start | bytes 1990660
  47.0 1.3 %copy-start.9 = (f32[1,16,32,128]{3,2,1,0:T(8,128)S(1)}, f32[1,16,32,128]{3,2,1,0:T(8,128)}, u32[]{:S(2)}) copy-start(f32[1,16,32,128]{3,2,1,0:T(8,128)} %param.11) | copy-start | bytes 786436
  47.0 1.4 %copy-start.15 = (f32[1,16,32,128]{3,2,1,0:T(8,128)S(1)}, f32[1,16,32,128]{3,2,1,0:T(8,128)}, u32[]{:S(2)}) copy-start(f32[1,16,32,128]{3,2,1,0:T(8,128)} %param.10) | copy-start | bytes 786436
  47.1 1.2 %copy-start.10 = (f32[16,34,256]{2,1,0:T(8,128)}, f32[16,34,256]{2,1,0:T(8,128)S(1)}, u32[]{:S(2)}) copy-start(f32[16,34,256]{2,1,0:T(8,128)S(1)} %get-tuple-element.71) | copy-start | bytes 1671172
  48.7 3.7 %copy-start.5 = (f32[16,32,128]{2,1,0:T(8,128)}, f32[16,32,128]{2,1,0:T(8,128)S(1)}, u32[]{:S(2)}) copy-start(f32[16,32,128]{2,1,0:T(8,128)S(1)} %fusion.54.field) | copy-start | bytes 786436
  53.2 13.1 %copy-start.6 = (f32[16,32,128]{2,1,0:T(8,128)S(1)}, f32[16,32,128]{2,1,0:T(8,128)}, u32[]{:S(2)}) copy-start(f32[16,32,128]{2,1,0:T(8,128)} %copy-done.5) | copy-start | bytes 786436
  66.3 0.7 copy-start.22
  66.3 0.7 copy-start.23
  66.4 0.7 copy-start.26
  66.4 0.7 copy-start.27
  67.4 3.7 %copy-start.3 = (f32[16,32,128]{2,1,0:T(8,128)}, f32[16,32,128]{2,1,0:T(8,128)S(1)}, u32[]{:S(2)}) copy-start(f32[16,32,128]{2,1,0:T(8,128)S(1)} %fusion.46.field) | copy-start | bytes 786436
  71.8 12.0 %copy-start.4 = (f32[16,32,128]{2,1,0:T(8,128)S(1)}, f32[16,32,128]{2,1,0:T(8,128)}, u32[]{:S(2)}) copy-start(f32[16,32,128]{2,1,0:T(8,128)} %copy-done.3) | copy-start | bytes 786436
  83.8 0.7 copy-start.20
  83.8 0.7 copy-start.21
  83.8 0.7 copy-start.24
  83.9 0.7 copy-start.25
  84.9 3.7 %copy-start.1 = (f32[16,32,128]{2,1,0:T(8,128)}, f32[16,32,128]{2,1,0:T(8,128)S(1)}, u32[]{:S(2)}) copy-start(f32[16,32,128]{2,1,0:T(8,128)S(1)} %fusion.28.field) | copy-start | bytes 786436
  84.9 16.4 %copy-start.13 = (f32[18,36,256]{2,1,0:T(8,128)S(1)}, f32[18,36,256]{2,1,0:T(8,128)}, u32[]{:S(2)}) copy-start(f32[18,36,256]{2,1,0:T(8,128)} %copy-done.12) | copy-start | bytes 1990660
  89.4 12.0 %copy-start.2 = (f32[16,32,128]{2,1,0:T(8,128)S(1)}, f32[16,32,128]{2,1,0:T(8,128)}, u32[]{:S(2)}) copy-start(f32[16,32,128]{2,1,0:T(8,128)} %copy-done.1) | copy-start | bytes 786436
  101.3 0.7 copy-start.16
  102.0 1.4 %copy-start.11 = (f32[16,34,256]{2,1,0:T(8,128)S(1)}, f32[16,34,256]{2,1,0:T(8,128)}, u32[]{:S(2)}) copy-start(f32[16,34,256]{2,1,0:T(8,128)} %copy-done.10) | copy-start | bytes 1671172
  102.0 1.4 %copy-start.17 = (f32[1,16,128]{2,1,0:T(8,128)S(1)}, f32[1,16,128]{2,1,0:T(8,128)}, u32[]{:S(2)}) copy-start(f32[1,16,128]{2,1,0:T(8,128)} %get-tuple-element.31) | copy-start | bytes 24580

commit v7 on v6

--- a/solution.py
+++ b/solution.py
@@ -32,7 +32,7 @@
         target = rows_at + row_step
         inside = (target >= 0) & (target < rows_dev)
         rows.append([jnp.clip(target, 0, rows_dev - 1).reshape(-1)])
-        cols.append([(cols_at + col_step).reshape(-1)])
+        cols.append([jnp.clip(cols_at + col_step, 0, cols_dev - 1).reshape(-1)])
         weights.append([jnp.where(inside, lat_weights[corner, :, :width], 0.0).reshape(-1)])
     chosen = lon_codes[:, :width]
     cols_at = chosen // rows_dev - first_col
@@ -40,21 +40,11 @@
     for corner, (row_step, col_step) in enumerate(stencil_offsets):
         target = cols_at + col_step
         inside = (target >= 0) & (target < cols_dev)
-        rows[corner].append((rows_at + row_step).reshape(-1))
+        rows[corner].append(jnp.clip(rows_at + row_step, 0, rows_dev - 1).reshape(-1))
         cols[corner].append(jnp.clip(target, 0, cols_dev - 1).reshape(-1))
         weights[corner].append(jnp.where(inside, lon_weights[corner, :, :width], 0.0).reshape(-1))
     join = lambda parts: jnp.stack([jnp.concatenate(p) for p in parts])
     return join(rows), join(cols), join(weights)
-
-
-def rim_terms(field, plan, width):
-    rows_dev, cols_dev, levels = field.shape
-    rows, cols, weights = plan
-    picked = field[rows, cols]
-    total = jnp.zeros(picked.shape[1:], jnp.float32)
-    for corner in range(len(stencil_offsets)):
-        total = total + weights[corner][:, None] * picked[corner]
-    return total
 
 
 def exchange_kernel(
@@ -62,11 +52,14 @@
     sizes,
     width,
     field,
-    rim,
+    rows_at,
+    cols_at,
+    weights_at,
     north,
     south,
     west,
     east,
+    rim,
     lat_buf,
     lon_buf,
     north_buf,
@@ -146,6 +139,16 @@
         def _():
             greet(target)
 
+    def gather_row(index, carry):
+        total = jnp.zeros((1, field.shape[2]), jnp.float32)
+        for corner in range(len(stencil_offsets)):
+            picked = field[rows_at[corner, index], pl.ds(cols_at[corner, index], 1), :]
+            total = total + weights_at[corner, index] * picked
+        rim[pl.ds(index, 1), :] = total
+        return carry
+
+    lax.fori_loop(0, rim.shape[0], gather_row, 0)
+
     def above_zero(index, count):
         return (index + count - 1) // count
 
@@ -238,13 +241,14 @@
             east[depth] = east_buf[:, depth, :]
 
 
-def exchange(field, rim, axes, width):
+def exchange(field, plan, axes, width):
     sizes = {name: lax.axis_size(name) for name in ("lat", "lon")}
     rows, cols, levels = field.shape
     lat_shape = (width, cols, levels)
     lon_shape = (width, rows, levels)
     vmem = pl.BlockSpec(memory_space=pltpu.VMEM)
-    moved = 4 * (rim.size + 2 * width * (rows + cols) * levels)
+    count = plan[0].shape[1]
+    moved = 4 * (count * levels + 2 * width * (rows + cols) * levels)
     return pl.pallas_call(
         functools.partial(exchange_kernel, axes, sizes, width),
         out_shape=(
@@ -253,9 +257,10 @@
             jax.ShapeDtypeStruct(lon_shape, jnp.float32),
             jax.ShapeDtypeStruct(lon_shape, jnp.float32),
         ),
-        in_specs=[vmem, vmem],
+        in_specs=[vmem] + [pl.BlockSpec(memory_space=pltpu.SMEM)] * 3,
         out_specs=(vmem, vmem, vmem, vmem),
         scratch_shapes=[
+            pltpu.VMEM((count, levels), jnp.float32),
             pltpu.VMEM((sizes["lat"], width * cols, levels), jnp.float32),
             pltpu.VMEM((sizes["lon"], width * rows, levels), jnp.float32),
             pltpu.VMEM(lat_shape, jnp.float32),
@@ -267,12 +272,11 @@
         ],
         compiler_params=pltpu.CompilerParams(collective_id=width - 1, has_side_effects=True),
         cost_estimate=pl.CostEstimate(flops=0, transcendentals=0, bytes_accessed=moved),
-    )(field, rim)
+    )(field, *plan)
 
 
 def surround(field, width, plan, axes):
-    rim = rim_terms(field, plan, width)
-    north, south, west, east = exchange(field, rim, axes, width)
+    north, south, west, east = exchange(field, plan, axes, width)
     middle = jnp.concatenate(
         [jnp.moveaxis(west, 0, 1), field, jnp.moveaxis(east, 0, 1)], axis=1
     )

time: 106 us -> 91.7 us (0.87)
  local copies, waits for them, and re-layouts: 27.9 us -> 11.1 us
  other arithmetic: 12.4 us -> 14.7 us
    gather x4 -> x0, local copies, waits for them, and re-layouts: 16.5 us -> none  [rim_terms(): picked = field[rows, cols]]
    another operation x4 -> x12, other arithmetic: 0.31 us -> 4.05 us  [rim_plan(): join = lambda parts: jnp.stack([jnp.concatenate(p) for p in parts])]
    add x6 -> x0, other arithmetic: 3.09 us -> none  [the longest x4 3.07 us: rim_terms(): total = total + weights[corner][:, None] * picked[corner]]
    div x3, other arithmetic: 1.01 us -> 3.2 us  [body(): neighbour_total(padded, source_now, lat_face, lon_face, mean_rad)]
    unnamed x56 -> x46, local copies, waits for them, and re-layouts: 3.88 us -> 4.28 us
where the time goes in v7:
time: 91.7 us; the launch traced here: 91 us
  Pallas kernels  64.2 us (70%)
  other arithmetic  14.7 us (16%)
  local copies, waits for them, and re-layouts  11.1 us (12%)
  between operations  1.04 us (1%)
    pallas_call x4, Pallas kernels, exchange(): pl.pallas_call(functools.partial(exchange_kernel, axes, sizes, width), ou...  64.2 us
    unnamed x46, local copies, waits for them, and re-layouts  4.28 us
    another operation x12, other arithmetic, rim_plan(): join = lambda parts: jnp.stack([jnp.concatenate(p) for p in parts])  4.05 us
    div x3, other arithmetic, body(): neighbour_total(padded, source_now, lat_face, lon_face, mean_rad)  3.2 us

profile of v7, /device:TPU:2, one launch (start us, length us, event | category | flops | bytes accessed | tf_op | source)
XLA Modules:
  0.0 91.0 jit_solution(15561082602045115506)
XLA Ops:
  0.6 0.8 squeeze.79
  1.5 0.8 squeeze.80
  2.2 0.8 fusion.76
  3.0 0.1 reshape.133
  3.1 0.1 reshape.139
  3.2 0.1 reshape.137
  3.2 0.1 reshape.135
  3.4 0.1 reshape.129
  3.4 0.1 reshape.131
  3.5 0.1 reshape.127
  3.6 0.1 reshape.125
  3.7 0.8 fusion.78
  4.5 0.1 reshape.132
  4.5 0.1 reshape.138
  4.6 0.1 reshape.136
  4.7 0.1 maximum_bitcast_fusion.2
  4.8 0.1 reshape.134
  4.9 0.6 pad_maximum_fusion.25.weights_at
  5.6 0.1 reshape.128
  5.7 0.1 reshape.130
  5.9 0.1 reshape.126
  6.0 0.1 reshape.124
  6.2 0.6 pad_add_fusion.2.rows_at
  6.8 0.6 pad_add_fusion.3.cols_at
  7.4 0.7 fusion.87
  8.1 0.1 squeeze.83
  8.2 0.1 squeeze.85
  8.3 0.1 squeeze.81
  8.4 0.1 squeeze.87
  8.5 0.7 fusion.88
  9.2 0.1 squeeze.84
  9.3 0.1 squeeze.86
  9.4 0.1 squeeze.82
  9.5 0.1 squeeze.88
  9.6 0.6 pad_maximum_fusion.24.weights_at
  10.3 0.6 pad_add_fusion.rows_at
  10.9 0.6 pad_add_fusion.1.cols_at
  11.5 1.8 %pad_maximum_fusion.2.field = f32[16,32,256]{2,1,0:T(8,128)} fusion(f32[16,32,128]{2,1,0:T(8,128)} %bitcast.141, f32[16,32,128]{2,1,0:T(8,128)S(1)} %bitcast.136), kind=kLoop, calls=%fused_computation.5 | loop fusion | flops 131072 | bytes 1048576 | tf_op jit(solution)/shard_map/concatenate | solution.py:357
  13.3 26.5 %shard_map.95 = (f32[2,32,256]{2,1,0:T(8,128)}, f32[2,32,256]{2,1,0:T(8,128)}, f32[2,16,256]{2,1,0:T(8,128)}, f32[2,16,256]{2,1,0:T(8,128)}) custom-call(f32[16,32,256]{2,1,0:T(8,128)} %pad_maximum_fusion.2.field, s32[4,192]{1,0:T(4,128)} %pad_add_fusion.rows_at, s32[4,192]{1,0:T(4,128)} %pad_add_fusion.1.cols_at, f32[4,192]{1,0:T(4,128)} %pad_maximum_fusion.24.weights_at), custom_call_target="tpu_custom_call" | custom-call | bytes 393216 | tf_op jit(solution)/shard_map/pallas_call | solution.py:252
  39.8 0.9 pad.58
  40.7 0.9 pad.59
  41.6 0.7 copy-done.13
  42.5 0.1 slice_multiply_fusion.13
  42.7 0.1 slice_multiply_fusion.12
  42.8 0.1 maximum_maximum_fusion
  43.0 0.1 maximum_maximum_fusion.1
  43.1 0.7 copy-done.6
  43.8 0.3 copy-done.7
  44.1 0.3 copy-done.8
  44.4 1.1 %fusion.54.field = f32[16,32,128]{2,1,0:T(8,128)} fusion(f32[16,34,256]{2,1,0:T(8,128)S(1)} %get-tuple-element.69, f32[16,34,256]{2,1,0:T(8,128)S(1)} %get-tuple-element.68, f32[18,36,256]{2,1,0:T(8,128)S(1)} %get-tuple-element.63, f32[18,36,256]{2,1,0:T(8,128)S(1)} %get-tuple-element.62, f32[1,16,32,128]{3,2,1,0:T(8,128)S(1)} %copy-done.8, ...), kind=kLoop, calls=%fused_computation.114 | loop fusion | flops 1114112 | bytes 3663872 | tf_op jit(solution)/shard_map/div | solution.py:369
  45.5 13.6 %shard_map.96 = (f32[1,32,128]{2,1,0:T(8,128)}, f32[1,32,128]{2,1,0:T(8,128)}, f32[1,16,128]{2,1,0:T(8,128)}, f32[1,16,128]{2,1,0:T(8,128)}) custom-call(f32[16,32,128]{2,1,0:T(8,128)} %fusion.54.field, s32[4,96]{1,0:T(4,128)} %pad_add_fusion.2.rows_at, s32[4,96]{1,0:T(4,128)} %pad_add_fusion.3.cols_at, f32[4,96]{1,0:T(4,128)} %pad_maximum_fusion.25.weights_at), custom_call_target="tpu_custom_call" | custom-call | bytes 98304 | tf_op jit(solution)/shard_map/pallas_call | solution.py:252
  59.1 0.1 slice_multiply_fusion.11
  59.3 0.8 copy-done.9
  60.1 1.1 %fusion.46.field = f32[16,32,128]{2,1,0:T(8,128)} fusion(f32[16,1,128]{2,1,0:T(1,128)S(1)} %bitcast.162, f32[16,32,128]{2,1,0:T(8,128)S(1)} %copy-done.3, f32[16,1,128]{2,1,0:T(1,128)S(1)} %bitcast.161, f32[1,32,128]{2,1,0:T(8,128)S(1)} %copy-done.18, f32[1,32,128]{2,1,0:T(8,128)S(1)} %copy-done.17, f32[1,16,32,128]{3,2,1,0:T(8,128)S(1)} %copy-done.9, ...), kind=kLoop, calls=%fused_computation.91 | loop fusion | flops 2031616 | bytes 2926592 | tf_op jit(solution)/shard_map/div | solution.py:369
  61.1 12.1 %shard_map.97 = (f32[1,32,128]{2,1,0:T(8,128)}, f32[1,32,128]{2,1,0:T(8,128)}, f32[1,16,128]{2,1,0:T(8,128)}, f32[1,16,128]{2,1,0:T(8,128)}) custom-call(f32[16,32,128]{2,1,0:T(8,128)} %fusion.46.field, s32[4,96]{1,0:T(4,128)} %pad_add_fusion.2.rows_at, s32[4,96]{1,0:T(4,128)} %pad_add_fusion.3.cols_at, f32[4,96]{1,0:T(4,128)} %pad_maximum_fusion.25.weights_at), custom_call_target="tpu_custom_call" | custom-call | bytes 98304 | tf_op jit(solution)/shard_map/pallas_call | solution.py:252
  73.2 0.1 slice_multiply_fusion.9
  73.4 0.8 copy-done.10
  74.1 1.1 %fusion.28.field = f32[16,32,128]{2,1,0:T(8,128)} fusion(f32[16,1,128]{2,1,0:T(1,128)S(1)} %bitcast.160, f32[16,32,128]{2,1,0:T(8,128)S(1)} %copy-done.4, f32[16,1,128]{2,1,0:T(1,128)S(1)} %bitcast.159, f32[1,32,128]{2,1,0:T(8,128)S(1)} %copy-done.16, f32[1,32,128]{2,1,0:T(8,128)S(1)} %copy-done.15, f32[1,16,32,128]{3,2,1,0:T(8,128)S(1)} %copy-done.10, ...), kind=kLoop, calls=%fused_computation.66 | loop fusion | flops 2031616 | bytes 2926592 | tf_op jit(solution)/shard_map/div | solution.py:369
  75.2 12.1 %shard_map.98 = (f32[1,32,128]{2,1,0:T(8,128)}, f32[1,32,128]{2,1,0:T(8,128)}, f32[1,16,128]{2,1,0:T(8,128)}, f32[1,16,128]{2,1,0:T(8,128)}) custom-call(f32[16,32,128]{2,1,0:T(8,128)} %fusion.28.field, s32[4,96]{1,0:T(4,128)} %pad_add_fusion.2.rows_at, s32[4,96]{1,0:T(4,128)} %pad_add_fusion.3.cols_at, f32[4,96]{1,0:T(4,128)} %pad_maximum_fusion.25.weights_at), custom_call_target="tpu_custom_call" | custom-call | bytes 98304 | tf_op jit(solution)/shard_map/pallas_call | solution.py:252
  87.3 0.7 copy-done.11
  88.0 1.6 %fusion.8 = f32[17,32,128]{2,1,0:T(8,128)S(1)} fusion(f32[18,36,256]{2,1,0:T(8,128)} %copy-done.7, f32[18,36,256]{2,1,0:T(8,128)} %copy-done.6, f32[16,1,128]{2,1,0:T(1,128)} %bitcast.155, f32[16,32,128]{2,1,0:T(8,128)S(1)} %copy-done, f32[16,1,128]{2,1,0:T(1,128)S(1)} %bitcast.153, f32[1,32,128]{2,1,0:T(8,128)} %get-tuple-element.33, ...), kind=kLoop, calls=%fused_computation.26 | loop fusion | flops 1671168 | bytes 2260992 | tf_op jit(solution)/shard_map/mul | solution.py:325
  89.6 0.3 fusion.2
  89.8 0.3 fusion.15
  90.1 0.9 fusion.23
  (64 shorter events, 0.9 us)
Async XLA Ops:
  0.6 10.9 %copy-start.1 = (f32[1,16,32,128]{3,2,1,0:T(8,128)S(1)}, f32[1,16,32,128]{3,2,1,0:T(8,128)}, u32[]{:S(2)}) copy-start(f32[1,16,32,128]{3,2,1,0:T(8,128)} %param.9) | copy-start | bytes 786436
  39.8 2.6 %copy-start.2 = (f32[1,16,32,128]{3,2,1,0:T(8,128)S(1)}, f32[1,16,32,128]{3,2,1,0:T(8,128)}, u32[]{:S(2)}) copy-start(f32[1,16,32,128]{3,2,1,0:T(8,128)} %param.8) | copy-start | bytes 786436
  40.7 0.9 copy-start.14
  41.6 0.8 copy-start.13
  43.0 0.9 copy-start.6
  43.0 1.1 %copy-start.7 = (f32[18,36,256]{2,1,0:T(8,128)}, f32[18,36,256]{2,1,0:T(8,128)S(1)}, u32[]{:S(2)}) copy-start(f32[18,36,256]{2,1,0:T(8,128)S(1)} %get-tuple-element.63) | copy-start | bytes 1990660
  43.0 1.2 %copy-start.5 = (f32[1,16,32,128]{3,2,1,0:T(8,128)S(1)}, f32[1,16,32,128]{3,2,1,0:T(8,128)}, u32[]{:S(2)}) copy-start(f32[1,16,32,128]{3,2,1,0:T(8,128)} %param.11) | copy-start | bytes 786436
  43.0 1.4 %copy-start.8 = (f32[1,16,32,128]{3,2,1,0:T(8,128)S(1)}, f32[1,16,32,128]{3,2,1,0:T(8,128)}, u32[]{:S(2)}) copy-start(f32[1,16,32,128]{3,2,1,0:T(8,128)} %param.10) | copy-start | bytes 786436
  45.5 13.6 %copy-start.3 = (f32[16,32,128]{2,1,0:T(8,128)S(1)}, f32[16,32,128]{2,1,0:T(8,128)}, u32[]{:S(2)}) copy-start(f32[16,32,128]{2,1,0:T(8,128)} %fusion.54.field) | copy-start | bytes 786436
  59.1 1.0 %copy-start.9 = (f32[1,16,32,128]{3,2,1,0:T(8,128)S(1)}, f32[1,16,32,128]{3,2,1,0:T(8,128)}, u32[]{:S(2)}) copy-start(f32[1,16,32,128]{3,2,1,0:T(8,128)} %param.10) | copy-start | bytes 786436
  59.1 0.9 %copy-start.17 = (f32[1,32,128]{2,1,0:T(8,128)S(1)}, f32[1,32,128]{2,1,0:T(8,128)}, u32[]{:S(2)}) copy-start(f32[1,32,128]{2,1,0:T(8,128)} %get-tuple-element.22) | copy-start | bytes 49156
  59.1 0.9 %copy-start.18 = (f32[1,32,128]{2,1,0:T(8,128)S(1)}, f32[1,32,128]{2,1,0:T(8,128)}, u32[]{:S(2)}) copy-start(f32[1,32,128]{2,1,0:T(8,128)} %get-tuple-element.25) | copy-start | bytes 49156
  59.1 0.9 %copy-start.21 = (f32[1,16,128]{2,1,0:T(8,128)S(1)}, f32[1,16,128]{2,1,0:T(8,128)}, u32[]{:S(2)}) copy-start(f32[1,16,128]{2,1,0:T(8,128)} %get-tuple-element.23) | copy-start | bytes 24580
  59.1 0.9 %copy-start.22 = (f32[1,16,128]{2,1,0:T(8,128)S(1)}, f32[1,16,128]{2,1,0:T(8,128)}, u32[]{:S(2)}) copy-start(f32[1,16,128]{2,1,0:T(8,128)} %get-tuple-element.24) | copy-start | bytes 24580
  61.1 12.1 %copy-start.4 = (f32[16,32,128]{2,1,0:T(8,128)S(1)}, f32[16,32,128]{2,1,0:T(8,128)}, u32[]{:S(2)}) copy-start(f32[16,32,128]{2,1,0:T(8,128)} %fusion.46.field) | copy-start | bytes 786436
  73.2 1.0 %copy-start.10 = (f32[1,16,32,128]{3,2,1,0:T(8,128)S(1)}, f32[1,16,32,128]{3,2,1,0:T(8,128)}, u32[]{:S(2)}) copy-start(f32[1,16,32,128]{3,2,1,0:T(8,128)} %param.10) | copy-start | bytes 786436
  73.2 0.9 %copy-start.15 = (f32[1,32,128]{2,1,0:T(8,128)S(1)}, f32[1,32,128]{2,1,0:T(8,128)}, u32[]{:S(2)}) copy-start(f32[1,32,128]{2,1,0:T(8,128)} %get-tuple-element.26) | copy-start | bytes 49156
  73.2 0.9 %copy-start.16 = (f32[1,32,128]{2,1,0:T(8,128)S(1)}, f32[1,32,128]{2,1,0:T(8,128)}, u32[]{:S(2)}) copy-start(f32[1,32,128]{2,1,0:T(8,128)} %get-tuple-element.29) | copy-start | bytes 49156
  73.2 0.9 %copy-start.19 = (f32[1,16,128]{2,1,0:T(8,128)S(1)}, f32[1,16,128]{2,1,0:T(8,128)}, u32[]{:S(2)}) copy-start(f32[1,16,128]{2,1,0:T(8,128)} %get-tuple-element.27) | copy-start | bytes 24580
  73.2 0.9 %copy-start.20 = (f32[1,16,128]{2,1,0:T(8,128)S(1)}, f32[1,16,128]{2,1,0:T(8,128)}, u32[]{:S(2)}) copy-start(f32[1,16,128]{2,1,0:T(8,128)} %get-tuple-element.28) | copy-start | bytes 24580
  75.2 12.1 %copy-start = (f32[16,32,128]{2,1,0:T(8,128)S(1)}, f32[16,32,128]{2,1,0:T(8,128)}, u32[]{:S(2)}) copy-start(f32[16,32,128]{2,1,0:T(8,128)} %fusion.28.field) | copy-start | bytes 786436
  87.3 0.7 copy-start.11
  88.0 1.6 %copy-start.12 = (f32[1,16,128]{2,1,0:T(8,128)S(1)}, f32[1,16,128]{2,1,0:T(8,128)}, u32[]{:S(2)}) copy-start(f32[1,16,128]{2,1,0:T(8,128)} %get-tuple-element.31) | copy-start | bytes 24580

commit v8 on v7

--- a/solution.py
+++ b/solution.py
@@ -349,11 +349,19 @@
     lon_weight_now = lon_weights[0]
     rows_dev, cols_dev, levels = porosity_now.shape
     plans = {
-        width: rim_plan(
-            lat_code_now, lat_weight_now, lon_code_now, lon_weight_now, width, rows_dev, cols_dev
-        )
-        for width in (1, 2)
+        2: rim_plan(lat_code_now, lat_weight_now, lon_code_now, lon_weight_now, 2, rows_dev, cols_dev)
     }
+    lat_span, lon_span = 4 * cols_dev, 2 * rows_dev
+    starts = (
+        (0, cols_dev),
+        (2 * cols_dev, cols_dev),
+        (lat_span, rows_dev),
+        (lat_span + lon_span, rows_dev),
+    )
+    plans[1] = tuple(
+        jnp.concatenate([part[:, at : at + size] for at, size in starts], axis=1)
+        for part in plans[2]
+    )
     both_pad = surround(jnp.concatenate([porosity_now, current], axis=-1), 2, plans[2], axes)
     porosity_pad = both_pad[..., :levels]
     first_pad = both_pad[1:-1, 1:-1, levels:]

time: 91.7 us -> 87.8 us (0.957)
  other arithmetic: 14.7 us -> 11.1 us
    another operation x12 -> x3, other arithmetic: 4.05 us -> 0.04 us  [rim_plan(): join = lambda parts: jnp.stack([jnp.concatenate(p) for p in parts])]
    concatenate x0 -> x3, other arithmetic: none -> 2.01 us  [body(): jnp.concatenate([part[:, at:at + size] for at, size in starts], axis=1)]
    reshape x16 -> x0, local copies, waits for them, and re-layouts: 1.3 us -> none  [the longest x4 0.32 us: rim_plan(): jnp.where(inside, lat_weights[corner, :, :width], 0.0).reshape(-1)]
    unnamed x46 -> x52, local copies, waits for them, and re-layouts: 4.28 us -> 4.81 us
where the time goes in v8:
time: 87.8 us; the launch traced here: 87.2 us
  Pallas kernels  64.2 us (73%)
  other arithmetic  11.1 us (13%)
  local copies, waits for them, and re-layouts  10.7 us (12%)
  between operations  1.08 us (1%)
    pallas_call x4, Pallas kernels, exchange(): pl.pallas_call(functools.partial(exchange_kernel, axes, sizes, width), ou...  64.2 us
    unnamed x52, local copies, waits for them, and re-layouts  4.81 us
    div x3, other arithmetic, body(): neighbour_total(padded, source_now, lat_face, lon_face, mean_rad)  3.2 us
    concatenate x3, other arithmetic, body(): jnp.concatenate([part[:, at:at + size] for at, size in starts], axis=1)  2.01 us
    concatenate x1, other arithmetic, body(): jnp.concatenate([porosity_now, current], axis=-1)  1.79 us

profile of v8, /device:TPU:2, one launch (start us, length us, event | category | flops | bytes accessed | tf_op | source)
XLA Modules:
  0.0 87.2 jit_solution(74115130451387201)
XLA Ops:
  0.6 0.8 squeeze.47
  1.5 0.8 squeeze.48
  2.2 0.7 fusion.67
  2.9 0.1 squeeze.51
  3.0 0.1 squeeze.49
  3.1 0.1 squeeze.55
  3.2 0.1 squeeze.53
  3.3 0.7 fusion.68
  4.1 0.1 squeeze.52
  4.1 0.1 squeeze.50
  4.3 0.1 squeeze.56
  4.3 0.1 squeeze.54
  4.6 0.0 copy-start.12
  4.6 0.0 copy-start.13
  4.6 0.1 fusion.72
  4.7 0.5 copy-done.13
  5.2 0.1 fusion.71
  5.3 0.7 pad_add_fusion.3.cols_at
  5.9 0.1 fusion.74
  6.0 0.1 fusion.73
  6.1 0.7 pad_add_fusion.2.rows_at
  6.8 0.1 fusion.70
  6.8 0.1 fusion.69
  6.9 0.7 pad_maximum_fusion.25.weights_at
  7.6 1.8 %pad_maximum_fusion.2.field = f32[16,32,256]{2,1,0:T(8,128)} fusion(f32[16,32,128]{2,1,0:T(8,128)} %bitcast.57, f32[16,32,128]{2,1,0:T(8,128)S(1)} %bitcast.52), kind=kLoop, calls=%fused_computation.5 | loop fusion | flops 131072 | bytes 1048576 | tf_op jit(solution)/shard_map/concatenate | solution.py:365
  9.4 26.5 %shard_map.95 = (f32[2,32,256]{2,1,0:T(8,128)}, f32[2,32,256]{2,1,0:T(8,128)}, f32[2,16,256]{2,1,0:T(8,128)}, f32[2,16,256]{2,1,0:T(8,128)}) custom-call(f32[16,32,256]{2,1,0:T(8,128)} %pad_maximum_fusion.2.field, s32[4,192]{1,0:T(4,128)} %copy-done.12, s32[4,192]{1,0:T(4,128)} %copy-done.13, f32[4,192]{1,0:T(4,128)} %copy-done.11), custom_call_target="tpu_custom_call" | custom-call | bytes 393216 | tf_op jit(solution)/shard_map/pallas_call | solution.py:252
  35.9 0.0 copy-start.2
  35.9 0.9 %pad.58 = f32[2,36,256]{2,1,0:T(8,128)S(1)} pad(f32[2,32,256]{2,1,0:T(8,128)} %get-tuple-element.18, f32[]{:T(128)} %constant.85.clone.1), padding=0_0x2_2x0_0 | pad | bytes 139268 | tf_op jit(solution)/shard_map/jit(_pad)/pad | solution.py:285
  36.8 0.9 pad.59
  37.7 0.7 copy-done.16
  38.5 0.1 multiply_multiply_fusion
  38.7 0.1 slice_multiply_fusion.13
  38.8 0.1 slice_multiply_fusion.12
  38.9 0.1 maximum_maximum_fusion
  39.1 0.0 copy-start.6
  39.1 0.0 copy-start.7
  39.1 0.0 copy-start.5
  39.1 0.0 copy-start.8
  39.1 0.1 maximum_maximum_fusion.1
  39.2 0.7 copy-done.6
  39.9 0.2 copy-done.7
  40.2 0.1 copy-done.5
  40.3 0.3 copy-done.8
  40.5 1.1 %fusion.54.field = f32[16,32,128]{2,1,0:T(8,128)} fusion(f32[16,34,256]{2,1,0:T(8,128)S(1)} %get-tuple-element.49, f32[16,34,256]{2,1,0:T(8,128)S(1)} %get-tuple-element.48, f32[18,36,256]{2,1,0:T(8,128)S(1)} %get-tuple-element.43, f32[18,36,256]{2,1,0:T(8,128)S(1)} %get-tuple-element.42, f32[1,16,32,128]{3,2,1,0:T(8,128)S(1)} %copy-done.8, ...), kind=kLoop, calls=%fused_computation.114 | loop fusion | flops 1114112 | bytes 3663872 | tf_op jit(solution)/shard_map/div | solution.py:377
  41.6 13.6 %shard_map.96 = (f32[1,32,128]{2,1,0:T(8,128)}, f32[1,32,128]{2,1,0:T(8,128)}, f32[1,16,128]{2,1,0:T(8,128)}, f32[1,16,128]{2,1,0:T(8,128)}) custom-call(f32[16,32,128]{2,1,0:T(8,128)} %fusion.54.field, s32[4,96]{1,0:T(4,128)} %pad_add_fusion.2.rows_at, s32[4,96]{1,0:T(4,128)} %pad_add_fusion.3.cols_at, f32[4,96]{1,0:T(4,128)} %pad_maximum_fusion.25.weights_at), custom_call_target="tpu_custom_call" | custom-call | bytes 98304 | tf_op jit(solution)/shard_map/pallas_call | solution.py:252
  55.2 0.0 copy-start.9
  55.2 0.0 copy-start.20
  55.2 0.0 copy-start.21
  55.2 0.0 copy-start.24
  55.2 0.0 copy-start.25
  55.3 0.1 slice_multiply_fusion.11
  55.4 0.8 copy-done.9
  56.2 1.1 %fusion.46.field = f32[16,32,128]{2,1,0:T(8,128)} fusion(f32[16,1,128]{2,1,0:T(1,128)S(1)} %bitcast.76, f32[16,32,128]{2,1,0:T(8,128)S(1)} %copy-done.3, f32[16,1,128]{2,1,0:T(1,128)S(1)} %bitcast.75, f32[1,32,128]{2,1,0:T(8,128)S(1)} %copy-done.21, f32[1,32,128]{2,1,0:T(8,128)S(1)} %copy-done.20, f32[1,16,32,128]{3,2,1,0:T(8,128)S(1)} %copy-done.9, ...), kind=kLoop, calls=%fused_computation.91 | loop fusion | flops 2031616 | bytes 2926592 | tf_op jit(solution)/shard_map/div | solution.py:377
  57.2 12.1 %shard_map.97 = (f32[1,32,128]{2,1,0:T(8,128)}, f32[1,32,128]{2,1,0:T(8,128)}, f32[1,16,128]{2,1,0:T(8,128)}, f32[1,16,128]{2,1,0:T(8,128)}) custom-call(f32[16,32,128]{2,1,0:T(8,128)} %fusion.46.field, s32[4,96]{1,0:T(4,128)} %pad_add_fusion.2.rows_at, s32[4,96]{1,0:T(4,128)} %pad_add_fusion.3.cols_at, f32[4,96]{1,0:T(4,128)} %pad_maximum_fusion.25.weights_at), custom_call_target="tpu_custom_call" | custom-call | bytes 98304 | tf_op jit(solution)/shard_map/pallas_call | solution.py:252
  69.3 0.0 copy-start.10
  69.4 0.1 slice_multiply_fusion.9
  69.5 0.8 copy-done.10
  70.3 1.1 %fusion.28.field = f32[16,32,128]{2,1,0:T(8,128)} fusion(f32[16,1,128]{2,1,0:T(1,128)S(1)} %bitcast.74, f32[16,32,128]{2,1,0:T(8,128)S(1)} %copy-done.4, f32[16,1,128]{2,1,0:T(1,128)S(1)} %bitcast.73, f32[1,32,128]{2,1,0:T(8,128)S(1)} %copy-done.19, f32[1,32,128]{2,1,0:T(8,128)S(1)} %copy-done.18, f32[1,16,32,128]{3,2,1,0:T(8,128)S(1)} %copy-done.10, ...), kind=kLoop, calls=%fused_computation.66 | loop fusion | flops 2031616 | bytes 2926592 | tf_op jit(solution)/shard_map/div | solution.py:377
  71.3 12.1 %shard_map.98 = (f32[1,32,128]{2,1,0:T(8,128)}, f32[1,32,128]{2,1,0:T(8,128)}, f32[1,16,128]{2,1,0:T(8,128)}, f32[1,16,128]{2,1,0:T(8,128)}) custom-call(f32[16,32,128]{2,1,0:T(8,128)} %fusion.28.field, s32[4,96]{1,0:T(4,128)} %pad_add_fusion.2.rows_at, s32[4,96]{1,0:T(4,128)} %pad_add_fusion.3.cols_at, f32[4,96]{1,0:T(4,128)} %pad_maximum_fusion.25.weights_at), custom_call_target="tpu_custom_call" | custom-call | bytes 98304 | tf_op jit(solution)/shard_map/pallas_call | solution.py:252
  83.4 0.7 copy-done.14
  84.1 1.6 %fusion.8 = f32[17,32,128]{2,1,0:T(8,128)S(1)} fusion(f32[18,36,256]{2,1,0:T(8,128)} %copy-done.7, f32[18,36,256]{2,1,0:T(8,128)} %copy-done.6, f32[16,1,128]{2,1,0:T(1,128)} %bitcast.71, f32[16,32,128]{2,1,0:T(8,128)S(1)} %copy-done, f32[16,1,128]{2,1,0:T(1,128)S(1)} %bitcast.69, f32[1,32,128]{2,1,0:T(8,128)} %get-tuple-element.33, ...), kind=kLoop, calls=%fused_computation.26 | loop fusion | flops 1671168 | bytes 2260992 | tf_op jit(solution)/shard_map/mul | solution.py:325
  85.7 0.3 fusion.2
  86.0 0.3 fusion.15
  86.3 0.9 %fusion.23 = f32[1,16,32,128]{3,2,1,0:T(8,128)} fusion(f32[16,33,128]{2,1,0:T(8,128)S(1)} %fusion.2, f32[17,32,128]{2,1,0:T(8,128)S(1)} %fusion.8, f32[16,32,128]{2,1,0:T(8,128)S(1)} %copy-done, f32[1,16,32,128]{3,2,1,0:T(8,128)S(1)} %copy-done.5, f32[16,32,127]{2,1,0:T(8,128)S(1)} %fusion.15, f32[1,16,32,128]{3,2,1,0:T(8,128)S(1)} %copy-done.1), kind=kLoop, calls=%fused_computation.56 | loop fusion | flops 589824 | bytes 2357248 | tf_op jit(solution)/shard_map/broadcast_in_dim | solution.py:380
  (50 shorter events, 0.4 us)
Async XLA Ops:
  0.6 7.0 %copy-start.1 = (f32[1,16,32,128]{3,2,1,0:T(8,128)S(1)}, f32[1,16,32,128]{3,2,1,0:T(8,128)}, u32[]{:S(2)}) copy-start(f32[1,16,32,128]{3,2,1,0:T(8,128)} %param.9) | copy-start | bytes 786436
  4.5 2.4 %copy-start.11 = (f32[4,192]{1,0:T(4,128)}, f32[4,192]{1,0:T(4,128)S(1)}, u32[]{:S(2)}) copy-start(f32[4,192]{1,0:T(4,128)S(1)} %pad_maximum_fusion.24.weights_at) | copy-start | bytes 9220
  4.6 1.4 %copy-start.12 = (s32[4,192]{1,0:T(4,128)}, s32[4,192]{1,0:T(4,128)S(1)}, u32[]{:S(2)}) copy-start(s32[4,192]{1,0:T(4,128)S(1)} %pad_add_fusion.rows_at) | copy-start | bytes 9220
  4.6 0.6 copy-start.13
  35.9 2.6 %copy-start.2 = (f32[1,16,32,128]{3,2,1,0:T(8,128)S(1)}, f32[1,16,32,128]{3,2,1,0:T(8,128)}, u32[]{:S(2)}) copy-start(f32[1,16,32,128]{3,2,1,0:T(8,128)} %param.8) | copy-start | bytes 786436
  36.8 0.9 copy-start.17
  37.7 0.8 copy-start.16
  39.1 0.9 copy-start.6
  39.1 1.1 %copy-start.7 = (f32[18,36,256]{2,1,0:T(8,128)}, f32[18,36,256]{2,1,0:T(8,128)S(1)}, u32[]{:S(2)}) copy-start(f32[18,36,256]{2,1,0:T(8,128)S(1)} %get-tuple-element.43) | copy-start | bytes 1990660
  39.1 1.2 %copy-start.5 = (f32[1,16,32,128]{3,2,1,0:T(8,128)S(1)}, f32[1,16,32,128]{3,2,1,0:T(8,128)}, u32[]{:S(2)}) copy-start(f32[1,16,32,128]{3,2,1,0:T(8,128)} %param.11) | copy-start | bytes 786436
  39.1 1.4 %copy-start.8 = (f32[1,16,32,128]{3,2,1,0:T(8,128)S(1)}, f32[1,16,32,128]{3,2,1,0:T(8,128)}, u32[]{:S(2)}) copy-start(f32[1,16,32,128]{3,2,1,0:T(8,128)} %param.10) | copy-start | bytes 786436
  41.6 13.6 %copy-start.3 = (f32[16,32,128]{2,1,0:T(8,128)S(1)}, f32[16,32,128]{2,1,0:T(8,128)}, u32[]{:S(2)}) copy-start(f32[16,32,128]{2,1,0:T(8,128)} %fusion.54.field) | copy-start | bytes 786436
  55.2 1.0 %copy-start.9 = (f32[1,16,32,128]{3,2,1,0:T(8,128)S(1)}, f32[1,16,32,128]{3,2,1,0:T(8,128)}, u32[]{:S(2)}) copy-start(f32[1,16,32,128]{3,2,1,0:T(8,128)} %param.10) | copy-start | bytes 786436
  55.2 0.9 %copy-start.20 = (f32[1,32,128]{2,1,0:T(8,128)S(1)}, f32[1,32,128]{2,1,0:T(8,128)}, u32[]{:S(2)}) copy-start(f32[1,32,128]{2,1,0:T(8,128)} %get-tuple-element.22) | copy-start | bytes 49156
  55.2 0.9 %copy-start.21 = (f32[1,32,128]{2,1,0:T(8,128)S(1)}, f32[1,32,128]{2,1,0:T(8,128)}, u32[]{:S(2)}) copy-start(f32[1,32,128]{2,1,0:T(8,128)} %get-tuple-element.25) | copy-start | bytes 49156
  55.2 0.9 %copy-start.24 = (f32[1,16,128]{2,1,0:T(8,128)S(1)}, f32[1,16,128]{2,1,0:T(8,128)}, u32[]{:S(2)}) copy-start(f32[1,16,128]{2,1,0:T(8,128)} %get-tuple-element.23) | copy-start | bytes 24580
  55.2 0.9 %copy-start.25 = (f32[1,16,128]{2,1,0:T(8,128)S(1)}, f32[1,16,128]{2,1,0:T(8,128)}, u32[]{:S(2)}) copy-start(f32[1,16,128]{2,1,0:T(8,128)} %get-tuple-element.24) | copy-start | bytes 24580
  57.2 12.1 %copy-start.4 = (f32[16,32,128]{2,1,0:T(8,128)S(1)}, f32[16,32,128]{2,1,0:T(8,128)}, u32[]{:S(2)}) copy-start(f32[16,32,128]{2,1,0:T(8,128)} %fusion.46.field) | copy-start | bytes 786436
  69.3 1.0 %copy-start.10 = (f32[1,16,32,128]{3,2,1,0:T(8,128)S(1)}, f32[1,16,32,128]{3,2,1,0:T(8,128)}, u32[]{:S(2)}) copy-start(f32[1,16,32,128]{3,2,1,0:T(8,128)} %param.10) | copy-start | bytes 786436
  69.3 0.9 %copy-start.18 = (f32[1,32,128]{2,1,0:T(8,128)S(1)}, f32[1,32,128]{2,1,0:T(8,128)}, u32[]{:S(2)}) copy-start(f32[1,32,128]{2,1,0:T(8,128)} %get-tuple-element.26) | copy-start | bytes 49156
  69.3 0.9 %copy-start.19 = (f32[1,32,128]{2,1,0:T(8,128)S(1)}, f32[1,32,128]{2,1,0:T(8,128)}, u32[]{:S(2)}) copy-start(f32[1,32,128]{2,1,0:T(8,128)} %get-tuple-element.29) | copy-start | bytes 49156
  69.3 0.9 %copy-start.22 = (f32[1,16,128]{2,1,0:T(8,128)S(1)}, f32[1,16,128]{2,1,0:T(8,128)}, u32[]{:S(2)}) copy-start(f32[1,16,128]{2,1,0:T(8,128)} %get-tuple-element.27) | copy-start | bytes 24580
  69.3 0.9 %copy-start.23 = (f32[1,16,128]{2,1,0:T(8,128)S(1)}, f32[1,16,128]{2,1,0:T(8,128)}, u32[]{:S(2)}) copy-start(f32[1,16,128]{2,1,0:T(8,128)} %get-tuple-element.28) | copy-start | bytes 24580
  71.3 12.1 %copy-start = (f32[16,32,128]{2,1,0:T(8,128)S(1)}, f32[16,32,128]{2,1,0:T(8,128)}, u32[]{:S(2)}) copy-start(f32[16,32,128]{2,1,0:T(8,128)} %fusion.28.field) | copy-start | bytes 786436
  83.4 0.7 copy-start.14
  84.1 1.6 %copy-start.15 = (f32[1,16,128]{2,1,0:T(8,128)S(1)}, f32[1,16,128]{2,1,0:T(8,128)}, u32[]{:S(2)}) copy-start(f32[1,16,128]{2,1,0:T(8,128)} %get-tuple-element.31) | copy-start | bytes 24580

commit v9 on v8

--- a/solution.py
+++ b/solution.py
@@ -183,6 +183,11 @@
         def _():
             copy.wait_send()
 
+    corner = jnp.zeros((width, width, field.shape[2]), jnp.float32)
+    for strip in (north, south):
+        strip[:, pl.ds(0, width)] = corner
+        strip[:, pl.ds(cols + width, width)] = corner
+
     def arrived(buf, recv):
         pltpu.make_async_copy(buf, buf, recv_sems.at[recv]).wait()
 
@@ -198,23 +203,23 @@
     def _():
         total = jnp.sum(lat_buf[...], axis=0)
         for depth in range(width):
-            north[width - 1 - depth] = total[depth * cols : (depth + 1) * cols]
+            north[width - 1 - depth, pl.ds(width, cols)] = total[depth * cols : (depth + 1) * cols]
 
     @pl.when(lat > 0)
     def _():
         arrived(north_buf, 2)
-        north[...] = north_buf[...]
+        north[:, pl.ds(width, cols)] = north_buf[...]
 
     @pl.when(lat == last_lat)
     def _():
         total = jnp.sum(lat_buf[...], axis=0)
         for depth in range(width):
-            south[depth] = total[depth * cols : (depth + 1) * cols]
+            south[depth, pl.ds(width, cols)] = total[depth * cols : (depth + 1) * cols]
 
     @pl.when(lat < last_lat)
     def _():
         arrived(south_buf, 3)
-        south[...] = south_buf[...]
+        south[:, pl.ds(width, cols)] = south_buf[...]
 
     @pl.when(lon == 0)
     def _():
@@ -244,7 +249,7 @@
 def exchange(field, plan, axes, width):
     sizes = {name: lax.axis_size(name) for name in ("lat", "lon")}
     rows, cols, levels = field.shape
-    lat_shape = (width, cols, levels)
+    lat_shape = (width, cols + 2 * width, levels)
     lon_shape = (width, rows, levels)
     vmem = pl.BlockSpec(memory_space=pltpu.VMEM)
     count = plan[0].shape[1]
@@ -263,8 +268,8 @@
             pltpu.VMEM((count, levels), jnp.float32),
             pltpu.VMEM((sizes["lat"], width * cols, levels), jnp.float32),
             pltpu.VMEM((sizes["lon"], width * rows, levels), jnp.float32),
-            pltpu.VMEM(lat_shape, jnp.float32),
-            pltpu.VMEM(lat_shape, jnp.float32),
+            pltpu.VMEM((width, cols, levels), jnp.float32),
+            pltpu.VMEM((width, cols, levels), jnp.float32),
             pltpu.VMEM((rows, width, levels), jnp.float32),
             pltpu.VMEM((rows, width, levels), jnp.float32),
             pltpu.SemaphoreType.DMA((8,)),
@@ -280,10 +285,7 @@
     middle = jnp.concatenate(
         [jnp.moveaxis(west, 0, 1), field, jnp.moveaxis(east, 0, 1)], axis=1
     )
-    corners = ((0, 0), (width, width), (0, 0))
-    return jnp.concatenate(
-        [jnp.pad(north, corners), middle, jnp.pad(south, corners)], axis=0
-    )
+    return jnp.concatenate([north, middle, south], axis=0)
 
 
 def face_terms(mobility):

time: 87.8 us -> 88.6 us (level)
    pad x2 -> x0, local copies, waits for them, and re-layouts: 1.75 us -> none  [the longest x1 0.89 us: surround(): jnp.pad(north, corners)]
    pallas_call x2, local copies, waits for them, and re-layouts: 0.05 us -> 1.6 us  [exchange(): pl.pallas_call(functools.partial(exchange_kernel, axes, sizes, width), ou...]
where the time goes in v9:
time: 88.6 us; the launch traced here: 87.9 us
  Pallas kernels  64.4 us (73%)
  other arithmetic  11.8 us (13%)
  local copies, waits for them, and re-layouts  10.6 us (12%)
  between operations  1.07 us (1%)
    pallas_call x4, Pallas kernels, exchange(): pl.pallas_call(functools.partial(exchange_kernel, axes, sizes, width), ou...  64.4 us
    unnamed x52, local copies, waits for them, and re-layouts  4.83 us
    div x3, other arithmetic, body(): neighbour_total(padded, source_now, lat_face, lon_face, mean_rad)  3.2 us
    concatenate x3, other arithmetic, body(): jnp.concatenate([part[:, at:at + size] for at, size in starts], axis=1)  1.98 us
    concatenate x1, other arithmetic, body(): jnp.concatenate([porosity_now, current], axis=-1)  1.79 us

profile of v9, /device:TPU:2, one launch (start us, length us, event | category | flops | bytes accessed | tf_op | source)
XLA Modules:
  0.0 87.9 jit_solution(15948423443847917813)
XLA Ops:
  0.6 0.0 copy-start.1
  0.6 0.8 squeeze.47
  1.5 0.8 squeeze.48
  2.2 0.7 fusion.60
  2.9 0.1 squeeze.51
  3.0 0.1 squeeze.49
  3.1 0.1 squeeze.55
  3.2 0.1 squeeze.53
  3.3 0.7 fusion.61
  4.1 0.1 squeeze.52
  4.1 0.1 squeeze.50
  4.3 0.1 squeeze.56
  4.3 0.1 squeeze.54
  4.6 0.0 copy-start.14
  4.6 0.0 copy-start.15
  4.6 0.1 fusion.65
  4.7 0.5 copy-done.15
  5.2 0.1 fusion.64
  5.3 0.7 pad_add_fusion.3.cols_at
  5.9 0.1 fusion.67
  6.0 0.1 fusion.66
  6.1 0.7 pad_add_fusion.2.rows_at
  6.7 0.1 fusion.63
  6.8 0.1 fusion.62
  6.9 0.7 pad_maximum_fusion.31.weights_at
  7.6 1.8 %pad_maximum_fusion.2.field = f32[16,32,256]{2,1,0:T(8,128)} fusion(f32[16,32,128]{2,1,0:T(8,128)} %bitcast.57, f32[16,32,128]{2,1,0:T(8,128)S(1)} %bitcast.52), kind=kLoop, calls=%fused_computation.5 | loop fusion | flops 131072 | bytes 1048576 | tf_op jit(solution)/shard_map/concatenate | solution.py:367
  9.4 26.7 %shard_map.95 = (f32[2,36,256]{2,1,0:T(8,128)}, f32[2,36,256]{2,1,0:T(8,128)}, f32[2,16,256]{2,1,0:T(8,128)}, f32[2,16,256]{2,1,0:T(8,128)}) custom-call(f32[16,32,256]{2,1,0:T(8,128)} %pad_maximum_fusion.2.field, s32[4,192]{1,0:T(4,128)} %copy-done.14, s32[4,192]{1,0:T(4,128)} %copy-done.15, f32[4,192]{1,0:T(4,128)} %copy-done.13), custom_call_target="tpu_custom_call" | custom-call | bytes 393216 | tf_op jit(solution)/shard_map/pallas_call | solution.py:257
  36.0 0.8 copy.15
  36.9 0.8 copy.14
  37.7 0.0 copy-done.2
  37.7 0.0 copy-done.11
  37.7 0.8 multiply_multiply_fusion
  38.6 0.1 slice_multiply_fusion.13
  38.7 0.0 copy-start.12
  38.7 0.1 slice_multiply_fusion.12
  38.9 0.7 copy-done.12
  39.6 0.1 maximum_maximum_fusion
  39.8 0.0 copy-start.5
  39.8 0.0 copy-start.8
  39.8 0.1 maximum_maximum_fusion.1
  39.9 0.7 copy-done.6
  40.6 0.2 copy-done.7
  40.9 0.1 copy-done.5
  40.9 0.3 copy-done.8
  41.2 1.1 %fusion.47.field = f32[16,32,128]{2,1,0:T(8,128)} fusion(f32[16,34,256]{2,1,0:T(8,128)S(1)} %get-tuple-element.49, f32[16,34,256]{2,1,0:T(8,128)S(1)} %get-tuple-element.48, f32[18,36,256]{2,1,0:T(8,128)S(1)} %get-tuple-element.43, f32[18,36,256]{2,1,0:T(8,128)S(1)} %get-tuple-element.42, f32[1,16,32,128]{3,2,1,0:T(8,128)S(1)} %copy-done.8, ...), kind=kLoop, calls=%fused_computation.104 | loop fusion | flops 1114112 | bytes 3663872 | tf_op jit(solution)/shard_map/div | solution.py:379
  42.3 13.6 %shard_map.96 = (f32[1,34,128]{2,1,0:T(8,128)}, f32[1,34,128]{2,1,0:T(8,128)}, f32[1,16,128]{2,1,0:T(8,128)}, f32[1,16,128]{2,1,0:T(8,128)}) custom-call(f32[16,32,128]{2,1,0:T(8,128)} %fusion.47.field, s32[4,96]{1,0:T(4,128)} %pad_add_fusion.2.rows_at, s32[4,96]{1,0:T(4,128)} %pad_add_fusion.3.cols_at, f32[4,96]{1,0:T(4,128)} %pad_maximum_fusion.31.weights_at), custom_call_target="tpu_custom_call" | custom-call | bytes 98304 | tf_op jit(solution)/shard_map/pallas_call | solution.py:257
  55.9 0.0 copy-start.9
  55.9 0.1 slice_multiply_fusion.11
  56.1 0.8 copy-done.9
  56.8 0.0 copy-done.21
  56.9 1.1 %fusion.37.field = f32[16,32,128]{2,1,0:T(8,128)} fusion(f32[16,1,128]{2,1,0:T(1,128)S(1)} %bitcast.76, f32[16,32,128]{2,1,0:T(8,128)S(1)} %copy-done.3, f32[16,1,128]{2,1,0:T(1,128)S(1)} %bitcast.75, f32[1,34,128]{2,1,0:T(8,128)S(1)} %copy-done.21, f32[1,34,128]{2,1,0:T(8,128)S(1)} %copy-done.20, f32[1,16,32,128]{3,2,1,0:T(8,128)S(1)} %copy-done.9, ...), kind=kLoop, calls=%fused_computation.83 | loop fusion | flops 1638400 | bytes 2928640 | tf_op jit(solution)/shard_map/div | solution.py:379
  57.9 12.1 %shard_map.97 = (f32[1,34,128]{2,1,0:T(8,128)}, f32[1,34,128]{2,1,0:T(8,128)}, f32[1,16,128]{2,1,0:T(8,128)}, f32[1,16,128]{2,1,0:T(8,128)}) custom-call(f32[16,32,128]{2,1,0:T(8,128)} %fusion.37.field, s32[4,96]{1,0:T(4,128)} %pad_add_fusion.2.rows_at, s32[4,96]{1,0:T(4,128)} %pad_add_fusion.3.cols_at, f32[4,96]{1,0:T(4,128)} %pad_maximum_fusion.31.weights_at), custom_call_target="tpu_custom_call" | custom-call | bytes 98304 | tf_op jit(solution)/shard_map/pallas_call | solution.py:257
  70.0 0.0 copy-start.10
  70.0 0.1 slice_multiply_fusion.9
  70.2 0.8 copy-done.10
  70.9 0.0 copy-done.19
  71.0 0.0 copy-done.23
  71.0 1.1 %fusion.26.field = f32[16,32,128]{2,1,0:T(8,128)} fusion(f32[16,1,128]{2,1,0:T(1,128)S(1)} %bitcast.74, f32[16,32,128]{2,1,0:T(8,128)S(1)} %copy-done.4, f32[16,1,128]{2,1,0:T(1,128)S(1)} %bitcast.73, f32[1,34,128]{2,1,0:T(8,128)S(1)} %copy-done.19, f32[1,34,128]{2,1,0:T(8,128)S(1)} %copy-done.18, f32[1,16,32,128]{3,2,1,0:T(8,128)S(1)} %copy-done.10, ...), kind=kLoop, calls=%fused_computation.62 | loop fusion | flops 1638400 | bytes 2928640 | tf_op jit(solution)/shard_map/div | solution.py:379
  72.0 12.1 %shard_map.98 = (f32[1,34,128]{2,1,0:T(8,128)}, f32[1,34,128]{2,1,0:T(8,128)}, f32[1,16,128]{2,1,0:T(8,128)}, f32[1,16,128]{2,1,0:T(8,128)}) custom-call(f32[16,32,128]{2,1,0:T(8,128)} %fusion.26.field, s32[4,96]{1,0:T(4,128)} %pad_add_fusion.2.rows_at, s32[4,96]{1,0:T(4,128)} %pad_add_fusion.3.cols_at, f32[4,96]{1,0:T(4,128)} %pad_maximum_fusion.31.weights_at), custom_call_target="tpu_custom_call" | custom-call | bytes 98304 | tf_op jit(solution)/shard_map/pallas_call | solution.py:257
  84.1 0.7 copy-done.16
  84.8 1.6 %fusion.8 = f32[17,32,128]{2,1,0:T(8,128)S(1)} fusion(f32[18,36,256]{2,1,0:T(8,128)} %copy-done.7, f32[18,36,256]{2,1,0:T(8,128)} %copy-done.6, f32[16,1,128]{2,1,0:T(1,128)} %bitcast.71, f32[16,32,128]{2,1,0:T(8,128)S(1)} %copy-done, f32[16,1,128]{2,1,0:T(1,128)S(1)} %bitcast.69, f32[1,34,128]{2,1,0:T(8,128)} %get-tuple-element.33, ...), kind=kLoop, calls=%fused_computation.26 | loop fusion | flops 1392640 | bytes 2263040 | tf_op jit(solution)/shard_map/mul | solution.py:327
  86.4 0.3 fusion.2
  86.7 0.3 fusion.13
  87.0 0.9 %fusion.21 = f32[1,16,32,128]{3,2,1,0:T(8,128)} fusion(f32[16,33,128]{2,1,0:T(8,128)S(1)} %fusion.2, f32[17,32,128]{2,1,0:T(8,128)S(1)} %fusion.8, f32[16,32,128]{2,1,0:T(8,128)S(1)} %copy-done, f32[1,16,32,128]{3,2,1,0:T(8,128)S(1)} %copy-done.5, f32[16,32,127]{2,1,0:T(8,128)S(1)} %fusion.13, f32[1,16,32,128]{3,2,1,0:T(8,128)S(1)} %copy-done.1), kind=kLoop, calls=%fused_computation.52 | loop fusion | flops 589824 | bytes 2357248 | tf_op jit(solution)/shard_map/broadcast_in_dim | solution.py:382
  (48 shorter events, 0.3 us)
Async XLA Ops:
  0.6 6.9 %copy-start.1 = (f32[1,16,32,128]{3,2,1,0:T(8,128)S(1)}, f32[1,16,32,128]{3,2,1,0:T(8,128)}, u32[]{:S(2)}) copy-start(f32[1,16,32,128]{3,2,1,0:T(8,128)} %param.9) | copy-start | bytes 786436
  4.5 2.3 %copy-start.13 = (f32[4,192]{1,0:T(4,128)}, f32[4,192]{1,0:T(4,128)S(1)}, u32[]{:S(2)}) copy-start(f32[4,192]{1,0:T(4,128)S(1)} %pad_maximum_fusion.30.weights_at) | copy-start | bytes 9220
  4.6 1.4 %copy-start.14 = (s32[4,192]{1,0:T(4,128)}, s32[4,192]{1,0:T(4,128)S(1)}, u32[]{:S(2)}) copy-start(s32[4,192]{1,0:T(4,128)S(1)} %pad_add_fusion.rows_at) | copy-start | bytes 9220
  4.6 0.6 copy-start.15
  9.3 28.3 %copy-start.2 = (f32[1,16,32,128]{3,2,1,0:T(8,128)S(1)}, f32[1,16,32,128]{3,2,1,0:T(8,128)}, u32[]{:S(2)}) copy-start(f32[1,16,32,128]{3,2,1,0:T(8,128)} %param.8) | copy-start | bytes 786436
  36.0 1.6 %copy-start.11 = (f32[2,36,256]{2,1,0:T(8,128)S(1)}, f32[2,36,256]{2,1,0:T(8,128)}, u32[]{:S(2)}) copy-start(f32[2,36,256]{2,1,0:T(8,128)} %get-tuple-element.18) | copy-start | bytes 221188
  38.7 0.9 %copy-start.12 = (f32[2,36,256]{2,1,0:T(8,128)S(1)}, f32[2,36,256]{2,1,0:T(8,128)}, u32[]{:S(2)}) copy-start(f32[2,36,256]{2,1,0:T(8,128)} %get-tuple-element.21) | copy-start | bytes 221188
  39.7 0.9 copy-start.6
  39.8 1.1 %copy-start.7 = (f32[18,36,256]{2,1,0:T(8,128)}, f32[18,36,256]{2,1,0:T(8,128)S(1)}, u32[]{:S(2)}) copy-start(f32[18,36,256]{2,1,0:T(8,128)S(1)} %get-tuple-element.43) | copy-start | bytes 1990660
  39.8 1.2 %copy-start.5 = (f32[1,16,32,128]{3,2,1,0:T(8,128)S(1)}, f32[1,16,32,128]{3,2,1,0:T(8,128)}, u32[]{:S(2)}) copy-start(f32[1,16,32,128]{3,2,1,0:T(8,128)} %param.11) | copy-start | bytes 786436
  39.8 1.4 %copy-start.8 = (f32[1,16,32,128]{3,2,1,0:T(8,128)S(1)}, f32[1,16,32,128]{3,2,1,0:T(8,128)}, u32[]{:S(2)}) copy-start(f32[1,16,32,128]{3,2,1,0:T(8,128)} %param.10) | copy-start | bytes 786436
  42.3 13.6 %copy-start.3 = (f32[16,32,128]{2,1,0:T(8,128)S(1)}, f32[16,32,128]{2,1,0:T(8,128)}, u32[]{:S(2)}) copy-start(f32[16,32,128]{2,1,0:T(8,128)} %fusion.47.field) | copy-start | bytes 786436
  55.9 1.0 %copy-start.9 = (f32[1,16,32,128]{3,2,1,0:T(8,128)S(1)}, f32[1,16,32,128]{3,2,1,0:T(8,128)}, u32[]{:S(2)}) copy-start(f32[1,16,32,128]{3,2,1,0:T(8,128)} %param.10) | copy-start | bytes 786436
  55.9 0.9 %copy-start.20 = (f32[1,34,128]{2,1,0:T(8,128)S(1)}, f32[1,34,128]{2,1,0:T(8,128)}, u32[]{:S(2)}) copy-start(f32[1,34,128]{2,1,0:T(8,128)} %get-tuple-element.22) | copy-start | bytes 52228
  55.9 0.9 %copy-start.21 = (f32[1,34,128]{2,1,0:T(8,128)S(1)}, f32[1,34,128]{2,1,0:T(8,128)}, u32[]{:S(2)}) copy-start(f32[1,34,128]{2,1,0:T(8,128)} %get-tuple-element.25) | copy-start | bytes 52228
  55.9 0.9 %copy-start.24 = (f32[1,16,128]{2,1,0:T(8,128)S(1)}, f32[1,16,128]{2,1,0:T(8,128)}, u32[]{:S(2)}) copy-start(f32[1,16,128]{2,1,0:T(8,128)} %get-tuple-element.23) | copy-start | bytes 24580
  55.9 0.9 %copy-start.25 = (f32[1,16,128]{2,1,0:T(8,128)S(1)}, f32[1,16,128]{2,1,0:T(8,128)}, u32[]{:S(2)}) copy-start(f32[1,16,128]{2,1,0:T(8,128)} %get-tuple-element.24) | copy-start | bytes 24580
  57.9 12.1 %copy-start.4 = (f32[16,32,128]{2,1,0:T(8,128)S(1)}, f32[16,32,128]{2,1,0:T(8,128)}, u32[]{:S(2)}) copy-start(f32[16,32,128]{2,1,0:T(8,128)} %fusion.37.field) | copy-start | bytes 786436
  70.0 1.0 %copy-start.10 = (f32[1,16,32,128]{3,2,1,0:T(8,128)S(1)}, f32[1,16,32,128]{3,2,1,0:T(8,128)}, u32[]{:S(2)}) copy-start(f32[1,16,32,128]{3,2,1,0:T(8,128)} %param.10) | copy-start | bytes 786436
  70.0 0.9 %copy-start.18 = (f32[1,34,128]{2,1,0:T(8,128)S(1)}, f32[1,34,128]{2,1,0:T(8,128)}, u32[]{:S(2)}) copy-start(f32[1,34,128]{2,1,0:T(8,128)} %get-tuple-element.26) | copy-start | bytes 52228
  70.0 0.9 %copy-start.19 = (f32[1,34,128]{2,1,0:T(8,128)S(1)}, f32[1,34,128]{2,1,0:T(8,128)}, u32[]{:S(2)}) copy-start(f32[1,34,128]{2,1,0:T(8,128)} %get-tuple-element.29) | copy-start | bytes 52228
  70.0 0.9 %copy-start.22 = (f32[1,16,128]{2,1,0:T(8,128)S(1)}, f32[1,16,128]{2,1,0:T(8,128)}, u32[]{:S(2)}) copy-start(f32[1,16,128]{2,1,0:T(8,128)} %get-tuple-element.27) | copy-start | bytes 24580
  70.0 0.9 %copy-start.23 = (f32[1,16,128]{2,1,0:T(8,128)S(1)}, f32[1,16,128]{2,1,0:T(8,128)}, u32[]{:S(2)}) copy-start(f32[1,16,128]{2,1,0:T(8,128)} %get-tuple-element.28) | copy-start | bytes 24580
  72.0 12.1 %copy-start = (f32[16,32,128]{2,1,0:T(8,128)S(1)}, f32[16,32,128]{2,1,0:T(8,128)}, u32[]{:S(2)}) copy-start(f32[16,32,128]{2,1,0:T(8,128)} %fusion.26.field) | copy-start | bytes 786436
  84.1 0.7 copy-start.16
  84.8 1.6 %copy-start.17 = (f32[1,16,128]{2,1,0:T(8,128)S(1)}, f32[1,16,128]{2,1,0:T(8,128)}, u32[]{:S(2)}) copy-start(f32[1,16,128]{2,1,0:T(8,128)} %get-tuple-element.31) | copy-start | bytes 24580
